TPU v7x, 512 devices: a whole 4x4x16 slice. The times are simulated.
512 devices in a mesh: dp: 64 (over z, y), clus: 8 (over x, core).
Axes of the slice: x: 4, y: 4, z: 16, core: 2. Of those that a mesh axis runs over, the one named last changes fastest.
Arguments:
- embeddings: bfloat16 [32768, 4096], P('dp'), may hold values from -6 to 6
- assignment: int32 [32768], P('dp'), may hold values from 0 to 1535
- slot_of: int32 [1536], replicated, may hold values from 0 to 1535, each once
- old_centroids: bfloat16 [1536, 4096], P(('clus', 'dp')), may hold values from -6 to 6
Outputs:
- new_centroids: float32 [1536, 4096], P(('clus', 'dp'))
- distance: float32 [32768], P('dp')
All inputs are finite; a program needn't handle non-finite values.
Results may differ from a plain program's by a relative error of at most 0.0003.
Values may be sent and summed in bfloat16 or wider, within the bound.
No kernel may reach another device: no remote copies, remote signals or barrier semaphores. Data moves between devices by JAX's collectives and lax.ppermute only.
A program may use at most 64 MiB of HBM per device.

v0:
```python
import jax
import jax.numpy as jnp
from jax import lax
from jax.sharding import Mesh
from jax.sharding import PartitionSpec as P

D = 4096
DP = ("dp_0", "dp_1")
CLUS_DP = ("clus", "dp_0", "dp_1")


def gather_axes(shard, axes, dim):
    for axis in reversed(axes):
        shard = lax.all_gather(shard, axis, axis=dim, tiled=True)
    return shard


def from_everyone(shard, axis):
    copies = jnp.broadcast_to(shard, (lax.axis_size(axis), *shard.shape))
    return lax.all_to_all(copies, axis, split_axis=0, concat_axis=0, tiled=True)


def taken_together(shard, axis):
    return from_everyone(shard, axis).sum(axis=0)


def cut_along(shard, dim, peers):
    shape = shard.shape
    parts = shard.reshape(*shape[:dim], peers, shape[dim] // peers, *shape[dim + 1 :])
    return jnp.moveaxis(parts, dim, 0)


def sent_and_summed(shard, axis, dim):
    parts = cut_along(shard, dim, lax.axis_size(axis))
    arrived = lax.all_to_all(parts, axis, split_axis=0, concat_axis=0, tiled=True)
    return arrived.sum(axis=0)


def sum_by_axis(shard, axes, dim):
    far, near = axes
    own = sent_and_summed(cut_along(shard, dim, lax.axis_size(far)), near, dim + 1)
    return jnp.sum(lax.all_to_all(own, far, 0, 0, tiled=True), axis=0)


def per_device(embeddings, assignment, slot_of, old_centroids):
    rows_own = old_centroids.shape[0]
    block_rows = rows_own * lax.axis_size(DP)
    clusters = slot_of.shape[0]
    first_slot = lax.axis_index("clus") * block_rows
    matches = assignment[:, None] == jnp.arange(clusters, dtype=jnp.int32)[None, :]
    slot_ids = jnp.sum(jnp.where(matches, slot_of[None, :], 0), axis=1)
    local_ids = slot_ids - first_slot
    one_hot = (jnp.arange(block_rows, dtype=jnp.int32)[:, None] == local_ids[None, :]).astype(
        jnp.bfloat16
    )
    shard_rows = gather_axes(old_centroids, DP, 0)
    raw = lax.dot_general(
        shard_rows, embeddings, (((1,), (1,)), ((), ())), preferred_element_type=jnp.float32
    )
    cent_wide = shard_rows.astype(jnp.float32)
    cent_rms = jnp.sqrt(jnp.mean(cent_wide * cent_wide, axis=1, keepdims=True) + 1e-06)
    scores = raw / cent_rms
    picked = jnp.sum(one_hot.astype(jnp.float32) * scores, axis=0)
    widened = embeddings.astype(jnp.float32)
    root_mean = jnp.sqrt(jnp.mean(widened * widened, axis=1) + 1e-06)
    partial_value = picked / (jnp.float32(D) * root_mean)
    overall_scores = taken_together(partial_value, "clus")
    distance = 1.0 - overall_scores
    own_sums = sum_by_axis(
        jnp.dot(one_hot, embeddings, preferred_element_type=jnp.float32), ("dp_0", "dp_1"), 0
    )
    overall = own_sums + old_centroids.astype(jnp.float32)
    updated = overall * lax.rsqrt(jnp.mean(overall * overall, axis=1, keepdims=True) + 1e-06)
    return (updated, distance)


def solution(mesh):
    split = Mesh(mesh.devices.reshape(16, 4, mesh.shape["clus"]), ("dp_0", "dp_1", "clus"))
    return jax.shard_map(
        per_device,
        mesh=split,
        in_specs=(P(DP, None), P(DP), P(), P(CLUS_DP, None)),
        out_specs=(P(CLUS_DP, None), P(DP)),
        check_vma=False,
    )
```

profile of v0, /device:TPU:8, one launch (start us, length us, event | category | flops | bytes accessed | tf_op | source)
XLA Modules:
  0.0 182.7 jit_solution(3661711160169545653)
XLA Ops:
  7.2 0.0 all-gather.4.cloned.1.call-start
  7.2 14.8 %all-gather = bf16[4,3,4096]{2,1,0:T(4,128)(2,1)S(1)} all-gather(bf16[1,3,4096]{2,1,0:T(4,128)(2,1)} %bitcast.6), channel_id=1, replica_groups=mesh['dp_0'=16,'dp_1'=4,'clus'=8] {'dp_1'}, dimensions={0}, use_global_device_ids=true | all-gather | bytes 122880 | tf_op jit(solution)/shard_map/all_gather | solution.py:14
  22.1 0.7 reshape.31
  22.8 1.2 select_reduce_fusion
  24.1 3.2 %fusion.3 = f32[192,4096]{1,0:T(8,128)S(1)} fusion(bf16[512,4096]{1,0:T(8,128)(2,1)} %param.4, s32[512]{0:T(512)S(1)} %broadcast_subtract_fusion.1), kind=kOutput, calls=%fused_computation.9 | convolution fusion | flops 805404672 | bytes 7342080 | tf_op jit(solution)/shard_map/dot_general | solution.py:70
  27.3 3.1 %reshape_reshape.3 = f32[16,4,3,4096]{3,2,1,0:T(4,128)} reshape(f32[192,4096]{1,0:T(8,128)S(1)} %fusion.3) | data formatting | bytes 6291456 | tf_op jit(solution)/shard_map/reshape;reshape | solution.py:29
  30.3 5.7 %copy.12 = f32[4,16,3,4096]{3,1,2,0:T(8,128)} copy(f32[4,16,3,4096]{3,2,0,1:T(4,128)} %bitcast.5) | data formatting | bytes 6291456 | tf_op jit(solution)/shard_map/transpose | solution.py:30
  36.0 6.8 %all-to-all-start = ((f32[4,16,3,4096]{3,1,2,0:T(8,128)}), f32[4,16,3,4096]{3,1,2,0:T(8,128)S(1)}, u32[]{:S(2)}, u32[]{:S(2)}) async-start(f32[4,16,3,4096]{3,1,2,0:T(8,128)} %copy.12), calls=%async_computation | async-start | bytes 6291456 | tf_op jit(solution)/shard_map/all_to_all | solution.py:35
  42.8 3.1 %multiply_reduce_fusion = f32[512]{0:T(512)S(1)} fusion(bf16[512,4096]{1,0:T(8,128)(2,1)} %param.4), kind=kLoop, calls=%fused_computation | loop fusion | flops 6290944 | bytes 4196352 | tf_op jit(solution)/shard_map/reduce_sum | solution.py:65
  45.9 51.3 %all-gather.4.cloned.1.call-done = bf16[16,12,4096]{2,1,0:T(8,128)(2,1)} async-done(((bf16[1,12,4096]{2,1,0:T(8,128)(2,1)}), bf16[16,12,4096]{2,1,0:T(8,128)(2,1)}) %all-gather.4.cloned.1.call-update) | async-done | bytes 1572880 | tf_op jit(solution)/shard_map/all_gather | solution.py:14
  97.2 3.6 %reshape.32 = bf16[192,4096]{1,0:T(8,128)(2,1)} reshape(bf16[16,12,4096]{2,1,0:T(8,128)(2,1)} %all-gather.4.cloned.1.call-done) | data formatting | bytes 3145728
  100.8 1.8 multiply_reduce_fusion.1
  102.6 4.2 %fusion.1 = f32[512]{0:T(512)S(1)} fusion(bf16[192,4096]{1,0:T(8,128)(2,1)} %reshape.32, bf16[512,4096]{1,0:T(8,128)(2,1)} %param.4, f32[192]{0:T(256)S(1)} %add_sqrt_fusion, s32[512]{0:T(512)S(1)} %broadcast_subtract_fusion.1), kind=kOutput, calls=%fused_computation.6 | convolution fusion | flops 805895680 | bytes 5772032 | tf_op jit(solution)/shard_map/dot_general | solution.py:57
  106.8 0.6 broadcast_in_dim.24
  107.5 4.3 %all-to-all-start.2 = ((f32[8,1,512]{2,1,0:T(1,128)}), f32[8,1,512]{2,1,0:T(1,128)S(1)}, u32[]{:S(2)}, u32[]{:S(2)}) async-start(f32[8,1,512]{2,1,0:T(1,128)} %broadcast_in_dim.24), calls=%async_computation.2 | async-start | bytes 32768 | tf_op jit(solution)/shard_map/all_to_all | solution.py:20
  111.7 1.2 reduce_sum.73
  112.9 2.7 %copy.13 = f32[16,3,4096]{2,1,0:T(4,128)} copy(f32[16,3,4096]{2,0,1:T(8,128)} %reduce_sum.73) | data formatting | bytes 1572864 | tf_op jit(solution)/shard_map/reduce_sum | solution.py:36
  115.5 1.5 all-to-all-done.2
  117.1 7.9 %all-to-all-start.1 = ((f32[16,3,4096]{2,1,0:T(4,128)}), f32[16,3,4096]{2,1,0:T(4,128)S(1)}, u32[]{:S(2)}, u32[]{:S(2)}) async-start(f32[16,3,4096]{2,1,0:T(4,128)} %copy.13), calls=%async_computation.1 | async-start | bytes 2097152 | tf_op jit(solution)/shard_map/all_to_all | solution.py:42
  125.0 0.6 broadcast_subtract_fusion
  125.6 49.3 %all-to-all-done.1 = f32[16,3,4096]{2,1,0:T(4,128)S(1)} async-done(((f32[16,3,4096]{2,1,0:T(4,128)}), f32[16,3,4096]{2,1,0:T(4,128)S(1)}, u32[]{:S(2)}, u32[]{:S(2)}) %all-to-all-start.1) | async-done | bytes 786464 | tf_op jit(solution)/shard_map/all_to_all | solution.py:42
  174.9 0.2 reduce_sum.74
  175.0 0.1 multiply_reduce_fusion.2
  175.2 0.7 fusion.5
  (9 shorter events, 0.1 us)
Async XLA Ops:
  7.2 90.0 %all-gather.4.cloned.1.call-start = ((), (), s32[]{:S(2)}) async-start(), calls=%async_computation.3 | async-start | bytes 2228224 | tf_op jit(solution)/shard_map/all_gather | solution.py:14
  36.0 70.8 %all-to-all-start = ((f32[4,16,3,4096]{3,1,2,0:T(8,128)}), f32[4,16,3,4096]{3,1,2,0:T(8,128)S(1)}, u32[]{:S(2)}, u32[]{:S(2)}) async-start(f32[4,16,3,4096]{3,1,2,0:T(8,128)} %copy.12), calls=%async_computation | async-start | bytes 6291456 | tf_op jit(solution)/shard_map/all_to_all | solution.py:35
  107.5 9.6 %all-to-all-start.2 = ((f32[8,1,512]{2,1,0:T(1,128)}), f32[8,1,512]{2,1,0:T(1,128)S(1)}, u32[]{:S(2)}, u32[]{:S(2)}) async-start(f32[8,1,512]{2,1,0:T(1,128)} %broadcast_in_dim.24), calls=%async_computation.2 | async-start | bytes 32768 | tf_op jit(solution)/shard_map/all_to_all | solution.py:20
  112.9 62.1 %copy-start = (bf16[3,4096]{1,0:T(4,128)(2,1)S(1)}, bf16[3,4096]{1,0:T(4,128)(2,1)}, u32[]{:S(2)}) copy-start(bf16[3,4096]{1,0:T(4,128)(2,1)} %param.7) | copy-start | bytes 73732
  117.1 57.8 %all-to-all-start.1 = ((f32[16,3,4096]{2,1,0:T(4,128)}), f32[16,3,4096]{2,1,0:T(4,128)S(1)}, u32[]{:S(2)}, u32[]{:S(2)}) async-start(f32[16,3,4096]{2,1,0:T(4,128)} %copy.13), calls=%async_computation.1 | async-start | bytes 2097152 | tf_op jit(solution)/shard_map/all_to_all | solution.py:42
Sparse Core Ops, SparseCore 0:
  22.9 74.2 all-gather.3
where the time goes:
time: 183 us
  waiting for transfers between devices  102 us (56%)
  starting transfers between devices  19 us (10%)
  local copies, waits for them, and re-layouts  16.4 us (9%)
  blocking collectives  14.8 us (8%)
  between operations  14.1 us (8%)
  other arithmetic  8.95 us (5%)
  matrix products  7.4 us (4%)
    all_gather x1, waiting for transfers between devices, gather_axes(): shard = lax.all_gather(shard, axis, axis=dim, tiled=True)  51.3 us
    all_to_all x1, waiting for transfers between devices, sum_by_axis(): return jnp.sum(lax.all_to_all(own, far, 0, 0, tiled=True), axis=0)  49.3 us
    all_gather x1, blocking collectives, gather_axes(): shard = lax.all_gather(shard, axis, axis=dim, tiled=True)  14.8 us
    all_to_all x1, starting transfers between devices, sum_by_axis(): return jnp.sum(lax.all_to_all(own, far, 0, 0, tiled=True), axis=0)  7.88 us
    all_to_all x1, starting transfers between devices, sent_and_summed(): lax.all_to_all(parts, axis, split_axis=0, concat_axis=0, tiled=True)  6.82 us
    transpose x1, local copies, waits for them, and re-layouts, cut_along(): return jnp.moveaxis(parts, dim, 0)  5.69 us
    unnamed x4, local copies, waits for them, and re-layouts  4.34 us
    all_to_all x1, starting transfers between devices, from_everyone(): return lax.all_to_all(copies, axis, split_axis=0, concat_axis=0, tiled=True)  4.25 us
  transfers between devices with their start and end apart: 4, of which 3 were waited for; matrix products, arithmetic and copies ran while one was open for 17% of the time, Pallas kernels for 0%

commit v1 on v0

v1 whole, which is shorter than its diff:
```python
import jax
import jax.numpy as jnp
from jax import lax
from jax.experimental import pallas as pl
from jax.experimental.pallas import tpu as pltpu
from jax.sharding import Mesh
from jax.sharding import PartitionSpec as P

D = 4096
ZH, ZL, NY, NC = 8, 2, 4, 8
NZ = ZH * ZL
DP = ("zh", "zl", "y")
CLUS_DP = ("c", "zh", "zl", "y")
EPS = 1e-06


def swap(x, axis, pairs):
    return lax.ppermute(x, axis, pairs)


def shifted(x, axis, size, by):
    return lax.ppermute(x, axis, [(i, (i + by) % size) for i in range(size)])


def exchange(x, axis):
    return lax.all_to_all(x, axis, 0, 0, tiled=True)


def copies(x, count):
    return jnp.broadcast_to(x, (count, *x.shape))


def sums_kernel(pos_ref, own_ref, a_ref, b_ref, c_ref, away_ref, home_ref):
    y = pos_ref[0]
    zl = pos_ref[1]
    rows = home_ref.shape[0]
    points = own_ref.shape[0] - 16
    r = lax.broadcasted_iota(jnp.int32, (rows, 1), 0)
    per_z = NC * 3
    zh = r // per_z
    c = (r % per_z) // 3
    k = r % 3
    slot = c * (NZ * NY * 3) + (zh * ZL * NY + y) * 3 + k
    for out_ref, part in ((away_ref, 1 - zl), (home_ref, zl)):
        wanted = slot + part * (NY * 3)
        total = None
        for ref in (own_ref, a_ref, b_ref, c_ref):
            tail = ref[points : points + 16, :].astype(jnp.float32)
            ids = (tail[0:1, :] * 64.0 + tail[1:2, :]).astype(jnp.int32)
            hot = (wanted == ids).astype(jnp.float32).astype(jnp.bfloat16)
            got = jnp.dot(hot, ref[0:points, :], preferred_element_type=jnp.float32)
            total = got if total is None else total + got
        out_ref[...] = total


def local_sums(pos, own, others):
    rows = ZH * NC * 3
    width = own.shape[1]
    shape = jax.ShapeDtypeStruct((rows, width), jnp.float32)
    vmem = pl.BlockSpec(memory_space=pltpu.VMEM)
    return pl.pallas_call(
        sums_kernel,
        out_shape=(shape, shape),
        in_specs=[pl.BlockSpec(memory_space=pltpu.SMEM)] + [vmem] * 4,
        out_specs=(vmem, vmem),
        name="local_sums",
    )(pos, own, *others)


def score_kernel(ids_ref, root_ref, a_ref, b_ref, c_ref, d_ref, emb_ref, out_ref):
    n = a_ref.shape[0]
    emb = emb_ref[...]
    ids = ids_ref[...]
    total = None
    for j, ref in enumerate((a_ref, b_ref, c_ref, d_ref)):
        rows = ref[...]
        raw = lax.dot_general(
            rows, emb, (((1,), (1,)), ((), ())), preferred_element_type=jnp.float32
        )
        wide = rows.astype(jnp.float32)
        rms = jnp.sqrt(jnp.mean(wide * wide, axis=1, keepdims=True) + EPS)
        here = lax.broadcasted_iota(jnp.int32, (n, 1), 0) + j * n
        got = jnp.sum(jnp.where(here == ids, raw / rms, 0.0), axis=0, keepdims=True)
        total = got if total is None else total + got
    out_ref[...] = total / (jnp.float32(D) * root_ref[...])


def local_scores(ids, root, blocks, emb):
    points = emb.shape[0]
    step = 128
    row = pl.BlockSpec((1, step), lambda i: (0, i))
    whole = pl.BlockSpec(blocks[0].shape, lambda i: (0, 0))
    return pl.pallas_call(
        score_kernel,
        grid=(points // step,),
        out_shape=jax.ShapeDtypeStruct((1, points), jnp.float32),
        in_specs=[row, row] + [whole] * 4 + [pl.BlockSpec((step, D), lambda i: (i, 0))],
        out_specs=row,
        name="local_scores",
    )(ids, root, *blocks, emb)


def per_device(embeddings, assignment, slot_of, old_centroids):
    points = embeddings.shape[0]
    clusters = slot_of.shape[0]
    width = D // NC
    c = lax.axis_index("c")
    y = lax.axis_index("y")
    zl = lax.axis_index("zl")

    cent = copies(old_centroids.reshape(96, 128), NZ)
    cent = exchange(cent, ("zh", "zl"))

    matches = assignment[:, None] == jnp.arange(clusters, dtype=jnp.int32)[None, :]
    slot_ids = jnp.sum(jnp.where(matches, slot_of[None, :], 0), axis=1)
    digits = jnp.stack([slot_ids // 64, slot_ids % 64]).astype(jnp.bfloat16)
    mine = lax.dynamic_slice_in_dim(embeddings, c * width, width, 1)
    packed = jnp.concatenate([mine, digits, jnp.zeros((14, width), jnp.bfloat16)], axis=0)
    others = [shifted(packed, "y", NY, d) for d in (2, 1, -1)]

    pos = jnp.stack([y, zl]).astype(jnp.int32)
    away, home = local_sums(pos, packed, others)
    arrived = shifted(away, "zl", ZL, 1)
    both = (home + arrived).reshape(ZH, NC * 3, width)

    blocks = cent.reshape(NZ * 3, D)
    others = [shifted(blocks, "y", NY, d) for d in (2, 1, -1)]
    local = slot_ids - c * (NZ * NY * 3)
    owner = local // 3
    turn = (y - owner % NY) % NY
    place = jnp.where(turn == 0, 0, jnp.where(turn == 2, 1, jnp.where(turn == 1, 2, 3)))
    row_ids = place * (NZ * 3) + (owner // NY) * 3 + local % 3
    row_ids = jnp.where((local >= 0) & (local < NZ * NY * 3), row_ids, -1)
    widened = embeddings.astype(jnp.float32)
    root_mean = jnp.sqrt(jnp.mean(widened * widened, axis=1) + EPS)
    partial = local_scores(row_ids[None, :], root_mean[None, :], [blocks, *others], embeddings)

    summed = exchange(both, "zh").sum(axis=0)
    sends = jnp.concatenate(
        [summed.reshape(NC, 1, 3 * width), jnp.broadcast_to(partial[None], (NC, 1, points))], axis=2
    )
    got = exchange(sends, "c")[:, 0]
    distance = 1.0 - got[:, 3 * width :].sum(axis=0)
    own_sums = got[:, : 3 * width].reshape(NC, 3, width).swapaxes(0, 1).reshape(3, D)
    overall = own_sums + old_centroids.astype(jnp.float32)
    updated = overall * lax.rsqrt(jnp.mean(overall * overall, axis=1, keepdims=True) + EPS)
    return (updated, distance)


def solution(mesh):
    split = Mesh(mesh.devices.reshape(ZH, ZL, NY, NC), ("zh", "zl", "y", "c"))
    return jax.shard_map(
        per_device,
        mesh=split,
        in_specs=(P(DP, None), P(DP), P(), P(CLUS_DP, None)),
        out_specs=(P(CLUS_DP, None), P(DP)),
        check_vma=False,
    )
```

time: 183 us -> 126 us (0.69)
  the two profiles are of different devices: /device:TPU:8 before, /device:TPU:1 now
where the time goes in v1:
time: 126 us; the launch traced here: 125 us
  starting transfers between devices  53 us (42%)
  waiting for transfers between devices  33.9 us (27%)
  Pallas kernels  11.8 us (9%)
  other arithmetic  9.69 us (8%)
  blocking collectives  9.63 us (8%)
  local copies, waits for them, and re-layouts  6.3 us (5%)
    ppermute x7, waiting for transfers between devices, shifted(): return lax.ppermute(x, axis, [(i, (i + by) % size) for i in range(size)])  33.9 us
    all_to_all x2, starting transfers between devices, exchange(): return lax.all_to_all(x, axis, 0, 0, tiled=True)  27.1 us
    ppermute x7, starting transfers between devices, shifted(): return lax.ppermute(x, axis, [(i, (i + by) % size) for i in range(size)])  25.9 us
    all_to_all x1, blocking collectives, exchange(): return lax.all_to_all(x, axis, 0, 0, tiled=True)  9.63 us
    pallas_call x1, Pallas kernels, local_scores(): pl.pallas_call(score_kernel, grid=(points // step,), out_shape=jax.ShapeD...  8.39 us
    pallas_call x1, Pallas kernels, local_sums(): pl.pallas_call(sums_kernel, out_shape=(shape, shape), in_specs=[pl.BlockS...  3.4 us
    reduce_sum x1, other arithmetic, per_device(): root_mean = jnp.sqrt(jnp.mean(widened * widened, axis=1) + EPS)  3.08 us
    unnamed x20, local copies, waits for them, and re-layouts  2.62 us
  transfers between devices with their start and end apart: 9, of which 4 were waited for; matrix products, arithmetic and copies ran while one was open for 8% of the time, Pallas kernels for 9%

profile of v1, /device:TPU:1, one launch (start us, length us, event | category | flops | bytes accessed | tf_op | source)
XLA Modules:
  0.0 125.1 jit_solution(9632018721323510247)
XLA Ops:
  0.6 0.8 reshape.312
  1.4 0.8 broadcast_in_dim.44
  2.2 15.7 %all-to-all-start.1 = ((bf16[16,96,128]{2,1,0:T(8,128)(2,1)}), bf16[16,96,128]{2,1,0:T(8,128)(2,1)S(1)}, u32[]{:S(2)}, u32[]{:S(2)}) async-start(bf16[16,96,128]{2,1,0:T(8,128)(2,1)} %broadcast_in_dim.44), calls=%async_computation.1 | async-start | bytes 786432 | tf_op jit(solution)/shard_map/all_to_all | solution.py:26
  18.0 1.2 select_reduce_fusion
  20.0 1.1 constant_dynamic-slice_fusion
  21.2 4.8 %collective-permute-start = (bf16[528,512]{1,0:T(8,128)(2,1)S(1)}, bf16[528,512]{1,0:T(8,128)(2,1)S(1)}, u32[]{:S(2)}, u32[]{:S(2)}) collective-permute-start(bf16[528,512]{1,0:T(8,128)(2,1)S(1)} %maximum_maximum_fusion.own_ref), channel_id=1, source_target_pairs={{0,16},{8,24},{16,0},{24,8},{1,17},{9,25},{17,1},{25,9},{2,18},{10... | collective-permute-start | bytes 1622024 | tf_op jit(solution)/shard_map/ppermute | solution.py:22
  26.1 2.3 %collective-permute-start.1 = (bf16[528,512]{1,0:T(8,128)(2,1)S(1)}, bf16[528,512]{1,0:T(8,128)(2,1)S(1)}, u32[]{:S(2)}, u32[]{:S(2)}) collective-permute-start(bf16[528,512]{1,0:T(8,128)(2,1)S(1)} %maximum_maximum_fusion.own_ref), channel_id=1, source_target_pairs={{0,8},{8,16},{16,24},{24,0},{1,9},{9,17},{17,25},{25,1},{2,10},{10... | collective-permute-start | bytes 1622024 | tf_op jit(solution)/shard_map/ppermute | solution.py:22
  28.4 4.2 %collective-permute-start.2 = (bf16[528,512]{1,0:T(8,128)(2,1)S(1)}, bf16[528,512]{1,0:T(8,128)(2,1)S(1)}, u32[]{:S(2)}, u32[]{:S(2)}) collective-permute-start(bf16[528,512]{1,0:T(8,128)(2,1)S(1)} %maximum_maximum_fusion.own_ref), channel_id=1, source_target_pairs={{0,24},{8,0},{16,8},{24,16},{1,25},{9,1},{17,9},{25,17},{2,26},{10... | collective-permute-start | bytes 1622024 | tf_op jit(solution)/shard_map/ppermute | solution.py:22
  33.2 4.4 %collective-permute-done.a_ref = bf16[528,512]{1,0:T(8,128)(2,1)S(1)} collective-permute-done((bf16[528,512]{1,0:T(8,128)(2,1)S(1)}, bf16[528,512]{1,0:T(8,128)(2,1)S(1)}, u32[]{:S(2)}, u32[]{:S(2)}) %collective-permute-start) | collective-permute-done | bytes 540704 | tf_op jit(solution)/shard_map/ppermute | solution.py:22
  37.6 12.9 %collective-permute-done.1.b_ref = bf16[528,512]{1,0:T(8,128)(2,1)S(1)} collective-permute-done((bf16[528,512]{1,0:T(8,128)(2,1)S(1)}, bf16[528,512]{1,0:T(8,128)(2,1)S(1)}, u32[]{:S(2)}, u32[]{:S(2)}) %collective-permute-start.1) | collective-permute-done | bytes 540704 | tf_op jit(solution)/shard_map/ppermute | solution.py:22
  50.4 0.8 copy-done.3
  51.3 0.8 copy-done.4
  52.1 3.4 %local_sums.1 = (f32[192,512]{1,0:T(8,128)}, f32[192,512]{1,0:T(8,128)}) custom-call(s32[2]{0:T(128)} %pad_add_fusion.pos_ref, bf16[528,512]{1,0:T(8,128)(2,1)} %copy-done, bf16[528,512]{1,0:T(8,128)(2,1)} %copy-done.2, bf16[528,512]{1,0:T(8,128)(2,1)} %copy-done.3, bf16[528,512]{1,0:T(8,128)(2,1)} %copy-done.4), custom_call_target="tpu_custom_call" | custom-call | tf_op jit(solution)/shard_map/local_sums/pallas_call | solution.py:61
  55.5 3.3 %collective-permute-start.3 = (f32[192,512]{1,0:T(8,128)}, f32[192,512]{1,0:T(8,128)S(1)}, u32[]{:S(2)}, u32[]{:S(2)}) collective-permute-start(f32[192,512]{1,0:T(8,128)} %get-tuple-element.5), channel_id=1, source_target_pairs={{0,32},{32,0},{1,33},{33,1},{2,34},{34,2},{3,35},{35,3},{4,36},{36... | collective-permute-start | bytes 1179656 | tf_op jit(solution)/shard_map/ppermute | solution.py:22
  58.7 9.0 %collective-permute-done.3 = f32[192,512]{1,0:T(8,128)S(1)} collective-permute-done((f32[192,512]{1,0:T(8,128)}, f32[192,512]{1,0:T(8,128)S(1)}, u32[]{:S(2)}, u32[]{:S(2)}) %collective-permute-start.3) | collective-permute-done | bytes 393248 | tf_op jit(solution)/shard_map/ppermute | solution.py:22
  67.7 1.8 %add.123 = f32[192,512]{1,0:T(8,128)} add(f32[192,512]{1,0:T(8,128)} %get-tuple-element.4, f32[192,512]{1,0:T(8,128)S(1)} %collective-permute-done.3) | non-fusion elementwise | flops 98304 | bytes 1179648 | tf_op jit(solution)/shard_map/add | solution.py:124
  69.5 11.3 %all-to-all-start = ((f32[8,24,512]{2,1,0:T(8,128)}), f32[8,24,512]{2,1,0:T(8,128)S(1)}, u32[]{:S(2)}, u32[]{:S(2)}) async-start(f32[8,24,512]{2,1,0:T(8,128)} %bitcast.3), calls=%async_computation | async-start | bytes 786432 | tf_op jit(solution)/shard_map/all_to_all | solution.py:26
  81.1 4.8 %collective-permute-start.4 = (bf16[48,4096]{1,0:T(8,128)(2,1)S(1)}, bf16[48,4096]{1,0:T(8,128)(2,1)S(1)}, u32[]{:S(2)}, u32[]{:S(2)}) collective-permute-start(bf16[48,4096]{1,0:T(8,128)(2,1)S(1)} %reshape.313.a_ref), channel_id=1, source_target_pairs={{0,16},{8,24},{16,0},{24,8},{1,17},{9,25},{17,1},{25,9},{2,18},{10... | collective-permute-start | bytes 1179656 | tf_op jit(solution)/shard_map/ppermute | solution.py:22
  85.9 1.9 %collective-permute-start.5 = (bf16[48,4096]{1,0:T(8,128)(2,1)S(1)}, bf16[48,4096]{1,0:T(8,128)(2,1)S(1)}, u32[]{:S(2)}, u32[]{:S(2)}) collective-permute-start(bf16[48,4096]{1,0:T(8,128)(2,1)S(1)} %reshape.313.a_ref), channel_id=1, source_target_pairs={{0,8},{8,16},{16,24},{24,0},{1,9},{9,17},{17,25},{25,1},{2,10},{10... | collective-permute-start | bytes 1179656 | tf_op jit(solution)/shard_map/ppermute | solution.py:22
  87.8 4.6 %collective-permute-start.6 = (bf16[48,4096]{1,0:T(8,128)(2,1)S(1)}, bf16[48,4096]{1,0:T(8,128)(2,1)S(1)}, u32[]{:S(2)}, u32[]{:S(2)}) collective-permute-start(bf16[48,4096]{1,0:T(8,128)(2,1)S(1)} %reshape.313.a_ref), channel_id=1, source_target_pairs={{0,24},{8,0},{16,8},{24,16},{1,25},{9,1},{17,9},{25,17},{2,26},{10... | collective-permute-start | bytes 1179656 | tf_op jit(solution)/shard_map/ppermute | solution.py:22
  92.4 3.1 %multiply_reduce_fusion = f32[512]{0:T(512)S(1)} fusion(bf16[512,4096]{1,0:T(8,128)(2,1)} %emb_ref.1), kind=kLoop, calls=%fused_computation | loop fusion | flops 6290944 | bytes 4196352 | tf_op jit(solution)/shard_map/reduce_sum | solution.py:135
  96.1 7.6 %collective-permute-done.5.c_ref = bf16[48,4096]{1,0:T(8,128)(2,1)S(1)} collective-permute-done((bf16[48,4096]{1,0:T(8,128)(2,1)S(1)}, bf16[48,4096]{1,0:T(8,128)(2,1)S(1)}, u32[]{:S(2)}, u32[]{:S(2)}) %collective-permute-start.5) | collective-permute-done | bytes 393248 | tf_op jit(solution)/shard_map/ppermute | solution.py:22
  104.7 8.4 %local_scores.1 = f32[1,512]{1,0:T(1,128)} custom-call(s32[1,512]{1,0:T(1,128)} %get-tuple-element.8.ids_ref, f32[1,512]{1,0:T(1,128)} %bitcast.19, bf16[48,4096]{1,0:T(8,128)(2,1)} %copy-done.1, bf16[48,4096]{1,0:T(8,128)(2,1)} %copy-done.5, bf16[48,4096]{1,0:T(8,128)(2,1)} %copy-done.6, bf16[48,4096]{1,0:T(8,128)(2,1)} %copy-done.7, bf16[512,4096]{1,0:T(8,128)(2,1)} %emb_ref.1), custom_call_target="tpu_custom_call" | custom-call | tf_op jit(solution)/shard_map/local_scores/pallas_call | solution.py:93
  113.9 9.6 %all_to_all.15 = f32[8,1,2048]{2,1,0:T(1,128)S(1)} all-to-all(f32[8,1,2048]{2,1,0:T(1,128)S(1)} %pad_maximum_fusion), channel_id=1, replica_groups=mesh['zh'=8,'zl'=2,'y'=4,'c'=8] {'c'}, dimensions={0} | all-to-all | bytes 131072 | tf_op jit(solution)/shard_map/all_to_all | solution.py:26
  (41 shorter events, 5.6 us)
Async XLA Ops:
  2.2 67.3 %all-to-all-start.1 = ((bf16[16,96,128]{2,1,0:T(8,128)(2,1)}), bf16[16,96,128]{2,1,0:T(8,128)(2,1)S(1)}, u32[]{:S(2)}, u32[]{:S(2)}) async-start(bf16[16,96,128]{2,1,0:T(8,128)(2,1)} %broadcast_in_dim.44), calls=%async_computation.1 | async-start | bytes 786432 | tf_op jit(solution)/shard_map/all_to_all | solution.py:26
  21.2 29.2 %copy-start = (bf16[528,512]{1,0:T(8,128)(2,1)}, bf16[528,512]{1,0:T(8,128)(2,1)S(1)}, u32[]{:S(2)}) copy-start(bf16[528,512]{1,0:T(8,128)(2,1)S(1)} %maximum_maximum_fusion.own_ref) | copy-start | bytes 1622020
  21.2 16.3 %collective-permute-start = (bf16[528,512]{1,0:T(8,128)(2,1)S(1)}, bf16[528,512]{1,0:T(8,128)(2,1)S(1)}, u32[]{:S(2)}, u32[]{:S(2)}) collective-permute-start(bf16[528,512]{1,0:T(8,128)(2,1)S(1)} %maximum_maximum_fusion.own_ref), channel_id=1, source_target_pairs={{0,16},{8,24},{16,0},{24,8},{1,17},{9,25},{17,1},{25,9},{2,18},{10... | collective-permute-start | bytes 1622024 | tf_op jit(solution)/shard_map/ppermute | solution.py:22
  26.1 24.4 %collective-permute-start.1 = (bf16[528,512]{1,0:T(8,128)(2,1)S(1)}, bf16[528,512]{1,0:T(8,128)(2,1)S(1)}, u32[]{:S(2)}, u32[]{:S(2)}) collective-permute-start(bf16[528,512]{1,0:T(8,128)(2,1)S(1)} %maximum_maximum_fusion.own_ref), channel_id=1, source_target_pairs={{0,8},{8,16},{16,24},{24,0},{1,9},{9,17},{17,25},{25,1},{2,10},{10... | collective-permute-start | bytes 1622024 | tf_op jit(solution)/shard_map/ppermute | solution.py:22
  28.4 22.0 %collective-permute-start.2 = (bf16[528,512]{1,0:T(8,128)(2,1)S(1)}, bf16[528,512]{1,0:T(8,128)(2,1)S(1)}, u32[]{:S(2)}, u32[]{:S(2)}) collective-permute-start(bf16[528,512]{1,0:T(8,128)(2,1)S(1)} %maximum_maximum_fusion.own_ref), channel_id=1, source_target_pairs={{0,24},{8,0},{16,8},{24,16},{1,25},{9,1},{17,9},{25,17},{2,26},{10... | collective-permute-start | bytes 1622024 | tf_op jit(solution)/shard_map/ppermute | solution.py:22
  37.6 12.9 %copy-start.2 = (bf16[528,512]{1,0:T(8,128)(2,1)}, bf16[528,512]{1,0:T(8,128)(2,1)S(1)}, u32[]{:S(2)}) copy-start(bf16[528,512]{1,0:T(8,128)(2,1)S(1)} %collective-permute-done.a_ref) | copy-start | bytes 1622020
  50.4 0.8 copy-start.3
  51.3 0.8 copy-start.4
  55.5 12.3 %collective-permute-start.3 = (f32[192,512]{1,0:T(8,128)}, f32[192,512]{1,0:T(8,128)S(1)}, u32[]{:S(2)}, u32[]{:S(2)}) collective-permute-start(f32[192,512]{1,0:T(8,128)} %get-tuple-element.5), channel_id=1, source_target_pairs={{0,32},{32,0},{1,33},{33,1},{2,34},{34,2},{3,35},{35,3},{4,36},{36... | collective-permute-start | bytes 1179656 | tf_op jit(solution)/shard_map/ppermute | solution.py:22
  69.5 44.2 %all-to-all-start = ((f32[8,24,512]{2,1,0:T(8,128)}), f32[8,24,512]{2,1,0:T(8,128)S(1)}, u32[]{:S(2)}, u32[]{:S(2)}) async-start(f32[8,24,512]{2,1,0:T(8,128)} %bitcast.3), calls=%async_computation | async-start | bytes 786432 | tf_op jit(solution)/shard_map/all_to_all | solution.py:26
  81.1 22.7 %copy-start.1 = (bf16[48,4096]{1,0:T(8,128)(2,1)}, bf16[48,4096]{1,0:T(8,128)(2,1)S(1)}, u32[]{:S(2)}) copy-start(bf16[48,4096]{1,0:T(8,128)(2,1)S(1)} %reshape.313.a_ref) | copy-start | bytes 1179652
  81.1 15.0 %collective-permute-start.4 = (bf16[48,4096]{1,0:T(8,128)(2,1)S(1)}, bf16[48,4096]{1,0:T(8,128)(2,1)S(1)}, u32[]{:S(2)}, u32[]{:S(2)}) collective-permute-start(bf16[48,4096]{1,0:T(8,128)(2,1)S(1)} %reshape.313.a_ref), channel_id=1, source_target_pairs={{0,16},{8,24},{16,0},{24,8},{1,17},{9,25},{17,1},{25,9},{2,18},{10... | collective-permute-start | bytes 1179656 | tf_op jit(solution)/shard_map/ppermute | solution.py:22
  85.9 17.8 %collective-permute-start.5 = (bf16[48,4096]{1,0:T(8,128)(2,1)S(1)}, bf16[48,4096]{1,0:T(8,128)(2,1)S(1)}, u32[]{:S(2)}, u32[]{:S(2)}) collective-permute-start(bf16[48,4096]{1,0:T(8,128)(2,1)S(1)} %reshape.313.a_ref), channel_id=1, source_target_pairs={{0,8},{8,16},{16,24},{24,0},{1,9},{9,17},{17,25},{25,1},{2,10},{10... | collective-permute-start | bytes 1179656 | tf_op jit(solution)/shard_map/ppermute | solution.py:22
  87.8 15.9 %collective-permute-start.6 = (bf16[48,4096]{1,0:T(8,128)(2,1)S(1)}, bf16[48,4096]{1,0:T(8,128)(2,1)S(1)}, u32[]{:S(2)}, u32[]{:S(2)}) collective-permute-start(bf16[48,4096]{1,0:T(8,128)(2,1)S(1)} %reshape.313.a_ref), channel_id=1, source_target_pairs={{0,24},{8,0},{16,8},{24,16},{1,25},{9,1},{17,9},{25,17},{2,26},{10... | collective-permute-start | bytes 1179656 | tf_op jit(solution)/shard_map/ppermute | solution.py:22
  96.1 7.7 %copy-start.5 = (bf16[48,4096]{1,0:T(8,128)(2,1)}, bf16[48,4096]{1,0:T(8,128)(2,1)S(1)}, u32[]{:S(2)}) copy-start(bf16[48,4096]{1,0:T(8,128)(2,1)S(1)} %collective-permute-done.4.b_ref) | copy-start | bytes 1179652
  103.7 0.8 copy-start.6
  103.7 0.9 copy-start.7
  104.7 19.0 %copy-start.8 = (bf16[3,4096]{1,0:T(4,128)(2,1)S(1)}, bf16[3,4096]{1,0:T(4,128)(2,1)}, u32[]{:S(2)}) copy-start(bf16[3,4096]{1,0:T(4,128)(2,1)} %param.7) | copy-start | bytes 73732

commit v2 on v1

v2 whole, which is shorter than its diff:
```python
import jax
import jax.numpy as jnp
from jax import lax
from jax.experimental import pallas as pl
from jax.experimental.pallas import tpu as pltpu
from jax.sharding import Mesh
from jax.sharding import PartitionSpec as P


D = 4096
ZH, ZL, NY, NC = 8, 2, 4, 8
NZ = ZH * ZL
DP = ("zh", "zl", "y")
CLUS_DP = ("c", "zh", "zl", "y")
EPS = 1e-06


def shifted(x, axis, size, by):
    return lax.ppermute(x, axis, [(i, (i + by) % size) for i in range(size)])


def exchange(x, axis):
    return lax.all_to_all(x, axis, 0, 0, tiled=True)


def copies(x, count):
    return jnp.broadcast_to(x, (count, *x.shape))


def sums_kernel(pos_ref, own_ref, a_ref, b_ref, c_ref, out_ref):
    rows = out_ref.shape[0]
    points = own_ref.shape[0] - 16
    r = lax.broadcasted_iota(jnp.int32, (rows, 1), 0)
    per_z = NC * 3
    zh = r // per_z
    c = (r % per_z) // 3
    slot = c * (NZ * NY * 3) + zh * (ZL * NY * 3) + r % 3
    wanted = slot + pos_ref[0]
    total = None
    for ref in (own_ref, a_ref, b_ref, c_ref):
        tail = ref[points : points + 16, :].astype(jnp.float32)
        ids = (tail[0:1, :] * 64.0 + tail[1:2, :]).astype(jnp.int32)
        hot = (wanted == ids).astype(jnp.float32).astype(jnp.bfloat16)
        got = jnp.dot(hot, ref[0:points, :], preferred_element_type=jnp.float32)
        total = got if total is None else total + got
    out_ref[...] = total


def local_sums(first, own, others):
    rows = ZH * NC * 3
    width = own.shape[1]
    vmem = pl.BlockSpec(memory_space=pltpu.VMEM)
    return pl.pallas_call(
        sums_kernel,
        out_shape=jax.ShapeDtypeStruct((rows, width), jnp.float32),
        in_specs=[pl.BlockSpec(memory_space=pltpu.SMEM)] + [vmem] * 4,
        out_specs=vmem,
        name="local_sums",
    )(first.reshape(1), own, *others)


def score_kernel(ids_ref, root_ref, a_ref, b_ref, c_ref, d_ref, emb_ref, out_ref, inv_ref):
    n = a_ref.shape[0]
    blocks = (a_ref, b_ref, c_ref, d_ref)

    @pl.when(pl.program_id(0) == 0)
    def _():
        for j, ref in enumerate(blocks):
            wide = ref[...].astype(jnp.float32)
            rms = jnp.sqrt(jnp.mean(wide * wide, axis=1, keepdims=True) + EPS)
            inv_ref[j * n : (j + 1) * n, :] = jnp.broadcast_to(1.0 / rms, (n, inv_ref.shape[1]))

    emb = emb_ref[...]
    ids = ids_ref[...]
    total = None
    for j, ref in enumerate(blocks):
        raw = lax.dot_general(
            ref[...], emb, (((1,), (1,)), ((), ())), preferred_element_type=jnp.float32
        )
        here = lax.broadcasted_iota(jnp.int32, raw.shape, 0) + j * n
        scaled = raw * inv_ref[j * n : (j + 1) * n, :]
        got = jnp.sum(jnp.where(here == ids, scaled, 0.0), axis=0, keepdims=True)
        total = got if total is None else total + got
    out_ref[...] = total / (jnp.float32(D) * root_ref[...])


def local_scores(ids, root, blocks, emb):
    points = emb.shape[0]
    step = 128
    row = pl.BlockSpec((1, step), lambda i: (0, i))
    whole = pl.BlockSpec(blocks[0].shape, lambda i: (0, 0))
    return pl.pallas_call(
        score_kernel,
        grid=(points // step,),
        out_shape=jax.ShapeDtypeStruct((1, points), jnp.float32),
        in_specs=[row, row] + [whole] * 4 + [pl.BlockSpec((step, D), lambda i: (i, 0))],
        out_specs=row,
        scratch_shapes=[pltpu.VMEM((4 * blocks[0].shape[0], step), jnp.float32)],
        name="local_scores",
    )(ids, root, *blocks, emb)


def steps(embeddings, assignment, slot_of, old_centroids):
    points = embeddings.shape[0]
    clusters = slot_of.shape[0]
    width = D // NC
    c = lax.axis_index("c")
    y = lax.axis_index("y")
    zl = lax.axis_index("zl")

    matches = assignment[:, None] == jnp.arange(clusters, dtype=jnp.int32)[None, :]
    slot_ids = jnp.sum(jnp.where(matches, slot_of[None, :], 0), axis=1)
    digits = jnp.stack([slot_ids // 64, slot_ids % 64]).astype(jnp.bfloat16)
    mine = lax.dynamic_slice_in_dim(embeddings, c * width, width, 1)
    packed = jnp.concatenate([mine, digits, jnp.zeros((14, width), jnp.bfloat16)], axis=0)
    others = [shifted(packed, "y", NY, d) for d in (2, 1, -1)]

    cent = copies(old_centroids.reshape(96, 128), NZ)
    cent = exchange(cent, ("zh", "zl"))

    widened = embeddings.astype(jnp.float32)
    root_mean = jnp.sqrt(jnp.mean(widened * widened, axis=1) + EPS)

    away = local_sums(y * 3 + (1 - zl) * (NY * 3), packed, others)
    arrived = shifted(away, "zl", ZL, 1)
    home = local_sums(y * 3 + zl * (NY * 3), packed, others)
    both = (home + arrived).reshape(ZH, NC * 3, width)
    summed = exchange(both, "zh")
    summed = summed.sum(axis=0)

    blocks = cent.reshape(NZ * 3, D)
    others = [shifted(blocks, "y", NY, d) for d in (2, 1, -1)]
    local = slot_ids - c * (NZ * NY * 3)
    owner = local // 3
    turn = (y - owner % NY) % NY
    place = jnp.where(turn == 0, 0, jnp.where(turn == 2, 1, jnp.where(turn == 1, 2, 3)))
    row_ids = place * (NZ * 3) + (owner // NY) * 3 + local % 3
    row_ids = jnp.where((local >= 0) & (local < NZ * NY * 3), row_ids, -1)
    partial = local_scores(row_ids[None, :], root_mean[None, :], [blocks, *others], embeddings)

    sends = jnp.concatenate(
        [summed.reshape(NC, 1, 3 * width), jnp.broadcast_to(partial[None], (NC, 1, points))], axis=2
    )
    got = exchange(sends, "c")[:, 0]
    distance = 1.0 - got[:, 3 * width :].sum(axis=0)
    own_sums = got[:, : 3 * width].reshape(NC, 3, width).swapaxes(0, 1).reshape(3, D)
    overall = own_sums + old_centroids.astype(jnp.float32)
    updated = overall * lax.rsqrt(jnp.mean(overall * overall, axis=1, keepdims=True) + EPS)
    return (updated, distance)


def solution(mesh):
    split = Mesh(mesh.devices.reshape(ZH, ZL, NY, NC), ("zh", "zl", "y", "c"))
    return jax.shard_map(
        steps,
        mesh=split,
        in_specs=(P(DP, None), P(DP), P(), P(CLUS_DP, None)),
        out_specs=(P(CLUS_DP, None), P(DP)),
        check_vma=False,
    )
```

time: 126 us -> 125 us (level)
  Pallas kernels: 11.8 us -> 14.7 us
  waiting for transfers between devices: 33.9 us -> 31.3 us
    ppermute x7, waiting for transfers between devices: 33.9 us -> 31.3 us  [shifted(): return lax.ppermute(x, axis, [(i, (i + by) % size) for i in range(size)])]
    pallas_call x1 -> x2, Pallas kernels: 3.4 us -> 5.9 us  [local_sums(): pl.pallas_call(sums_kernel, out_shape=jax.ShapeDtypeStruct((rows, width),...]
  transfers between devices with their start and end apart: 9 -> 9, of which waited for: 4 -> 4; matrix products, arithmetic and copies ran while one was open for 8% -> 8% of each run, Pallas kernels for 9% -> 12%
where the time goes in v2:
time: 125 us; the launch traced here: 124 us
  starting transfers between devices  53.2 us (43%)
  waiting for transfers between devices  31.3 us (25%)
  Pallas kernels  14.7 us (12%)
  blocking collectives  9.69 us (8%)
  other arithmetic  9.1 us (7%)
  local copies, waits for them, and re-layouts  5.63 us (5%)
    ppermute x7, waiting for transfers between devices, shifted(): return lax.ppermute(x, axis, [(i, (i + by) % size) for i in range(size)])  31.3 us
    all_to_all x2, starting transfers between devices, exchange(): return lax.all_to_all(x, axis, 0, 0, tiled=True)  27.1 us
    ppermute x7, starting transfers between devices, shifted(): return lax.ppermute(x, axis, [(i, (i + by) % size) for i in range(size)])  26.1 us
    all_to_all x1, blocking collectives, exchange(): return lax.all_to_all(x, axis, 0, 0, tiled=True)  9.69 us
    pallas_call x1, Pallas kernels, local_scores(): pl.pallas_call(score_kernel, grid=(points // step,), out_shape=jax.ShapeD...  8.79 us
    pallas_call x2, Pallas kernels, local_sums(): pl.pallas_call(sums_kernel, out_shape=jax.ShapeDtypeStruct((rows, width),...  5.9 us
    reduce_sum x1, other arithmetic, steps(): root_mean = jnp.sqrt(jnp.mean(widened * widened, axis=1) + EPS)  3.08 us
  transfers between devices with their start and end apart: 9, of which 4 were waited for; matrix products, arithmetic and copies ran while one was open for 8% of the time, Pallas kernels for 12%

profile of v2, /device:TPU:1, one launch (start us, length us, event | category | flops | bytes accessed | tf_op | source)
XLA Modules:
  0.0 124.4 jit_solution(1931166019893178646)
XLA Ops:
  0.6 0.8 reshape.320
  1.4 0.8 broadcast_in_dim.44
  2.2 15.7 %all-to-all-start.1 = ((bf16[16,96,128]{2,1,0:T(8,128)(2,1)}), bf16[16,96,128]{2,1,0:T(8,128)(2,1)S(1)}, u32[]{:S(2)}, u32[]{:S(2)}) async-start(bf16[16,96,128]{2,1,0:T(8,128)(2,1)} %broadcast_in_dim.44), calls=%async_computation.1 | async-start | bytes 786432 | tf_op jit(solution)/shard_map/all_to_all | solution.py:23
  18.0 1.2 select_reduce_fusion
  20.0 1.1 constant_dynamic-slice_fusion
  21.2 4.8 %collective-permute-start = (bf16[528,512]{1,0:T(8,128)(2,1)S(1)}, bf16[528,512]{1,0:T(8,128)(2,1)S(1)}, u32[]{:S(2)}, u32[]{:S(2)}) collective-permute-start(bf16[528,512]{1,0:T(8,128)(2,1)S(1)} %maximum_maximum_fusion.own_ref), channel_id=1, source_target_pairs={{0,16},{8,24},{16,0},{24,8},{1,17},{9,25},{17,1},{25,9},{2,18},{10... | collective-permute-start | bytes 1622024 | tf_op jit(solution)/shard_map/ppermute | solution.py:19
  26.1 2.3 %collective-permute-start.1 = (bf16[528,512]{1,0:T(8,128)(2,1)S(1)}, bf16[528,512]{1,0:T(8,128)(2,1)S(1)}, u32[]{:S(2)}, u32[]{:S(2)}) collective-permute-start(bf16[528,512]{1,0:T(8,128)(2,1)S(1)} %maximum_maximum_fusion.own_ref), channel_id=1, source_target_pairs={{0,8},{8,16},{16,24},{24,0},{1,9},{9,17},{17,25},{25,1},{2,10},{10... | collective-permute-start | bytes 1622024 | tf_op jit(solution)/shard_map/ppermute | solution.py:19
  28.4 4.2 %collective-permute-start.2 = (bf16[528,512]{1,0:T(8,128)(2,1)S(1)}, bf16[528,512]{1,0:T(8,128)(2,1)S(1)}, u32[]{:S(2)}, u32[]{:S(2)}) collective-permute-start(bf16[528,512]{1,0:T(8,128)(2,1)S(1)} %maximum_maximum_fusion.own_ref), channel_id=1, source_target_pairs={{0,24},{8,0},{16,8},{24,16},{1,25},{9,1},{17,9},{25,17},{2,26},{10... | collective-permute-start | bytes 1622024 | tf_op jit(solution)/shard_map/ppermute | solution.py:19
  32.6 5.0 %collective-permute-done.a_ref = bf16[528,512]{1,0:T(8,128)(2,1)S(1)} collective-permute-done((bf16[528,512]{1,0:T(8,128)(2,1)S(1)}, bf16[528,512]{1,0:T(8,128)(2,1)S(1)}, u32[]{:S(2)}, u32[]{:S(2)}) %collective-permute-start) | collective-permute-done | bytes 540704 | tf_op jit(solution)/shard_map/ppermute | solution.py:19
  37.6 12.9 %collective-permute-done.1.b_ref = bf16[528,512]{1,0:T(8,128)(2,1)S(1)} collective-permute-done((bf16[528,512]{1,0:T(8,128)(2,1)S(1)}, bf16[528,512]{1,0:T(8,128)(2,1)S(1)}, u32[]{:S(2)}, u32[]{:S(2)}) %collective-permute-start.1) | collective-permute-done | bytes 540704 | tf_op jit(solution)/shard_map/ppermute | solution.py:19
  50.5 0.8 copy-done.2
  51.5 2.9 %local_sums.3 = f32[192,512]{1,0:T(8,128)} custom-call(s32[1]{0:T(128)} %bitcast.2.pos_ref, bf16[528,512]{1,0:T(8,128)(2,1)} %copy-done, bf16[528,512]{1,0:T(8,128)(2,1)} %copy-done.1, bf16[528,512]{1,0:T(8,128)(2,1)} %copy-done.2, bf16[528,512]{1,0:T(8,128)(2,1)} %copy-done.3), custom_call_target="tpu_custom_call" | custom-call | tf_op jit(solution)/shard_map/local_sums/pallas_call | solution.py:53
  54.4 3.2 %collective-permute-start.3 = (f32[192,512]{1,0:T(8,128)}, f32[192,512]{1,0:T(8,128)S(1)}, u32[]{:S(2)}, u32[]{:S(2)}) collective-permute-start(f32[192,512]{1,0:T(8,128)} %local_sums.3), channel_id=1, source_target_pairs={{0,32},{32,0},{1,33},{33,1},{2,34},{34,2},{3,35},{35,3},{4,36},{36... | collective-permute-start | bytes 1179656 | tf_op jit(solution)/shard_map/ppermute | solution.py:19
  57.7 3.0 %local_sums.2 = f32[192,512]{1,0:T(8,128)} custom-call(s32[1]{0:T(128)} %bitcast.pos_ref, bf16[528,512]{1,0:T(8,128)(2,1)} %copy-done, bf16[528,512]{1,0:T(8,128)(2,1)} %copy-done.1, bf16[528,512]{1,0:T(8,128)(2,1)} %copy-done.2, bf16[528,512]{1,0:T(8,128)(2,1)} %copy-done.3), custom_call_target="tpu_custom_call" | custom-call | tf_op jit(solution)/shard_map/local_sums/pallas_call | solution.py:53
  60.6 5.9 %collective-permute-done.3 = f32[192,512]{1,0:T(8,128)S(1)} collective-permute-done((f32[192,512]{1,0:T(8,128)}, f32[192,512]{1,0:T(8,128)S(1)}, u32[]{:S(2)}, u32[]{:S(2)}) %collective-permute-start.3) | collective-permute-done | bytes 393248 | tf_op jit(solution)/shard_map/ppermute | solution.py:19
  66.5 1.8 %add.131 = f32[192,512]{1,0:T(8,128)} add(f32[192,512]{1,0:T(8,128)} %local_sums.2, f32[192,512]{1,0:T(8,128)S(1)} %collective-permute-done.3) | non-fusion elementwise | flops 98304 | bytes 1179648 | tf_op jit(solution)/shard_map/add | solution.py:127
  68.3 11.3 %all-to-all-start = ((f32[8,24,512]{2,1,0:T(8,128)}), f32[8,24,512]{2,1,0:T(8,128)S(1)}, u32[]{:S(2)}, u32[]{:S(2)}) async-start(f32[8,24,512]{2,1,0:T(8,128)} %bitcast.3), calls=%async_computation | async-start | bytes 786432 | tf_op jit(solution)/shard_map/all_to_all | solution.py:23
  79.8 5.0 %collective-permute-start.4 = (bf16[48,4096]{1,0:T(8,128)(2,1)S(1)}, bf16[48,4096]{1,0:T(8,128)(2,1)S(1)}, u32[]{:S(2)}, u32[]{:S(2)}) collective-permute-start(bf16[48,4096]{1,0:T(8,128)(2,1)S(1)} %reshape.321.a_ref), channel_id=1, source_target_pairs={{0,16},{8,24},{16,0},{24,8},{1,17},{9,25},{17,1},{25,9},{2,18},{10... | collective-permute-start | bytes 1179656 | tf_op jit(solution)/shard_map/ppermute | solution.py:19
  84.9 2.1 %collective-permute-start.5 = (bf16[48,4096]{1,0:T(8,128)(2,1)S(1)}, bf16[48,4096]{1,0:T(8,128)(2,1)S(1)}, u32[]{:S(2)}, u32[]{:S(2)}) collective-permute-start(bf16[48,4096]{1,0:T(8,128)(2,1)S(1)} %reshape.321.a_ref), channel_id=1, source_target_pairs={{0,8},{8,16},{16,24},{24,0},{1,9},{9,17},{17,25},{25,1},{2,10},{10... | collective-permute-start | bytes 1179656 | tf_op jit(solution)/shard_map/ppermute | solution.py:19
  86.9 4.4 %collective-permute-start.6 = (bf16[48,4096]{1,0:T(8,128)(2,1)S(1)}, bf16[48,4096]{1,0:T(8,128)(2,1)S(1)}, u32[]{:S(2)}, u32[]{:S(2)}) collective-permute-start(bf16[48,4096]{1,0:T(8,128)(2,1)S(1)} %reshape.321.a_ref), channel_id=1, source_target_pairs={{0,24},{8,0},{16,8},{24,16},{1,25},{9,1},{17,9},{25,17},{2,26},{10... | collective-permute-start | bytes 1179656 | tf_op jit(solution)/shard_map/ppermute | solution.py:19
  91.4 3.1 %multiply_reduce_fusion = f32[512]{0:T(512)S(1)} fusion(bf16[512,4096]{1,0:T(8,128)(2,1)} %emb_ref.1), kind=kLoop, calls=%fused_computation | loop fusion | flops 6290944 | bytes 4196352 | tf_op jit(solution)/shard_map/reduce_sum | solution.py:122
  95.1 7.6 %collective-permute-done.5.c_ref = bf16[48,4096]{1,0:T(8,128)(2,1)S(1)} collective-permute-done((bf16[48,4096]{1,0:T(8,128)(2,1)S(1)}, bf16[48,4096]{1,0:T(8,128)(2,1)S(1)}, u32[]{:S(2)}, u32[]{:S(2)}) %collective-permute-start.5) | collective-permute-done | bytes 393248 | tf_op jit(solution)/shard_map/ppermute | solution.py:19
  103.5 8.8 %local_scores.1 = f32[1,512]{1,0:T(1,128)} custom-call(s32[1,512]{1,0:T(1,128)} %get-tuple-element.4.ids_ref, f32[1,512]{1,0:T(1,128)} %bitcast.19, bf16[48,4096]{1,0:T(8,128)(2,1)} %copy-done.4, bf16[48,4096]{1,0:T(8,128)(2,1)} %copy-done.5, bf16[48,4096]{1,0:T(8,128)(2,1)} %copy-done.6, bf16[48,4096]{1,0:T(8,128)(2,1)} %copy-done.7, bf16[512,4096]{1,0:T(8,128)(2,1)} %emb_ref.1), custom_call_target="tpu_custom_call" | custom-call | tf_op jit(solution)/shard_map/local_scores/pallas_call | solution.py:92
  113.1 9.7 %all_to_all.15 = f32[8,1,2048]{2,1,0:T(1,128)S(1)} all-to-all(f32[8,1,2048]{2,1,0:T(1,128)S(1)} %pad_maximum_fusion), channel_id=1, replica_groups=mesh['zh'=8,'zl'=2,'y'=4,'c'=8] {'c'}, dimensions={0} | all-to-all | bytes 131072 | tf_op jit(solution)/shard_map/all_to_all | solution.py:23
  (41 shorter events, 5.1 us)
Async XLA Ops:
  2.2 66.1 %all-to-all-start.1 = ((bf16[16,96,128]{2,1,0:T(8,128)(2,1)}), bf16[16,96,128]{2,1,0:T(8,128)(2,1)S(1)}, u32[]{:S(2)}, u32[]{:S(2)}) async-start(bf16[16,96,128]{2,1,0:T(8,128)(2,1)} %broadcast_in_dim.44), calls=%async_computation.1 | async-start | bytes 786432 | tf_op jit(solution)/shard_map/all_to_all | solution.py:23
  21.2 29.2 %copy-start = (bf16[528,512]{1,0:T(8,128)(2,1)}, bf16[528,512]{1,0:T(8,128)(2,1)S(1)}, u32[]{:S(2)}) copy-start(bf16[528,512]{1,0:T(8,128)(2,1)S(1)} %maximum_maximum_fusion.own_ref) | copy-start | bytes 1622020
  21.2 16.3 %collective-permute-start = (bf16[528,512]{1,0:T(8,128)(2,1)S(1)}, bf16[528,512]{1,0:T(8,128)(2,1)S(1)}, u32[]{:S(2)}, u32[]{:S(2)}) collective-permute-start(bf16[528,512]{1,0:T(8,128)(2,1)S(1)} %maximum_maximum_fusion.own_ref), channel_id=1, source_target_pairs={{0,16},{8,24},{16,0},{24,8},{1,17},{9,25},{17,1},{25,9},{2,18},{10... | collective-permute-start | bytes 1622024 | tf_op jit(solution)/shard_map/ppermute | solution.py:19
  26.1 24.4 %collective-permute-start.1 = (bf16[528,512]{1,0:T(8,128)(2,1)S(1)}, bf16[528,512]{1,0:T(8,128)(2,1)S(1)}, u32[]{:S(2)}, u32[]{:S(2)}) collective-permute-start(bf16[528,512]{1,0:T(8,128)(2,1)S(1)} %maximum_maximum_fusion.own_ref), channel_id=1, source_target_pairs={{0,8},{8,16},{16,24},{24,0},{1,9},{9,17},{17,25},{25,1},{2,10},{10... | collective-permute-start | bytes 1622024 | tf_op jit(solution)/shard_map/ppermute | solution.py:19
  28.4 22.0 %collective-permute-start.2 = (bf16[528,512]{1,0:T(8,128)(2,1)S(1)}, bf16[528,512]{1,0:T(8,128)(2,1)S(1)}, u32[]{:S(2)}, u32[]{:S(2)}) collective-permute-start(bf16[528,512]{1,0:T(8,128)(2,1)S(1)} %maximum_maximum_fusion.own_ref), channel_id=1, source_target_pairs={{0,24},{8,0},{16,8},{24,16},{1,25},{9,1},{17,9},{25,17},{2,26},{10... | collective-permute-start | bytes 1622024 | tf_op jit(solution)/shard_map/ppermute | solution.py:19
  37.6 12.9 %copy-start.1 = (bf16[528,512]{1,0:T(8,128)(2,1)}, bf16[528,512]{1,0:T(8,128)(2,1)S(1)}, u32[]{:S(2)}) copy-start(bf16[528,512]{1,0:T(8,128)(2,1)S(1)} %collective-permute-done.a_ref) | copy-start | bytes 1622020
  50.4 0.8 copy-start.2
  50.4 1.0 copy-start.3
  54.4 12.1 %collective-permute-start.3 = (f32[192,512]{1,0:T(8,128)}, f32[192,512]{1,0:T(8,128)S(1)}, u32[]{:S(2)}, u32[]{:S(2)}) collective-permute-start(f32[192,512]{1,0:T(8,128)} %local_sums.3), channel_id=1, source_target_pairs={{0,32},{32,0},{1,33},{33,1},{2,34},{34,2},{3,35},{35,3},{4,36},{36... | collective-permute-start | bytes 1179656 | tf_op jit(solution)/shard_map/ppermute | solution.py:19
  68.3 44.7 %all-to-all-start = ((f32[8,24,512]{2,1,0:T(8,128)}), f32[8,24,512]{2,1,0:T(8,128)S(1)}, u32[]{:S(2)}, u32[]{:S(2)}) async-start(f32[8,24,512]{2,1,0:T(8,128)} %bitcast.3), calls=%async_computation | async-start | bytes 786432 | tf_op jit(solution)/shard_map/all_to_all | solution.py:23
  79.8 22.8 %copy-start.4 = (bf16[48,4096]{1,0:T(8,128)(2,1)}, bf16[48,4096]{1,0:T(8,128)(2,1)S(1)}, u32[]{:S(2)}) copy-start(bf16[48,4096]{1,0:T(8,128)(2,1)S(1)} %reshape.321.a_ref) | copy-start | bytes 1179652
  79.8 15.2 %collective-permute-start.4 = (bf16[48,4096]{1,0:T(8,128)(2,1)S(1)}, bf16[48,4096]{1,0:T(8,128)(2,1)S(1)}, u32[]{:S(2)}, u32[]{:S(2)}) collective-permute-start(bf16[48,4096]{1,0:T(8,128)(2,1)S(1)} %reshape.321.a_ref), channel_id=1, source_target_pairs={{0,16},{8,24},{16,0},{24,8},{1,17},{9,25},{17,1},{25,9},{2,18},{10... | collective-permute-start | bytes 1179656 | tf_op jit(solution)/shard_map/ppermute | solution.py:19
  84.9 17.8 %collective-permute-start.5 = (bf16[48,4096]{1,0:T(8,128)(2,1)S(1)}, bf16[48,4096]{1,0:T(8,128)(2,1)S(1)}, u32[]{:S(2)}, u32[]{:S(2)}) collective-permute-start(bf16[48,4096]{1,0:T(8,128)(2,1)S(1)} %reshape.321.a_ref), channel_id=1, source_target_pairs={{0,8},{8,16},{16,24},{24,0},{1,9},{9,17},{17,25},{25,1},{2,10},{10... | collective-permute-start | bytes 1179656 | tf_op jit(solution)/shard_map/ppermute | solution.py:19
  86.9 15.7 %collective-permute-start.6 = (bf16[48,4096]{1,0:T(8,128)(2,1)S(1)}, bf16[48,4096]{1,0:T(8,128)(2,1)S(1)}, u32[]{:S(2)}, u32[]{:S(2)}) collective-permute-start(bf16[48,4096]{1,0:T(8,128)(2,1)S(1)} %reshape.321.a_ref), channel_id=1, source_target_pairs={{0,24},{8,0},{16,8},{24,16},{1,25},{9,1},{17,9},{25,17},{2,26},{10... | collective-permute-start | bytes 1179656 | tf_op jit(solution)/shard_map/ppermute | solution.py:19
  95.1 7.6 %copy-start.5 = (bf16[48,4096]{1,0:T(8,128)(2,1)}, bf16[48,4096]{1,0:T(8,128)(2,1)S(1)}, u32[]{:S(2)}) copy-start(bf16[48,4096]{1,0:T(8,128)(2,1)S(1)} %collective-permute-done.4.b_ref) | copy-start | bytes 1179652
  102.6 0.8 copy-start.6
  102.6 0.9 copy-start.7
  103.5 19.4 %copy-start.8 = (bf16[3,4096]{1,0:T(4,128)(2,1)S(1)}, bf16[3,4096]{1,0:T(4,128)(2,1)}, u32[]{:S(2)}) copy-start(bf16[3,4096]{1,0:T(4,128)(2,1)} %param.7) | copy-start | bytes 73732

commit v3 on v2

--- a/solution.py
+++ b/solution.py
@@ -59,49 +59,49 @@
     )(first.reshape(1), own, *others)
 
 
-def score_kernel(ids_ref, root_ref, a_ref, b_ref, c_ref, d_ref, emb_ref, out_ref, inv_ref):
+def score_kernel(
+    ids_ref, root_ref, a_ref, b_ref, c_ref, d_ref, emb_ref, out_ref, rows_ref, inv_ref
+):
     n = a_ref.shape[0]
-    blocks = (a_ref, b_ref, c_ref, d_ref)
 
     @pl.when(pl.program_id(0) == 0)
     def _():
-        for j, ref in enumerate(blocks):
-            wide = ref[...].astype(jnp.float32)
+        for j, ref in enumerate((a_ref, b_ref, c_ref, d_ref)):
+            rows = ref[...]
+            rows_ref[j * n : (j + 1) * n, :] = rows
+            wide = rows.astype(jnp.float32)
             rms = jnp.sqrt(jnp.mean(wide * wide, axis=1, keepdims=True) + EPS)
             inv_ref[j * n : (j + 1) * n, :] = jnp.broadcast_to(1.0 / rms, (n, inv_ref.shape[1]))
 
-    emb = emb_ref[...]
-    ids = ids_ref[...]
-    total = None
-    for j, ref in enumerate(blocks):
-        raw = lax.dot_general(
-            ref[...], emb, (((1,), (1,)), ((), ())), preferred_element_type=jnp.float32
-        )
-        here = lax.broadcasted_iota(jnp.int32, raw.shape, 0) + j * n
-        scaled = raw * inv_ref[j * n : (j + 1) * n, :]
-        got = jnp.sum(jnp.where(here == ids, scaled, 0.0), axis=0, keepdims=True)
-        total = got if total is None else total + got
-    out_ref[...] = total / (jnp.float32(D) * root_ref[...])
+    raw = lax.dot_general(
+        rows_ref[...], emb_ref[...], (((1,), (1,)), ((), ())), preferred_element_type=jnp.float32
+    )
+    here = lax.broadcasted_iota(jnp.int32, raw.shape, 0)
+    picked = jnp.where(here == ids_ref[...], raw * inv_ref[...], 0.0)
+    total = jnp.sum(picked, axis=0, keepdims=True) / (jnp.float32(D) * root_ref[...])
+    out_ref[...] = jnp.broadcast_to(total, out_ref.shape)
 
 
 def local_scores(ids, root, blocks, emb):
     points = emb.shape[0]
-    step = 128
+    step = 256
     row = pl.BlockSpec((1, step), lambda i: (0, i))
     whole = pl.BlockSpec(blocks[0].shape, lambda i: (0, 0))
     return pl.pallas_call(
         score_kernel,
         grid=(points // step,),
-        out_shape=jax.ShapeDtypeStruct((1, points), jnp.float32),
+        out_shape=jax.ShapeDtypeStruct((NC, points), jnp.float32),
         in_specs=[row, row] + [whole] * 4 + [pl.BlockSpec((step, D), lambda i: (i, 0))],
-        out_specs=row,
-        scratch_shapes=[pltpu.VMEM((4 * blocks[0].shape[0], step), jnp.float32)],
+        out_specs=pl.BlockSpec((NC, step), lambda i: (0, i)),
+        scratch_shapes=[
+            pltpu.VMEM((4 * blocks[0].shape[0], D), jnp.bfloat16),
+            pltpu.VMEM((4 * blocks[0].shape[0], step), jnp.float32),
+        ],
         name="local_scores",
     )(ids, root, *blocks, emb)
 
 
 def steps(embeddings, assignment, slot_of, old_centroids):
-    points = embeddings.shape[0]
     clusters = slot_of.shape[0]
     width = D // NC
     c = lax.axis_index("c")
@@ -129,17 +129,18 @@
     summed = summed.sum(axis=0)
 
     blocks = cent.reshape(NZ * 3, D)
-    others = [shifted(blocks, "y", NY, d) for d in (2, 1, -1)]
+    near = [shifted(blocks, "y", NY, d) for d in (1, -1)]
+    far = shifted(blocks, "y", NY, 2)
     local = slot_ids - c * (NZ * NY * 3)
     owner = local // 3
     turn = (y - owner % NY) % NY
     place = jnp.where(turn == 0, 0, jnp.where(turn == 2, 1, jnp.where(turn == 1, 2, 3)))
     row_ids = place * (NZ * 3) + (owner // NY) * 3 + local % 3
     row_ids = jnp.where((local >= 0) & (local < NZ * NY * 3), row_ids, -1)
-    partial = local_scores(row_ids[None, :], root_mean[None, :], [blocks, *others], embeddings)
+    partial = local_scores(row_ids[None, :], root_mean[None, :], [blocks, far, *near], embeddings)
 
     sends = jnp.concatenate(
-        [summed.reshape(NC, 1, 3 * width), jnp.broadcast_to(partial[None], (NC, 1, points))], axis=2
+        [summed.reshape(NC, 1, 3 * width), partial[:, None]], axis=2
     )
     got = exchange(sends, "c")[:, 0]
     distance = 1.0 - got[:, 3 * width :].sum(axis=0)

time: 125 us -> 121 us (0.968)
  Pallas kernels: 14.7 us -> 10.7 us
    pallas_call x1, Pallas kernels: 8.79 us -> 4.8 us  [local_scores(): pl.pallas_call(score_kernel, grid=(points // step,), out_shape=jax.ShapeD...]
  transfers between devices with their start and end apart: 9 -> 9, of which waited for: 4 -> 4; matrix products, arithmetic and copies ran while one was open for 8% -> 8% of each run, Pallas kernels for 12% -> 9%
where the time goes in v3:
time: 121 us; the launch traced here: 120 us
  starting transfers between devices  53.2 us (44%)
  waiting for transfers between devices  31.3 us (26%)
  Pallas kernels  10.7 us (9%)
  blocking collectives  9.69 us (8%)
  other arithmetic  9.11 us (8%)
  local copies, waits for them, and re-layouts  5.69 us (5%)
    ppermute x7, waiting for transfers between devices, shifted(): return lax.ppermute(x, axis, [(i, (i + by) % size) for i in range(size)])  31.3 us
    all_to_all x2, starting transfers between devices, exchange(): return lax.all_to_all(x, axis, 0, 0, tiled=True)  27.1 us
    ppermute x7, starting transfers between devices, shifted(): return lax.ppermute(x, axis, [(i, (i + by) % size) for i in range(size)])  26.1 us
    all_to_all x1, blocking collectives, exchange(): return lax.all_to_all(x, axis, 0, 0, tiled=True)  9.69 us
    pallas_call x2, Pallas kernels, local_sums(): pl.pallas_call(sums_kernel, out_shape=jax.ShapeDtypeStruct((rows, width),...  5.9 us
    pallas_call x1, Pallas kernels, local_scores(): pl.pallas_call(score_kernel, grid=(points // step,), out_shape=jax.ShapeD...  4.8 us
    reduce_sum x1, other arithmetic, steps(): root_mean = jnp.sqrt(jnp.mean(widened * widened, axis=1) + EPS)  3.08 us
  transfers between devices with their start and end apart: 9, of which 4 were waited for; matrix products, arithmetic and copies ran while one was open for 8% of the time, Pallas kernels for 9%

profile of v3, /device:TPU:1, one launch (start us, length us, event | category | flops | bytes accessed | tf_op | source)
XLA Modules:
  0.0 120.5 jit_solution(3756674252243414813)
XLA Ops:
  0.6 0.8 reshape.317
  1.4 0.8 broadcast_in_dim.39
  2.2 15.7 %all-to-all-start.1 = ((bf16[16,96,128]{2,1,0:T(8,128)(2,1)}), bf16[16,96,128]{2,1,0:T(8,128)(2,1)S(1)}, u32[]{:S(2)}, u32[]{:S(2)}) async-start(bf16[16,96,128]{2,1,0:T(8,128)(2,1)} %broadcast_in_dim.39), calls=%async_computation.1 | async-start | bytes 786432 | tf_op jit(solution)/shard_map/all_to_all | solution.py:23
  18.0 1.2 %select_reduce_fusion = s32[512]{0:T(512)S(1)} fusion(s32[1536]{0:T(1024)} %param.6, s32[512]{0:T(512)} %param.5), kind=kLoop, calls=%fused_computation.1 | loop fusion | flops 2358784 | bytes 10240 | tf_op jit(solution)/shard_map/reduce_sum | solution.py:112
  20.0 1.1 constant_dynamic-slice_fusion
  21.2 4.8 %collective-permute-start = (bf16[528,512]{1,0:T(8,128)(2,1)S(1)}, bf16[528,512]{1,0:T(8,128)(2,1)S(1)}, u32[]{:S(2)}, u32[]{:S(2)}) collective-permute-start(bf16[528,512]{1,0:T(8,128)(2,1)S(1)} %maximum_maximum_fusion.own_ref), channel_id=1, source_target_pairs={{0,16},{8,24},{16,0},{24,8},{1,17},{9,25},{17,1},{25,9},{2,18},{10... | collective-permute-start | bytes 1622024 | tf_op jit(solution)/shard_map/ppermute | solution.py:19
  26.1 2.3 %collective-permute-start.1 = (bf16[528,512]{1,0:T(8,128)(2,1)S(1)}, bf16[528,512]{1,0:T(8,128)(2,1)S(1)}, u32[]{:S(2)}, u32[]{:S(2)}) collective-permute-start(bf16[528,512]{1,0:T(8,128)(2,1)S(1)} %maximum_maximum_fusion.own_ref), channel_id=1, source_target_pairs={{0,8},{8,16},{16,24},{24,0},{1,9},{9,17},{17,25},{25,1},{2,10},{10... | collective-permute-start | bytes 1622024 | tf_op jit(solution)/shard_map/ppermute | solution.py:19
  28.4 4.2 %collective-permute-start.2 = (bf16[528,512]{1,0:T(8,128)(2,1)S(1)}, bf16[528,512]{1,0:T(8,128)(2,1)S(1)}, u32[]{:S(2)}, u32[]{:S(2)}) collective-permute-start(bf16[528,512]{1,0:T(8,128)(2,1)S(1)} %maximum_maximum_fusion.own_ref), channel_id=1, source_target_pairs={{0,24},{8,0},{16,8},{24,16},{1,25},{9,1},{17,9},{25,17},{2,26},{10... | collective-permute-start | bytes 1622024 | tf_op jit(solution)/shard_map/ppermute | solution.py:19
  32.6 5.0 %collective-permute-done.a_ref = bf16[528,512]{1,0:T(8,128)(2,1)S(1)} collective-permute-done((bf16[528,512]{1,0:T(8,128)(2,1)S(1)}, bf16[528,512]{1,0:T(8,128)(2,1)S(1)}, u32[]{:S(2)}, u32[]{:S(2)}) %collective-permute-start) | collective-permute-done | bytes 540704 | tf_op jit(solution)/shard_map/ppermute | solution.py:19
  37.6 12.9 %collective-permute-done.1.b_ref = bf16[528,512]{1,0:T(8,128)(2,1)S(1)} collective-permute-done((bf16[528,512]{1,0:T(8,128)(2,1)S(1)}, bf16[528,512]{1,0:T(8,128)(2,1)S(1)}, u32[]{:S(2)}, u32[]{:S(2)}) %collective-permute-start.1) | collective-permute-done | bytes 540704 | tf_op jit(solution)/shard_map/ppermute | solution.py:19
  50.5 0.8 copy-done.2
  51.5 2.9 %local_sums.3 = f32[192,512]{1,0:T(8,128)} custom-call(s32[1]{0:T(128)} %bitcast.2.pos_ref, bf16[528,512]{1,0:T(8,128)(2,1)} %copy-done, bf16[528,512]{1,0:T(8,128)(2,1)} %copy-done.1, bf16[528,512]{1,0:T(8,128)(2,1)} %copy-done.2, bf16[528,512]{1,0:T(8,128)(2,1)} %copy-done.3), custom_call_target="tpu_custom_call" | custom-call | tf_op jit(solution)/shard_map/local_sums/pallas_call | solution.py:53
  54.4 3.2 %collective-permute-start.3 = (f32[192,512]{1,0:T(8,128)}, f32[192,512]{1,0:T(8,128)S(1)}, u32[]{:S(2)}, u32[]{:S(2)}) collective-permute-start(f32[192,512]{1,0:T(8,128)} %local_sums.3), channel_id=1, source_target_pairs={{0,32},{32,0},{1,33},{33,1},{2,34},{34,2},{3,35},{35,3},{4,36},{36... | collective-permute-start | bytes 1179656 | tf_op jit(solution)/shard_map/ppermute | solution.py:19
  57.7 3.0 %local_sums.2 = f32[192,512]{1,0:T(8,128)} custom-call(s32[1]{0:T(128)} %bitcast.pos_ref, bf16[528,512]{1,0:T(8,128)(2,1)} %copy-done, bf16[528,512]{1,0:T(8,128)(2,1)} %copy-done.1, bf16[528,512]{1,0:T(8,128)(2,1)} %copy-done.2, bf16[528,512]{1,0:T(8,128)(2,1)} %copy-done.3), custom_call_target="tpu_custom_call" | custom-call | tf_op jit(solution)/shard_map/local_sums/pallas_call | solution.py:53
  60.6 5.9 %collective-permute-done.3 = f32[192,512]{1,0:T(8,128)S(1)} collective-permute-done((f32[192,512]{1,0:T(8,128)}, f32[192,512]{1,0:T(8,128)S(1)}, u32[]{:S(2)}, u32[]{:S(2)}) %collective-permute-start.3) | collective-permute-done | bytes 393248 | tf_op jit(solution)/shard_map/ppermute | solution.py:19
  66.5 1.8 %add.131 = f32[192,512]{1,0:T(8,128)} add(f32[192,512]{1,0:T(8,128)} %local_sums.2, f32[192,512]{1,0:T(8,128)S(1)} %collective-permute-done.3) | non-fusion elementwise | flops 98304 | bytes 1179648 | tf_op jit(solution)/shard_map/add | solution.py:127
  68.3 11.3 %all-to-all-start = ((f32[8,24,512]{2,1,0:T(8,128)}), f32[8,24,512]{2,1,0:T(8,128)S(1)}, u32[]{:S(2)}, u32[]{:S(2)}) async-start(f32[8,24,512]{2,1,0:T(8,128)} %bitcast.3), calls=%async_computation | async-start | bytes 786432 | tf_op jit(solution)/shard_map/all_to_all | solution.py:23
  79.8 5.0 %collective-permute-start.4 = (bf16[48,4096]{1,0:T(8,128)(2,1)S(1)}, bf16[48,4096]{1,0:T(8,128)(2,1)S(1)}, u32[]{:S(2)}, u32[]{:S(2)}) collective-permute-start(bf16[48,4096]{1,0:T(8,128)(2,1)S(1)} %reshape.318.a_ref), channel_id=1, source_target_pairs={{0,16},{8,24},{16,0},{24,8},{1,17},{9,25},{17,1},{25,9},{2,18},{10... | collective-permute-start | bytes 1179656 | tf_op jit(solution)/shard_map/ppermute | solution.py:19
  84.9 2.1 %collective-permute-start.5 = (bf16[48,4096]{1,0:T(8,128)(2,1)S(1)}, bf16[48,4096]{1,0:T(8,128)(2,1)S(1)}, u32[]{:S(2)}, u32[]{:S(2)}) collective-permute-start(bf16[48,4096]{1,0:T(8,128)(2,1)S(1)} %reshape.318.a_ref), channel_id=1, source_target_pairs={{0,8},{8,16},{16,24},{24,0},{1,9},{9,17},{17,25},{25,1},{2,10},{10... | collective-permute-start | bytes 1179656 | tf_op jit(solution)/shard_map/ppermute | solution.py:19
  86.9 4.4 %collective-permute-start.6 = (bf16[48,4096]{1,0:T(8,128)(2,1)S(1)}, bf16[48,4096]{1,0:T(8,128)(2,1)S(1)}, u32[]{:S(2)}, u32[]{:S(2)}) collective-permute-start(bf16[48,4096]{1,0:T(8,128)(2,1)S(1)} %reshape.318.a_ref), channel_id=1, source_target_pairs={{0,24},{8,0},{16,8},{24,16},{1,25},{9,1},{17,9},{25,17},{2,26},{10... | collective-permute-start | bytes 1179656 | tf_op jit(solution)/shard_map/ppermute | solution.py:19
  91.4 3.1 %multiply_reduce_fusion = f32[512]{0:T(512)S(1)} fusion(bf16[512,4096]{1,0:T(8,128)(2,1)} %emb_ref.1), kind=kLoop, calls=%fused_computation | loop fusion | flops 6290944 | bytes 4196352 | tf_op jit(solution)/shard_map/reduce_sum | solution.py:122
  95.1 7.6 %collective-permute-done.5.c_ref = bf16[48,4096]{1,0:T(8,128)(2,1)S(1)} collective-permute-done((bf16[48,4096]{1,0:T(8,128)(2,1)S(1)}, bf16[48,4096]{1,0:T(8,128)(2,1)S(1)}, u32[]{:S(2)}, u32[]{:S(2)}) %collective-permute-start.5) | collective-permute-done | bytes 393248 | tf_op jit(solution)/shard_map/ppermute | solution.py:19
  103.5 4.8 %local_scores.1 = f32[8,512]{1,0:T(8,128)} custom-call(s32[1,512]{1,0:T(1,128)} %get-tuple-element.4.ids_ref, f32[1,512]{1,0:T(1,128)} %bitcast.20, bf16[48,4096]{1,0:T(8,128)(2,1)} %copy-done.4, bf16[48,4096]{1,0:T(8,128)(2,1)} %copy-done.5, bf16[48,4096]{1,0:T(8,128)(2,1)} %copy-done.6, bf16[48,4096]{1,0:T(8,128)(2,1)} %copy-done.7, bf16[512,4096]{1,0:T(8,128)(2,1)} %emb_ref.1), custom_call_target="tpu_custom_call" | custom-call | tf_op jit(solution)/shard_map/local_scores/pallas_call | solution.py:90
  109.2 9.7 %all_to_all.15 = f32[8,1,2048]{2,1,0:T(1,128)S(1)} all-to-all(f32[8,1,2048]{2,1,0:T(1,128)S(1)} %pad_maximum_fusion), channel_id=1, replica_groups=mesh['zh'=8,'zl'=2,'y'=4,'c'=8] {'c'}, dimensions={0} | all-to-all | bytes 131072 | tf_op jit(solution)/shard_map/all_to_all | solution.py:23
  (41 shorter events, 5.2 us)
Async XLA Ops:
  2.2 66.1 %all-to-all-start.1 = ((bf16[16,96,128]{2,1,0:T(8,128)(2,1)}), bf16[16,96,128]{2,1,0:T(8,128)(2,1)S(1)}, u32[]{:S(2)}, u32[]{:S(2)}) async-start(bf16[16,96,128]{2,1,0:T(8,128)(2,1)} %broadcast_in_dim.39), calls=%async_computation.1 | async-start | bytes 786432 | tf_op jit(solution)/shard_map/all_to_all | solution.py:23
  21.2 29.2 %copy-start = (bf16[528,512]{1,0:T(8,128)(2,1)}, bf16[528,512]{1,0:T(8,128)(2,1)S(1)}, u32[]{:S(2)}) copy-start(bf16[528,512]{1,0:T(8,128)(2,1)S(1)} %maximum_maximum_fusion.own_ref) | copy-start | bytes 1622020
  21.2 16.3 %collective-permute-start = (bf16[528,512]{1,0:T(8,128)(2,1)S(1)}, bf16[528,512]{1,0:T(8,128)(2,1)S(1)}, u32[]{:S(2)}, u32[]{:S(2)}) collective-permute-start(bf16[528,512]{1,0:T(8,128)(2,1)S(1)} %maximum_maximum_fusion.own_ref), channel_id=1, source_target_pairs={{0,16},{8,24},{16,0},{24,8},{1,17},{9,25},{17,1},{25,9},{2,18},{10... | collective-permute-start | bytes 1622024 | tf_op jit(solution)/shard_map/ppermute | solution.py:19
  26.1 24.4 %collective-permute-start.1 = (bf16[528,512]{1,0:T(8,128)(2,1)S(1)}, bf16[528,512]{1,0:T(8,128)(2,1)S(1)}, u32[]{:S(2)}, u32[]{:S(2)}) collective-permute-start(bf16[528,512]{1,0:T(8,128)(2,1)S(1)} %maximum_maximum_fusion.own_ref), channel_id=1, source_target_pairs={{0,8},{8,16},{16,24},{24,0},{1,9},{9,17},{17,25},{25,1},{2,10},{10... | collective-permute-start | bytes 1622024 | tf_op jit(solution)/shard_map/ppermute | solution.py:19
  28.4 22.0 %collective-permute-start.2 = (bf16[528,512]{1,0:T(8,128)(2,1)S(1)}, bf16[528,512]{1,0:T(8,128)(2,1)S(1)}, u32[]{:S(2)}, u32[]{:S(2)}) collective-permute-start(bf16[528,512]{1,0:T(8,128)(2,1)S(1)} %maximum_maximum_fusion.own_ref), channel_id=1, source_target_pairs={{0,24},{8,0},{16,8},{24,16},{1,25},{9,1},{17,9},{25,17},{2,26},{10... | collective-permute-start | bytes 1622024 | tf_op jit(solution)/shard_map/ppermute | solution.py:19
  37.6 12.9 %copy-start.1 = (bf16[528,512]{1,0:T(8,128)(2,1)}, bf16[528,512]{1,0:T(8,128)(2,1)S(1)}, u32[]{:S(2)}) copy-start(bf16[528,512]{1,0:T(8,128)(2,1)S(1)} %collective-permute-done.a_ref) | copy-start | bytes 1622020
  50.4 0.8 copy-start.2
  50.4 1.0 copy-start.3
  54.4 12.1 %collective-permute-start.3 = (f32[192,512]{1,0:T(8,128)}, f32[192,512]{1,0:T(8,128)S(1)}, u32[]{:S(2)}, u32[]{:S(2)}) collective-permute-start(f32[192,512]{1,0:T(8,128)} %local_sums.3), channel_id=1, source_target_pairs={{0,32},{32,0},{1,33},{33,1},{2,34},{34,2},{3,35},{35,3},{4,36},{36... | collective-permute-start | bytes 1179656 | tf_op jit(solution)/shard_map/ppermute | solution.py:19
  68.3 40.7 %all-to-all-start = ((f32[8,24,512]{2,1,0:T(8,128)}), f32[8,24,512]{2,1,0:T(8,128)S(1)}, u32[]{:S(2)}, u32[]{:S(2)}) async-start(f32[8,24,512]{2,1,0:T(8,128)} %bitcast.3), calls=%async_computation | async-start | bytes 786432 | tf_op jit(solution)/shard_map/all_to_all | solution.py:23
  79.8 22.8 %copy-start.4 = (bf16[48,4096]{1,0:T(8,128)(2,1)}, bf16[48,4096]{1,0:T(8,128)(2,1)S(1)}, u32[]{:S(2)}) copy-start(bf16[48,4096]{1,0:T(8,128)(2,1)S(1)} %reshape.318.a_ref) | copy-start | bytes 1179652
  79.8 15.2 %collective-permute-start.4 = (bf16[48,4096]{1,0:T(8,128)(2,1)S(1)}, bf16[48,4096]{1,0:T(8,128)(2,1)S(1)}, u32[]{:S(2)}, u32[]{:S(2)}) collective-permute-start(bf16[48,4096]{1,0:T(8,128)(2,1)S(1)} %reshape.318.a_ref), channel_id=1, source_target_pairs={{0,16},{8,24},{16,0},{24,8},{1,17},{9,25},{17,1},{25,9},{2,18},{10... | collective-permute-start | bytes 1179656 | tf_op jit(solution)/shard_map/ppermute | solution.py:19
  84.9 17.8 %collective-permute-start.5 = (bf16[48,4096]{1,0:T(8,128)(2,1)S(1)}, bf16[48,4096]{1,0:T(8,128)(2,1)S(1)}, u32[]{:S(2)}, u32[]{:S(2)}) collective-permute-start(bf16[48,4096]{1,0:T(8,128)(2,1)S(1)} %reshape.318.a_ref), channel_id=1, source_target_pairs={{0,8},{8,16},{16,24},{24,0},{1,9},{9,17},{17,25},{25,1},{2,10},{10... | collective-permute-start | bytes 1179656 | tf_op jit(solution)/shard_map/ppermute | solution.py:19
  86.9 15.7 %collective-permute-start.6 = (bf16[48,4096]{1,0:T(8,128)(2,1)S(1)}, bf16[48,4096]{1,0:T(8,128)(2,1)S(1)}, u32[]{:S(2)}, u32[]{:S(2)}) collective-permute-start(bf16[48,4096]{1,0:T(8,128)(2,1)S(1)} %reshape.318.a_ref), channel_id=1, source_target_pairs={{0,24},{8,0},{16,8},{24,16},{1,25},{9,1},{17,9},{25,17},{2,26},{10... | collective-permute-start | bytes 1179656 | tf_op jit(solution)/shard_map/ppermute | solution.py:19
  95.1 7.6 %copy-start.5 = (bf16[48,4096]{1,0:T(8,128)(2,1)}, bf16[48,4096]{1,0:T(8,128)(2,1)S(1)}, u32[]{:S(2)}) copy-start(bf16[48,4096]{1,0:T(8,128)(2,1)S(1)} %collective-permute-done.4.b_ref) | copy-start | bytes 1179652
  102.6 0.8 copy-start.6
  102.6 0.9 copy-start.7
  103.5 15.5 %copy-start.8 = (bf16[3,4096]{1,0:T(4,128)(2,1)S(1)}, bf16[3,4096]{1,0:T(4,128)(2,1)}, u32[]{:S(2)}) copy-start(bf16[3,4096]{1,0:T(4,128)(2,1)} %param.7) | copy-start | bytes 73732

commit v4 on v2

v4 whole, which is shorter than its diff:
```python
import jax
import jax.numpy as jnp
from jax import lax
from jax.experimental import pallas as pl
from jax.experimental.pallas import tpu as pltpu
from jax.sharding import Mesh
from jax.sharding import PartitionSpec as P


D = 4096
ZH, ZL, NY, NC = 8, 2, 4, 8
NZ = ZH * ZL
DP = ("zh", "zl", "y")
CLUS_DP = ("c", "zh", "zl", "y")
EPS = 1e-06


def shifted(x, axis, size, by):
    return lax.ppermute(x, axis, [(i, (i + by) % size) for i in range(size)])


def exchange(x, axis):
    return lax.all_to_all(x, axis, 0, 0, tiled=True)


def copies(x, count):
    return jnp.broadcast_to(x, (count, *x.shape))


def slot_column(rows, first):
    r = lax.broadcasted_iota(jnp.int32, (rows, 1), 0)
    per_z = NC * 3
    zh = r // per_z
    c = (r % per_z) // 3
    return c * (NZ * NY * 3) + zh * (ZL * NY * 3) + r % 3 + first


def id_row(ref, points):
    tail = ref[points : points + 16, :].astype(jnp.float32)
    return (tail[0:1, :] * 64.0 + tail[1:2, :]).astype(jnp.int32)


def sums_kernel(pos_ref, own_ref, a_ref, b_ref, c_ref, out_ref):
    points = own_ref.shape[0] - 16
    wanted = slot_column(out_ref.shape[0], pos_ref[0])
    total = None
    for ref in (own_ref, a_ref, b_ref, c_ref):
        hot = (wanted == id_row(ref, points)).astype(jnp.float32).astype(jnp.bfloat16)
        got = jnp.dot(hot, ref[0:points, :], preferred_element_type=jnp.float32)
        total = got if total is None else total + got
    out_ref[...] = total


def local_sums(first, own, others):
    rows = ZH * NC * 3
    width = own.shape[1]
    vmem = pl.BlockSpec(memory_space=pltpu.VMEM)
    return pl.pallas_call(
        sums_kernel,
        out_shape=jax.ShapeDtypeStruct((rows, width), jnp.float32),
        in_specs=[pl.BlockSpec(memory_space=pltpu.SMEM)] + [vmem] * 4,
        out_specs=vmem,
        name="local_sums",
    )(first.reshape(1), own, *others)


def score_kernel(pos_ref, own_ref, a_ref, b_ref, c_ref, here_ref, there_ref, keep_ref, give_ref):
    points = own_ref.shape[0] - 16
    parts = []
    for ref, first in ((here_ref, pos_ref[0]), (there_ref, pos_ref[1])):
        rows = ref[...]
        wide = rows.astype(jnp.float32)
        square = jnp.sum(wide * wide, axis=1, keepdims=True)
        parts.append((rows, square, slot_column(rows.shape[0], first)))
    for by, ref in enumerate((own_ref, a_ref, b_ref, c_ref)):
        ids = id_row(ref, points)
        score = size = None
        for rows, square, wanted in parts:
            raw = lax.dot_general(
                rows,
                ref[0:points, :],
                (((1,), (1,)), ((), ())),
                preferred_element_type=jnp.float32,
            )
            hit = wanted == ids
            got = jnp.sum(jnp.where(hit, raw, 0.0), axis=0, keepdims=True)
            more = jnp.sum(jnp.where(hit, square, 0.0), axis=0, keepdims=True)
            score = got if score is None else score + got
            size = more if size is None else size + more
        role = pos_ref[2 + by]
        for out_ref, wanted in ((keep_ref, role < 2), (give_ref, role >= 2)):

            @pl.when(wanted)
            def _(out_ref=out_ref, score=score, size=size, place=lax.rem(role, 2)):
                out_ref[place, 0:1, :] = score
                out_ref[place, 1:2, :] = size


def local_scores(firsts, own, others, here, there):
    points = own.shape[0] - 16
    vmem = pl.BlockSpec(memory_space=pltpu.VMEM)
    return pl.pallas_call(
        score_kernel,
        out_shape=(jax.ShapeDtypeStruct((2, 2, points), jnp.float32),) * 2,
        in_specs=[pl.BlockSpec(memory_space=pltpu.SMEM)] + [vmem] * 6,
        out_specs=(vmem, vmem),
        name="local_scores",
    )(firsts, own, *others, here, there)


def steps(embeddings, assignment, slot_of, old_centroids):
    points = embeddings.shape[0]
    clusters = slot_of.shape[0]
    width = D // NC
    c = lax.axis_index("c")
    y = lax.axis_index("y")
    zl = lax.axis_index("zl")

    matches = assignment[:, None] == jnp.arange(clusters, dtype=jnp.int32)[None, :]
    slot_ids = jnp.sum(jnp.where(matches, slot_of[None, :], 0), axis=1)
    digits = jnp.stack([slot_ids // 64, slot_ids % 64]).astype(jnp.bfloat16)
    mine = lax.dynamic_slice_in_dim(embeddings, c * width, width, 1)
    packed = jnp.concatenate([mine, digits, jnp.zeros((14, width), jnp.bfloat16)], axis=0)
    after, before = shifted(packed, "y", NY, -1), shifted(packed, "y", NY, 1)
    others = [after, shifted(packed, "y", NY, 2), before]
    cent = exchange(old_centroids.reshape(3, NC, width).swapaxes(0, 1), "c")

    here = exchange(copies(cent.reshape(NC * 3, width), ZH), "zh")
    here = here.reshape(ZH * NC * 3, width)

    widened = embeddings.astype(jnp.float32)
    root_mean = jnp.sqrt(jnp.mean(widened * widened, axis=1) + EPS)

    first_here = y * 3 + zl * (NY * 3)
    first_there = y * 3 + (1 - zl) * (NY * 3)
    away = local_sums(first_there, packed, others)
    arrived = shifted(away, "zl", ZL, 1)
    home = local_sums(first_here, packed, others)
    there = shifted(here, "zl", ZL, 1)
    both = (home + arrived).reshape(ZH, NC * 3, width)
    summed = exchange(both, "zh")
    summed = summed.sum(axis=0)

    sources = (y + jnp.arange(NY)) % NY
    roles = jnp.where(
        sources == y, 0, jnp.where(sources == 3 - y, 1, jnp.where(sources == (y ^ 1), 2, 3))
    )
    where = jnp.concatenate([jnp.stack([first_here, first_there]), roles]).astype(jnp.int32)
    keep, give = local_scores(where, packed, others, here, there)
    kept = keep + lax.ppermute(give, "y", [(0, 1), (1, 0), (2, 3), (3, 2)])
    scored = kept[0] + lax.ppermute(kept[1], "y", [(0, 3), (3, 0), (1, 2), (2, 1)])

    sends = jnp.concatenate(
        [
            summed.reshape(NC, 1, 3 * width),
            jnp.broadcast_to(scored.reshape(1, 1, 2 * points), (NC, 1, 2 * points)),
        ],
        axis=2,
    )
    got = exchange(sends, "c")[:, 0]
    both = got[:, 3 * width :].sum(axis=0)
    cent_rms = jnp.sqrt(both[points:] / jnp.float32(D) + EPS)
    distance = 1.0 - both[:points] / (jnp.float32(D) * root_mean * cent_rms)
    own_sums = got[:, : 3 * width].reshape(NC, 3, width).swapaxes(0, 1).reshape(3, D)
    overall = own_sums + old_centroids.astype(jnp.float32)
    updated = overall * lax.rsqrt(jnp.mean(overall * overall, axis=1, keepdims=True) + EPS)
    return (updated, distance)


def solution(mesh):
    split = Mesh(mesh.devices.reshape(ZH, ZL, NY, NC), ("zh", "zl", "y", "c"))
    return jax.shard_map(
        steps,
        mesh=split,
        in_specs=(P(DP, None), P(DP), P(), P(CLUS_DP, None)),
        out_specs=(P(CLUS_DP, None), P(DP)),
        check_vma=False,
    )
```

time: 125 us -> 126 us (level)
  waiting for transfers between devices: 31.3 us -> 36.1 us
  Pallas kernels: 14.7 us -> 10.3 us
  blocking collectives: 9.69 us -> 12.5 us
  local copies, waits for them, and re-layouts: 5.63 us -> 3.81 us
  starting transfers between devices: 53.2 us -> 51.9 us
    ppermute x7 -> x5, starting transfers between devices: 26.1 us -> 16.8 us  [shifted(): return lax.ppermute(x, axis, [(i, (i + by) % size) for i in range(size)])]
    ppermute x0 -> x2, waiting for transfers between devices: none -> 6.31 us  [the longest x1 3.63 us: steps(): lax.ppermute(kept[1], 'y', [(0, 3), (3, 0), (1, 2), (2, 1)])]
    pallas_call x1, Pallas kernels: 8.79 us -> 4.42 us  [local_scores(): pl.pallas_call(score_kernel, out_shape=(jax.ShapeDtypeStruct((2, 2, point...]
    all_to_all x2 -> x3, starting transfers between devices: 27.1 us -> 31.1 us  [exchange(): return lax.all_to_all(x, axis, 0, 0, tiled=True)]
    ppermute x0 -> x2, starting transfers between devices: none -> 3.95 us  [the longest x1 2.04 us: steps(): kept = keep + lax.ppermute(give, 'y', [(0, 1), (1, 0), (2, 3), (3, 2)])]
    ppermute x7 -> x5, waiting for transfers between devices: 31.3 us -> 28 us  [shifted(): return lax.ppermute(x, axis, [(i, (i + by) % size) for i in range(size)])]
    all_to_all x1, blocking collectives: 9.69 us -> 12.5 us  [exchange(): return lax.all_to_all(x, axis, 0, 0, tiled=True)]
    all_to_all x2 -> x3, waiting for transfers between devices: 0.01 us -> 1.86 us  [exchange(): return lax.all_to_all(x, axis, 0, 0, tiled=True)]
  transfers between devices with their start and end apart: 9 -> 10, of which waited for: 4 -> 5; matrix products, arithmetic and copies ran while one was open for 8% -> 6% of each run, Pallas kernels for 12% -> 8%
where the time goes in v4:
time: 126 us; the launch traced here: 125 us
  starting transfers between devices  51.9 us (41%)
  waiting for transfers between devices  36.1 us (29%)
  blocking collectives  12.5 us (10%)
  Pallas kernels  10.3 us (8%)
  other arithmetic  9.91 us (8%)
  local copies, waits for them, and re-layouts  3.81 us (3%)
    all_to_all x3, starting transfers between devices, exchange(): return lax.all_to_all(x, axis, 0, 0, tiled=True)  31.1 us
    ppermute x5, waiting for transfers between devices, shifted(): return lax.ppermute(x, axis, [(i, (i + by) % size) for i in range(size)])  28 us
    ppermute x5, starting transfers between devices, shifted(): return lax.ppermute(x, axis, [(i, (i + by) % size) for i in range(size)])  16.8 us
    all_to_all x1, blocking collectives, exchange(): return lax.all_to_all(x, axis, 0, 0, tiled=True)  12.5 us
    pallas_call x2, Pallas kernels, local_sums(): pl.pallas_call(sums_kernel, out_shape=jax.ShapeDtypeStruct((rows, width),...  5.9 us
    pallas_call x1, Pallas kernels, local_scores(): pl.pallas_call(score_kernel, out_shape=(jax.ShapeDtypeStruct((2, 2, point...  4.42 us
    ppermute x1, waiting for transfers between devices, steps(): lax.ppermute(kept[1], 'y', [(0, 3), (3, 0), (1, 2), (2, 1)])  3.63 us
    reduce_sum x1, other arithmetic, steps(): root_mean = jnp.sqrt(jnp.mean(widened * widened, axis=1) + EPS)  3.08 us
  transfers between devices with their start and end apart: 10, of which 5 were waited for; matrix products, arithmetic and copies ran while one was open for 6% of the time, Pallas kernels for 8%

profile of v4, /device:TPU:1, one launch (start us, length us, event | category | flops | bytes accessed | tf_op | source)
XLA Modules:
  0.0 125.5 jit_solution(8727113166662429172)
XLA Ops:
  0.6 1.2 select_reduce_fusion
  2.0 1.1 constant_dynamic-slice_fusion
  3.3 4.0 %collective-permute-start.2 = (bf16[528,512]{1,0:T(8,128)(2,1)S(1)}, bf16[528,512]{1,0:T(8,128)(2,1)S(1)}, u32[]{:S(2)}, u32[]{:S(2)}) collective-permute-start(bf16[528,512]{1,0:T(8,128)(2,1)S(1)} %maximum_maximum_fusion.own_ref), channel_id=1, source_target_pairs={{0,8},{8,16},{16,24},{24,0},{1,9},{9,17},{17,25},{25,1},{2,10},{10... | collective-permute-start | bytes 1622024 | tf_op jit(solution)/shard_map/ppermute | solution.py:19
  7.3 4.5 %collective-permute-start.1 = (bf16[528,512]{1,0:T(8,128)(2,1)S(1)}, bf16[528,512]{1,0:T(8,128)(2,1)S(1)}, u32[]{:S(2)}, u32[]{:S(2)}) collective-permute-start(bf16[528,512]{1,0:T(8,128)(2,1)S(1)} %maximum_maximum_fusion.own_ref), channel_id=1, source_target_pairs={{0,16},{8,24},{16,0},{24,8},{1,17},{9,25},{17,1},{25,9},{2,18},{10... | collective-permute-start | bytes 1622024 | tf_op jit(solution)/shard_map/ppermute | solution.py:19
  11.8 3.0 %collective-permute-start = (bf16[528,512]{1,0:T(8,128)(2,1)S(1)}, bf16[528,512]{1,0:T(8,128)(2,1)S(1)}, u32[]{:S(2)}, u32[]{:S(2)}) collective-permute-start(bf16[528,512]{1,0:T(8,128)(2,1)S(1)} %maximum_maximum_fusion.own_ref), channel_id=1, source_target_pairs={{0,24},{8,0},{16,8},{24,16},{1,25},{9,1},{17,9},{25,17},{2,26},{10... | collective-permute-start | bytes 1622024 | tf_op jit(solution)/shard_map/ppermute | solution.py:19
  14.8 12.5 %all_to_all.20 = bf16[8,3,512]{2,1,0:T(4,128)(2,1)S(1)} all-to-all(bf16[8,3,512]{2,1,0:T(4,128)(2,1)} %bitcast.33), channel_id=1, replica_groups=mesh['zh'=8,'zl'=2,'y'=4,'c'=8] {'c'}, dimensions={0} | all-to-all | bytes 49152 | tf_op jit(solution)/shard_map/all_to_all | solution.py:23
  28.1 13.1 %all-to-all-start.2 = ((bf16[8,24,512]{2,1,0:T(8,128)(2,1)}), bf16[8,24,512]{2,1,0:T(8,128)(2,1)S(1)}, u32[]{:S(2)}, u32[]{:S(2)}) async-start(bf16[8,24,512]{2,1,0:T(8,128)(2,1)} %broadcast_in_dim.45), calls=%async_computation.2 | async-start | bytes 393216 | tf_op jit(solution)/shard_map/all_to_all | solution.py:23
  41.3 0.7 copy-done.1
  42.4 2.9 %local_sums.3 = f32[192,512]{1,0:T(8,128)} custom-call(s32[1]{0:T(128)} %bitcast.2.pos_ref, bf16[528,512]{1,0:T(8,128)(2,1)} %copy-done, bf16[528,512]{1,0:T(8,128)(2,1)} %copy-done.3, bf16[528,512]{1,0:T(8,128)(2,1)} %copy-done.2, bf16[528,512]{1,0:T(8,128)(2,1)} %copy-done.1), custom_call_target="tpu_custom_call" | custom-call | tf_op jit(solution)/shard_map/local_sums/pallas_call | solution.py:58
  45.3 2.6 %collective-permute-start.3 = (f32[192,512]{1,0:T(8,128)}, f32[192,512]{1,0:T(8,128)S(1)}, u32[]{:S(2)}, u32[]{:S(2)}) collective-permute-start(f32[192,512]{1,0:T(8,128)} %local_sums.3), channel_id=1, source_target_pairs={{0,32},{32,0},{1,33},{33,1},{2,34},{34,2},{3,35},{35,3},{4,36},{36... | collective-permute-start | bytes 1179656 | tf_op jit(solution)/shard_map/ppermute | solution.py:19
  48.0 3.0 %local_sums.2 = f32[192,512]{1,0:T(8,128)} custom-call(s32[1]{0:T(128)} %bitcast.pos_ref, bf16[528,512]{1,0:T(8,128)(2,1)} %copy-done, bf16[528,512]{1,0:T(8,128)(2,1)} %copy-done.3, bf16[528,512]{1,0:T(8,128)(2,1)} %copy-done.2, bf16[528,512]{1,0:T(8,128)(2,1)} %copy-done.1), custom_call_target="tpu_custom_call" | custom-call | tf_op jit(solution)/shard_map/local_sums/pallas_call | solution.py:58
  50.9 9.1 %collective-permute-done.3 = f32[192,512]{1,0:T(8,128)S(1)} collective-permute-done((f32[192,512]{1,0:T(8,128)}, f32[192,512]{1,0:T(8,128)S(1)}, u32[]{:S(2)}, u32[]{:S(2)}) %collective-permute-start.3) | collective-permute-done | bytes 393248 | tf_op jit(solution)/shard_map/ppermute | solution.py:19
  60.0 1.8 %add.72 = f32[192,512]{1,0:T(8,128)} add(f32[192,512]{1,0:T(8,128)} %local_sums.2, f32[192,512]{1,0:T(8,128)S(1)} %collective-permute-done.3) | non-fusion elementwise | flops 98304 | bytes 1179648 | tf_op jit(solution)/shard_map/add | solution.py:140
  61.8 11.0 %all-to-all-start = ((f32[8,24,512]{2,1,0:T(8,128)}), f32[8,24,512]{2,1,0:T(8,128)S(1)}, u32[]{:S(2)}, u32[]{:S(2)}) async-start(f32[8,24,512]{2,1,0:T(8,128)} %bitcast.3), calls=%async_computation | async-start | bytes 786432 | tf_op jit(solution)/shard_map/all_to_all | solution.py:23
  72.8 2.7 %collective-permute-start.4 = (bf16[192,512]{1,0:T(8,128)(2,1)S(1)}, bf16[192,512]{1,0:T(8,128)(2,1)S(1)}, u32[]{:S(2)}, u32[]{:S(2)}) collective-permute-start(bf16[192,512]{1,0:T(8,128)(2,1)S(1)} %bitcast.27), channel_id=1, source_target_pairs={{0,32},{32,0},{1,33},{33,1},{2,34},{34,2},{3,35},{35,3},{4,36},{36... | collective-permute-start | bytes 589832 | tf_op jit(solution)/shard_map/ppermute | solution.py:19
  76.2 18.8 %collective-permute-done.4.there_ref = bf16[192,512]{1,0:T(8,128)(2,1)S(1)} collective-permute-done((bf16[192,512]{1,0:T(8,128)(2,1)S(1)}, bf16[192,512]{1,0:T(8,128)(2,1)S(1)}, u32[]{:S(2)}, u32[]{:S(2)}) %collective-permute-start.4) | collective-permute-done | bytes 196640 | tf_op jit(solution)/shard_map/ppermute | solution.py:19
  95.7 4.4 %local_scores.1 = (f32[2,2,512]{2,1,0:T(2,128)}, f32[2,2,512]{2,1,0:T(2,128)}) custom-call(s32[6]{0:T(128)} %pad_add_fusion.pos_ref, bf16[528,512]{1,0:T(8,128)(2,1)} %copy-done, bf16[528,512]{1,0:T(8,128)(2,1)} %copy-done.3, bf16[528,512]{1,0:T(8,128)(2,1)} %copy-done.2, bf16[528,512]{1,0:T(8,128)(2,1)} %copy-done.1, bf16[192,512]{1,0:T(8,128)(2,1)} %bitcast.28, ...), custom_call_target="tpu_custom_call" | custom-call | tf_op jit(solution)/shard_map/local_scores/pallas_call | solution.py:102
  100.1 2.0 %collective-permute-start.5 = (f32[2,2,512]{2,1,0:T(2,128)}, f32[2,2,512]{2,1,0:T(2,128)S(1)}, u32[]{:S(2)}, u32[]{:S(2)}) collective-permute-start(f32[2,2,512]{2,1,0:T(2,128)} %get-tuple-element.5), channel_id=1, source_target_pairs={{0,8},{8,0},{16,24},{24,16},{1,9},{9,1},{17,25},{25,17},{2,10},{10... | collective-permute-start | bytes 24584 | tf_op jit(solution)/shard_map/ppermute | solution.py:150
  102.2 2.7 %collective-permute-done.5 = f32[2,2,512]{2,1,0:T(2,128)S(1)} collective-permute-done((f32[2,2,512]{2,1,0:T(2,128)}, f32[2,2,512]{2,1,0:T(2,128)S(1)}, u32[]{:S(2)}, u32[]{:S(2)}) %collective-permute-start.5) | collective-permute-done | bytes 8224 | tf_op jit(solution)/shard_map/ppermute | solution.py:150
  105.5 1.9 %collective-permute-start.6 = (f32[2,512]{1,0:T(2,128)S(1)}, f32[2,512]{1,0:T(2,128)S(1)}, u32[]{:S(2)}, u32[]{:S(2)}) collective-permute-start(f32[2,512]{1,0:T(2,128)S(1)} %slice_bitcast_fusion), channel_id=1, source_target_pairs={{0,24},{24,0},{8,16},{16,8},{1,25},{25,1},{9,17},{17,9},{2,26},{26... | collective-permute-start | bytes 12296 | tf_op jit(solution)/shard_map/ppermute | solution.py:151
  107.5 3.6 %collective-permute-done.6 = f32[2,512]{1,0:T(2,128)S(1)} collective-permute-done((f32[2,512]{1,0:T(2,128)S(1)}, f32[2,512]{1,0:T(2,128)S(1)}, u32[]{:S(2)}, u32[]{:S(2)}) %collective-permute-start.6) | collective-permute-done | bytes 4128 | tf_op jit(solution)/shard_map/ppermute | solution.py:151
  111.9 7.1 %all-to-all-start.3 = ((f32[8,1,2560]{2,1,0:T(1,128)}), f32[8,1,2560]{2,1,0:T(1,128)S(1)}, u32[]{:S(2)}, u32[]{:S(2)}) async-start(f32[8,1,2560]{2,1,0:T(1,128)} %pad_maximum_fusion), calls=%async_computation.3 | async-start | bytes 163840 | tf_op jit(solution)/shard_map/all_to_all | solution.py:23
  119.0 3.1 %multiply_reduce_fusion = f32[512]{0:T(512)S(1)} fusion(bf16[512,4096]{1,0:T(8,128)(2,1)} %param.4), kind=kLoop, calls=%fused_computation | loop fusion | flops 6290944 | bytes 4196352 | tf_op jit(solution)/shard_map/reduce_sum | solution.py:132
  122.1 1.9 %all-to-all-done.3 = f32[8,1,2560]{2,1,0:T(1,128)S(1)} async-done(((f32[8,1,2560]{2,1,0:T(1,128)}), f32[8,1,2560]{2,1,0:T(1,128)S(1)}, u32[]{:S(2)}, u32[]{:S(2)}) %all-to-all-start.3) | async-done | bytes 81952 | tf_op jit(solution)/shard_map/all_to_all | solution.py:23
  (43 shorter events, 5.8 us)
Async XLA Ops:
  3.3 38.0 %copy-start = (bf16[528,512]{1,0:T(8,128)(2,1)}, bf16[528,512]{1,0:T(8,128)(2,1)S(1)}, u32[]{:S(2)}) copy-start(bf16[528,512]{1,0:T(8,128)(2,1)S(1)} %maximum_maximum_fusion.own_ref) | copy-start | bytes 1622020
  3.3 37.9 %collective-permute-start.2 = (bf16[528,512]{1,0:T(8,128)(2,1)S(1)}, bf16[528,512]{1,0:T(8,128)(2,1)S(1)}, u32[]{:S(2)}, u32[]{:S(2)}) collective-permute-start(bf16[528,512]{1,0:T(8,128)(2,1)S(1)} %maximum_maximum_fusion.own_ref), channel_id=1, source_target_pairs={{0,8},{8,16},{16,24},{24,0},{1,9},{9,17},{17,25},{25,1},{2,10},{10... | collective-permute-start | bytes 1622024 | tf_op jit(solution)/shard_map/ppermute | solution.py:19
  7.3 33.9 %collective-permute-start.1 = (bf16[528,512]{1,0:T(8,128)(2,1)S(1)}, bf16[528,512]{1,0:T(8,128)(2,1)S(1)}, u32[]{:S(2)}, u32[]{:S(2)}) collective-permute-start(bf16[528,512]{1,0:T(8,128)(2,1)S(1)} %maximum_maximum_fusion.own_ref), channel_id=1, source_target_pairs={{0,16},{8,24},{16,0},{24,8},{1,17},{9,25},{17,1},{25,9},{2,18},{10... | collective-permute-start | bytes 1622024 | tf_op jit(solution)/shard_map/ppermute | solution.py:19
  11.8 29.4 %collective-permute-start = (bf16[528,512]{1,0:T(8,128)(2,1)S(1)}, bf16[528,512]{1,0:T(8,128)(2,1)S(1)}, u32[]{:S(2)}, u32[]{:S(2)}) collective-permute-start(bf16[528,512]{1,0:T(8,128)(2,1)S(1)} %maximum_maximum_fusion.own_ref), channel_id=1, source_target_pairs={{0,24},{8,0},{16,8},{24,16},{1,25},{9,1},{17,9},{25,17},{2,26},{10... | collective-permute-start | bytes 1622024 | tf_op jit(solution)/shard_map/ppermute | solution.py:19
  28.1 33.7 %all-to-all-start.2 = ((bf16[8,24,512]{2,1,0:T(8,128)(2,1)}), bf16[8,24,512]{2,1,0:T(8,128)(2,1)S(1)}, u32[]{:S(2)}, u32[]{:S(2)}) async-start(bf16[8,24,512]{2,1,0:T(8,128)(2,1)} %broadcast_in_dim.45), calls=%async_computation.2 | async-start | bytes 393216 | tf_op jit(solution)/shard_map/all_to_all | solution.py:23
  41.2 0.8 copy-start.1
  41.2 1.0 copy-start.2
  41.2 1.1 copy-start.3
  45.3 14.7 %collective-permute-start.3 = (f32[192,512]{1,0:T(8,128)}, f32[192,512]{1,0:T(8,128)S(1)}, u32[]{:S(2)}, u32[]{:S(2)}) collective-permute-start(f32[192,512]{1,0:T(8,128)} %local_sums.3), channel_id=1, source_target_pairs={{0,32},{32,0},{1,33},{33,1},{2,34},{34,2},{3,35},{35,3},{4,36},{36... | collective-permute-start | bytes 1179656 | tf_op jit(solution)/shard_map/ppermute | solution.py:19
  61.8 33.2 %copy-start.4 = (bf16[8,24,512]{2,1,0:T(8,128)(2,1)}, bf16[8,24,512]{2,1,0:T(8,128)(2,1)S(1)}, u32[]{:S(2)}) copy-start(bf16[8,24,512]{2,1,0:T(8,128)(2,1)S(1)} %all-to-all-done.2) | copy-start | bytes 589828
  61.8 49.3 %all-to-all-start = ((f32[8,24,512]{2,1,0:T(8,128)}), f32[8,24,512]{2,1,0:T(8,128)S(1)}, u32[]{:S(2)}, u32[]{:S(2)}) async-start(f32[8,24,512]{2,1,0:T(8,128)} %bitcast.3), calls=%async_computation | async-start | bytes 786432 | tf_op jit(solution)/shard_map/all_to_all | solution.py:23
  72.8 22.2 %collective-permute-start.4 = (bf16[192,512]{1,0:T(8,128)(2,1)S(1)}, bf16[192,512]{1,0:T(8,128)(2,1)S(1)}, u32[]{:S(2)}, u32[]{:S(2)}) collective-permute-start(bf16[192,512]{1,0:T(8,128)(2,1)S(1)} %bitcast.27), channel_id=1, source_target_pairs={{0,32},{32,0},{1,33},{33,1},{2,34},{34,2},{3,35},{35,3},{4,36},{36... | collective-permute-start | bytes 589832 | tf_op jit(solution)/shard_map/ppermute | solution.py:19
  95.0 0.7 copy-start.6
  100.1 23.9 %copy-start.5 = (bf16[3,4096]{1,0:T(4,128)(2,1)S(1)}, bf16[3,4096]{1,0:T(4,128)(2,1)}, u32[]{:S(2)}) copy-start(bf16[3,4096]{1,0:T(4,128)(2,1)} %param.7) | copy-start | bytes 73732
  100.1 4.7 %collective-permute-start.5 = (f32[2,2,512]{2,1,0:T(2,128)}, f32[2,2,512]{2,1,0:T(2,128)S(1)}, u32[]{:S(2)}, u32[]{:S(2)}) collective-permute-start(f32[2,2,512]{2,1,0:T(2,128)} %get-tuple-element.5), channel_id=1, source_target_pairs={{0,8},{8,0},{16,24},{24,16},{1,9},{9,1},{17,25},{25,17},{2,10},{10... | collective-permute-start | bytes 24584 | tf_op jit(solution)/shard_map/ppermute | solution.py:150
  105.5 5.5 %collective-permute-start.6 = (f32[2,512]{1,0:T(2,128)S(1)}, f32[2,512]{1,0:T(2,128)S(1)}, u32[]{:S(2)}, u32[]{:S(2)}) collective-permute-start(f32[2,512]{1,0:T(2,128)S(1)} %slice_bitcast_fusion), channel_id=1, source_target_pairs={{0,24},{24,0},{8,16},{16,8},{1,25},{25,1},{9,17},{17,9},{2,26},{26... | collective-permute-start | bytes 12296 | tf_op jit(solution)/shard_map/ppermute | solution.py:151
  111.9 12.0 %all-to-all-start.3 = ((f32[8,1,2560]{2,1,0:T(1,128)}), f32[8,1,2560]{2,1,0:T(1,128)S(1)}, u32[]{:S(2)}, u32[]{:S(2)}) async-start(f32[8,1,2560]{2,1,0:T(1,128)} %pad_maximum_fusion), calls=%async_computation.3 | async-start | bytes 163840 | tf_op jit(solution)/shard_map/all_to_all | solution.py:23

commit v5 on v4

v5 whole, which is shorter than its diff:
```python
import functools

import jax
import jax.numpy as jnp
from jax import lax
from jax.experimental import pallas as pl
from jax.experimental.pallas import tpu as pltpu
from jax.sharding import Mesh
from jax.sharding import PartitionSpec as P


D = 4096
ZH, ZL, NY, NC = 8, 2, 4, 8
NZ = ZH * ZL
DP = ("zh", "zl", "y")
CLUS_DP = ("c", "zh", "zl", "y")
EPS = 1e-06


def shifted(x, axis, size, by):
    return lax.ppermute(x, axis, [(i, (i + by) % size) for i in range(size)])


def exchange(x, axis):
    return lax.all_to_all(x, axis, 0, 0, tiled=True)


def copies(x, count):
    return jnp.broadcast_to(x, (count, *x.shape))


LIMIT = pltpu.CompilerParams(vmem_limit_bytes=12 * 1024 * 1024)


def near(x):
    return pltpu.with_memory_space_constraint(x, pltpu.VMEM)


def far(x):
    return pltpu.with_memory_space_constraint(x, pltpu.HBM)


def pack_kernel(pos_ref, ids_ref, table_ref, emb_ref, out_ref, rows_ref, in_ref, list_ref, sems):
    points, width = emb_ref.shape[0], out_ref.shape[1]
    start = pl.multiple_of(pos_ref[2] * width, width)
    copy = pltpu.make_async_copy(
        emb_ref.at[:, pl.ds(start, width)], out_ref.at[pl.ds(0, points), :], sems.at[0]
    )
    copy.start()
    small = [
        pltpu.make_async_copy(ids_ref, in_ref, sems.at[1]),
        pltpu.make_async_copy(table_ref, list_ref, sems.at[2]),
    ]
    for each in small:
        each.start()
    for each in small:
        each.wait()
    groups = table_ref.shape[0] // 128
    rows_ref[...] = jnp.zeros(rows_ref.shape, jnp.float32)
    for g in range(groups):
        slots = list_ref[g * 128 : (g + 1) * 128].reshape(1, 128)
        rows_ref[g : g + 1, :] = lax.shift_right_logical(slots, 6).astype(jnp.float32)
        rows_ref[16 + g : 17 + g, :] = (slots & 63).astype(jnp.float32)
    ids = in_ref[...]
    low = lax.broadcasted_iota(jnp.int32, (128, points), 0) == (ids & 127)
    got = jnp.dot(
        rows_ref[...].astype(jnp.bfloat16),
        low.astype(jnp.float32).astype(jnp.bfloat16),
        preferred_element_type=jnp.float32,
    )
    high = lax.broadcasted_iota(jnp.int32, (16, points), 0)
    chosen = high == lax.shift_right_logical(ids, 7)
    coarse = jnp.sum(jnp.where(chosen, got[:16], 0.0), axis=0, keepdims=True)
    fine = jnp.sum(jnp.where(chosen, got[16:], 0.0), axis=0, keepdims=True)
    tail = jnp.where(high == 0, coarse, jnp.where(high == 1, fine, 0.0))
    out_ref[points : points + 16, :] = tail.astype(jnp.bfloat16)
    copy.wait()


def pack(pos, assignment, slot_of, embeddings):
    points, width = embeddings.shape[0], D // NC
    vmem = pl.BlockSpec(memory_space=pltpu.VMEM)
    return pl.pallas_call(
        pack_kernel,
        out_shape=jax.ShapeDtypeStruct((points + 16, width), jnp.bfloat16),
        in_specs=[pl.BlockSpec(memory_space=pltpu.SMEM)]
        + [pl.BlockSpec(memory_space=pltpu.HBM)] * 3,
        out_specs=vmem,
        scratch_shapes=[
            pltpu.VMEM((32, 128), jnp.float32),
            pltpu.VMEM((1, points), jnp.int32),
            pltpu.VMEM(slot_of.shape, jnp.int32),
            pltpu.SemaphoreType.DMA((3,)),
        ],
        compiler_params=LIMIT,
        name="pack",
    )(pos, *map(far, (assignment[None, :], slot_of, embeddings)))


def ending_kernel(got_ref, old_ref, new_ref, dist_ref):
    width = D // NC
    points = dist_ref.shape[1]
    old = old_ref[...].astype(jnp.float32)
    for c in range(NC):
        for k in range(3):
            new_ref[k : k + 1, c * width : (c + 1) * width] = got_ref[
                c : c + 1, k * width : (k + 1) * width
            ]
    overall = new_ref[...] + old
    size = jnp.mean(overall * overall, axis=1, keepdims=True)
    new_ref[...] = overall * lax.rsqrt(size + EPS)
    scores = jnp.sum(got_ref[:, 3 * width :], axis=0, keepdims=True)
    cent_rms = jnp.sqrt(scores[:, points : 2 * points] / jnp.float32(D) + EPS)
    root_mean = jnp.sqrt(scores[:, 2 * points :] / jnp.float32(D) + EPS)
    dist_ref[...] = 1.0 - scores[:, :points] / (jnp.float32(D) * root_mean * cent_rms)


def ending(got, old, points):
    vmem = pl.BlockSpec(memory_space=pltpu.VMEM)
    return pl.pallas_call(
        ending_kernel,
        out_shape=(
            jax.ShapeDtypeStruct(old.shape, jnp.float32),
            jax.ShapeDtypeStruct((1, points), jnp.float32),
        ),
        in_specs=[vmem, vmem],
        out_specs=(vmem, vmem),
        compiler_params=LIMIT,
        name="ending",
    )(near(got), near(old))


def slot_column(rows, pos_ref, partner):
    r = lax.broadcasted_iota(jnp.int32, (rows, 1), 0)
    per_z = NC * 3
    zh = r // per_z
    c = (r % per_z) // 3
    half = 1 - pos_ref[1] if partner else pos_ref[1]
    first = (half * NY + pos_ref[0]) * 3
    return c * (NZ * NY * 3) + zh * (ZL * NY * 3) + r % 3 + first


def id_row(ref, points):
    tail = ref[points : points + 16, :].astype(jnp.float32)
    return (tail[0:1, :] * 64.0 + tail[1:2, :]).astype(jnp.int32)


def sums_kernel(partner, pos_ref, own_ref, a_ref, b_ref, c_ref, *out_refs):
    points = own_ref.shape[0] - 16
    wanted = slot_column(out_refs[0].shape[0], pos_ref, partner)
    total = None
    for ref in (own_ref, a_ref, b_ref, c_ref):
        hot = (wanted == id_row(ref, points)).astype(jnp.float32).astype(jnp.bfloat16)
        got = jnp.dot(hot, ref[0:points, :], preferred_element_type=jnp.float32)
        total = got if total is None else total + got
    width = out_refs[0].shape[1]
    for i, out_ref in enumerate(out_refs):
        out_ref[...] = total[:, i * width : (i + 1) * width]


def local_sums(pos, own, others, cuts, partner):
    rows = ZH * NC * 3
    width = own.shape[1] // cuts
    vmem = pl.BlockSpec(memory_space=pltpu.VMEM)
    return pl.pallas_call(
        functools.partial(sums_kernel, partner),
        out_shape=(jax.ShapeDtypeStruct((rows, width), jnp.float32),) * cuts,
        in_specs=[pl.BlockSpec(memory_space=pltpu.SMEM)] + [vmem] * 4,
        out_specs=(vmem,) * cuts,
        compiler_params=LIMIT,
        name="local_sums",
    )(pos, *map(near, (own, *others)))


def merge_kernel(home_ref, a_ref, b_ref, out_ref):
    width = a_ref.shape[1]
    out_ref[:, :width] = home_ref[:, :width] + a_ref[...]
    out_ref[:, width:] = home_ref[:, width:] + b_ref[...]


def merged(home, a, b):
    vmem = pl.BlockSpec(memory_space=pltpu.VMEM)
    return pl.pallas_call(
        merge_kernel,
        out_shape=jax.ShapeDtypeStruct(home.shape, jnp.float32),
        in_specs=[vmem] * 3,
        out_specs=vmem,
        compiler_params=LIMIT,
        name="merged",
    )(*map(near, (home, a, b)))


def score_kernel(pos_ref, own_ref, a_ref, b_ref, c_ref, here_ref, there_ref, keep_ref, give_ref, size_ref):
    points = own_ref.shape[0] - 16
    wide = own_ref[0:points, :].astype(jnp.float32)
    wide = wide * wide
    high = wide.astype(jnp.bfloat16)
    low = (wide - high.astype(jnp.float32)).astype(jnp.bfloat16)
    ones = jnp.ones((16, wide.shape[1]), jnp.bfloat16)
    across = (((1,), (1,)), ((), ()))
    sizes = [
        lax.dot_general(ones, part, across, preferred_element_type=jnp.float32)
        for part in (high, low)
    ]
    size_ref[...] = (sizes[0] + sizes[1])[0:1, :]
    parts = []
    for partner, ref in enumerate((here_ref, there_ref)):
        rows = ref[...]
        wide = rows.astype(jnp.float32)
        square = jnp.sum(wide * wide, axis=1, keepdims=True)
        parts.append((rows, square, slot_column(rows.shape[0], pos_ref, partner)))
    for by, ref in enumerate((own_ref, a_ref, b_ref, c_ref)):
        ids = id_row(ref, points)
        score = size = None
        for rows, square, wanted in parts:
            raw = lax.dot_general(
                rows,
                ref[0:points, :],
                (((1,), (1,)), ((), ())),
                preferred_element_type=jnp.float32,
            )
            hit = wanted == ids
            got = jnp.sum(jnp.where(hit, raw, 0.0), axis=0, keepdims=True)
            more = jnp.sum(jnp.where(hit, square, 0.0), axis=0, keepdims=True)
            score = got if score is None else score + got
            size = more if size is None else size + more
        y = pos_ref[0]
        source = lax.rem(y + by, NY)
        beside = y + 1 - 2 * lax.rem(y, 2)
        role = jnp.where(
            source == y, 0, jnp.where(source == 3 - y, 1, jnp.where(source == beside, 2, 3))
        )
        for out_ref, wanted in ((keep_ref, role < 2), (give_ref, role >= 2)):

            @pl.when(wanted)
            def _(out_ref=out_ref, score=score, size=size, place=lax.rem(role, 2)):
                out_ref[place, 0:1, :] = score
                out_ref[place, 1:2, :] = size


def local_scores(pos, own, others, here, there):
    points = own.shape[0] - 16
    vmem = pl.BlockSpec(memory_space=pltpu.VMEM)
    return pl.pallas_call(
        score_kernel,
        out_shape=(jax.ShapeDtypeStruct((2, 2, points), jnp.float32),) * 2
        + (jax.ShapeDtypeStruct((1, points), jnp.float32),),
        in_specs=[pl.BlockSpec(memory_space=pltpu.SMEM)] + [vmem] * 6,
        out_specs=(vmem,) * 3,
        compiler_params=LIMIT,
        name="local_scores",
    )(pos, *map(near, (own, *others, here, there)))


def steps(embeddings, assignment, slot_of, old_centroids):
    points = embeddings.shape[0]
    width = D // NC
    c = lax.axis_index("c")
    y = lax.axis_index("y")
    zl = lax.axis_index("zl")

    pos = jnp.stack([y, zl, c]).astype(jnp.int32)
    packed = pack(pos, assignment, slot_of, embeddings)
    far = shifted(packed, "y", NY, 2)
    after = shifted(packed, "y", NY, -1)
    before = shifted(packed, "y", NY, 1)
    others = [after, far, before]
    cent = exchange(old_centroids.reshape(3, NC, width).swapaxes(0, 1), "c")

    here = exchange(copies(cent.reshape(NC * 3, width), ZH), "zh")
    here = here.reshape(ZH * NC * 3, width)

    away = local_sums(pos, packed, others, 2, True)
    beside = [(z, (z - 1 if z % ZL == 0 else z + 1) % NZ) for z in range(NZ)]
    arrived = shifted(away[0], "zl", ZL, 1), lax.ppermute(away[1], ("zh", "zl"), beside)
    (home,) = local_sums(pos, packed, others, 1, False)
    there = lax.ppermute(here, ("zh", "zl"), beside)
    both = merged(home, *arrived).reshape(ZH, NC * 3, width)
    summed = exchange(both, "zh")
    summed = summed.sum(axis=0)

    keep, give, size = local_scores(pos, packed, others, here, there)
    kept = keep + lax.ppermute(give, "y", [(0, 1), (1, 0), (2, 3), (3, 2)])
    scored = kept[0] + lax.ppermute(kept[1], "y", [(0, 3), (3, 0), (1, 2), (2, 1)])

    sends = jnp.concatenate(
        [
            summed.reshape(NC, 1, 3 * width),
            jnp.broadcast_to(scored.reshape(1, 1, 2 * points), (NC, 1, 2 * points)),
            jnp.broadcast_to(size[None], (NC, 1, points)),
        ],
        axis=2,
    )
    got = exchange(sends, "c")[:, 0]
    updated, distance = ending(got, old_centroids, points)
    return (updated, distance[0])


def solution(mesh):
    split = Mesh(mesh.devices.reshape(ZH, ZL, NY, NC), ("zh", "zl", "y", "c"))
    return jax.shard_map(
        steps,
        mesh=split,
        in_specs=(P(DP, None), P(DP), P(), P(CLUS_DP, None)),
        out_specs=(P(CLUS_DP, None), P(DP)),
        check_vma=False,
    )
```

time: 126 us -> 116 us (0.921)
  blocking collectives: 12.5 us -> 23 us
  waiting for transfers between devices: 36.1 us -> 26.2 us
  other arithmetic: 9.91 us -> 0.19 us
  starting transfers between devices: 51.9 us -> 55.8 us
  local copies, waits for them, and re-layouts: 3.81 us -> 0.82 us
  Pallas kernels: 10.3 us -> 8.67 us
    ppermute x5 -> x4, waiting for transfers between devices: 28 us -> 0.45 us  [shifted(): return lax.ppermute(x, axis, [(i, (i + by) % size) for i in range(size)])]
    ppermute x0 -> x2, waiting for transfers between devices: none -> 23.3 us  [the longest x1 19.8 us: steps(): there = lax.ppermute(here, ('zh', 'zl'), beside)]
    ppermute x0 -> x2, starting transfers between devices: none -> 14.2 us  [the longest x1 9.36 us: steps(): lax.ppermute(away[1], ('zh', 'zl'), beside)]
    all_to_all x1 -> x2, blocking collectives: 12.5 us -> 23 us  [exchange(): return lax.all_to_all(x, axis, 0, 0, tiled=True)]
    all_to_all x3 -> x2, starting transfers between devices: 31.1 us -> 21.1 us  [exchange(): return lax.all_to_all(x, axis, 0, 0, tiled=True)]
    reduce_sum x4 -> x0, other arithmetic: 4.49 us -> none  [the longest x1 3.08 us: steps(): root_mean = jnp.sqrt(jnp.mean(widened * widened, axis=1) + EPS)]
    ppermute x5 -> x4, starting transfers between devices: 16.8 us -> 13 us  [shifted(): return lax.ppermute(x, axis, [(i, (i + by) % size) for i in range(size)])]
    ppermute x1, waiting for transfers between devices: 3.63 us -> 1.45 us  [steps(): lax.ppermute(kept[1], 'y', [(0, 3), (3, 0), (1, 2), (2, 1)])]
  transfers between devices with their start and end apart: 10 -> 10, of which waited for: 5 -> 5; matrix products, arithmetic and copies ran while one was open for 6% -> 1% of each run, Pallas kernels for 8% -> 5%
where the time goes in v5:
time: 116 us
  starting transfers between devices  55.8 us (48%)
  waiting for transfers between devices  26.2 us (23%)
  blocking collectives  23 us (20%)
  Pallas kernels  8.67 us (7%)
    all_to_all x2, blocking collectives, exchange(): return lax.all_to_all(x, axis, 0, 0, tiled=True)  23 us
    all_to_all x2, starting transfers between devices, exchange(): return lax.all_to_all(x, axis, 0, 0, tiled=True)  21.1 us
    ppermute x1, waiting for transfers between devices, steps(): there = lax.ppermute(here, ('zh', 'zl'), beside)  19.8 us
    ppermute x4, starting transfers between devices, shifted(): return lax.ppermute(x, axis, [(i, (i + by) % size) for i in range(size)])  13 us
    ppermute x1, starting transfers between devices, steps(): lax.ppermute(away[1], ('zh', 'zl'), beside)  9.36 us
    ppermute x1, starting transfers between devices, steps(): there = lax.ppermute(here, ('zh', 'zl'), beside)  4.84 us
    ppermute x1, starting transfers between devices, steps(): lax.ppermute(kept[1], 'y', [(0, 3), (3, 0), (1, 2), (2, 1)])  4.09 us
    ppermute x1, starting transfers between devices, steps(): kept = keep + lax.ppermute(give, 'y', [(0, 1), (1, 0), (2, 3), (3, 2)])  3.54 us
  transfers between devices with their start and end apart: 10, of which 5 were waited for; matrix products, arithmetic and copies ran while one was open for 1% of the time, Pallas kernels for 5%

profile of v5, /device:TPU:1, one launch (start us, length us, event | category | flops | bytes accessed | tf_op | source)
XLA Modules:
  0.0 115.6 jit_solution(9045209766205609468)
XLA Ops:
  0.7 1.7 %pack.1.own_ref = bf16[528,512]{1,0:T(8,128)(2,1)S(1)} custom-call(s32[3]{0:T(128)S(1)} %pad_add_fusion.pos_ref, s32[1,512]{1,0:T(1,128)} %bitcast.31, s32[1536]{0:T(1024)} %table_ref.1, bf16[512,4096]{1,0:T(8,128)(2,1)} %emb_ref.1), custom_call_target="tpu_custom_call" | custom-call | tf_op jit(solution)/shard_map/pack/pallas_call | solution.py:83
  2.5 5.5 %collective-permute-start = (bf16[528,512]{1,0:T(8,128)(2,1)S(1)}, bf16[528,512]{1,0:T(8,128)(2,1)S(1)}, u32[]{:S(2)}, u32[]{:S(2)}) collective-permute-start(bf16[528,512]{1,0:T(8,128)(2,1)S(1)} %pack.1.own_ref), channel_id=1, source_target_pairs={{0,24},{8,0},{16,8},{24,16},{1,25},{9,1},{17,9},{25,17},{2,26},{10... | collective-permute-start | bytes 1622024 | tf_op jit(solution)/shard_map/ppermute | solution.py:21
  7.9 2.3 %collective-permute-start.1 = (bf16[528,512]{1,0:T(8,128)(2,1)S(1)}, bf16[528,512]{1,0:T(8,128)(2,1)S(1)}, u32[]{:S(2)}, u32[]{:S(2)}) collective-permute-start(bf16[528,512]{1,0:T(8,128)(2,1)S(1)} %pack.1.own_ref), channel_id=1, source_target_pairs={{0,16},{8,24},{16,0},{24,8},{1,17},{9,25},{17,1},{25,9},{2,18},{10... | collective-permute-start | bytes 1622024 | tf_op jit(solution)/shard_map/ppermute | solution.py:21
  10.2 2.6 %collective-permute-start.2 = (bf16[528,512]{1,0:T(8,128)(2,1)S(1)}, bf16[528,512]{1,0:T(8,128)(2,1)S(1)}, u32[]{:S(2)}, u32[]{:S(2)}) collective-permute-start(bf16[528,512]{1,0:T(8,128)(2,1)S(1)} %pack.1.own_ref), channel_id=1, source_target_pairs={{0,8},{8,16},{16,24},{24,0},{1,9},{9,17},{17,25},{25,1},{2,10},{10... | collective-permute-start | bytes 1622024 | tf_op jit(solution)/shard_map/ppermute | solution.py:21
  12.8 11.6 %all_to_all.20 = bf16[8,3,512]{2,1,0:T(4,128)(2,1)S(1)} all-to-all(bf16[8,3,512]{2,1,0:T(4,128)(2,1)S(1)} %bitcast.28), channel_id=1, replica_groups=mesh['zh'=8,'zl'=2,'y'=4,'c'=8] {'c'}, dimensions={0} | all-to-all | bytes 49152 | tf_op jit(solution)/shard_map/all_to_all | solution.py:25
  24.4 0.7 broadcast_in_dim.22
  25.1 13.7 %all-to-all-start.2 = ((bf16[8,24,512]{2,1,0:T(8,128)(2,1)}), bf16[8,24,512]{2,1,0:T(8,128)(2,1)S(1)}, u32[]{:S(2)}, u32[]{:S(2)}) async-start(bf16[8,24,512]{2,1,0:T(8,128)(2,1)} %broadcast_in_dim.22), calls=%async_computation.2 | async-start | bytes 393216 | tf_op jit(solution)/shard_map/all_to_all | solution.py:25
  38.9 1.2 %local_sums.3 = (f32[192,256]{1,0:T(8,128)S(1)}, f32[192,256]{1,0:T(8,128)S(1)}) custom-call(s32[3]{0:T(128)S(1)} %pad_add_fusion.pos_ref, bf16[528,512]{1,0:T(8,128)(2,1)S(1)} %pack.1.own_ref, bf16[528,512]{1,0:T(8,128)(2,1)S(1)} %collective-permute-done.a_ref, bf16[528,512]{1,0:T(8,128)(2,1)S(1)} %collective-permute-done.1.b_ref, ...), custom_call_target="tpu_custom_call" | custom-call | tf_op jit(solution)/shard_map/local_sums/pallas_call | solution.py:165
  40.1 2.6 %collective-permute-start.3 = (f32[192,256]{1,0:T(8,128)S(1)}, f32[192,256]{1,0:T(8,128)S(1)}, u32[]{:S(2)}, u32[]{:S(2)}) collective-permute-start(f32[192,256]{1,0:T(8,128)S(1)} %get-tuple-element.9), channel_id=1, source_target_pairs={{0,32},{32,0},{1,33},{33,1},{2,34},{34,2},{3,35},{35,3},{4,36},{36... | collective-permute-start | bytes 589832 | tf_op jit(solution)/shard_map/ppermute | solution.py:21
  42.7 9.4 %collective-permute-start.4 = (f32[192,256]{1,0:T(8,128)S(1)}, f32[192,256]{1,0:T(8,128)S(1)}, u32[]{:S(2)}, u32[]{:S(2)}) collective-permute-start(f32[192,256]{1,0:T(8,128)S(1)} %get-tuple-element.10), channel_id=1, source_target_pairs={{0,480},{32,64},{64,32},{96,128},{128,96},{160,192},{192,160},{224... | collective-permute-start | bytes 589832 | tf_op jit(solution)/shard_map/ppermute | solution.py:275
  52.1 1.2 %local_sums.2.home_ref = f32[192,512]{1,0:T(8,128)S(1)} custom-call(s32[3]{0:T(128)S(1)} %pad_add_fusion.pos_ref, bf16[528,512]{1,0:T(8,128)(2,1)S(1)} %pack.1.own_ref, bf16[528,512]{1,0:T(8,128)(2,1)S(1)} %collective-permute-done.a_ref, bf16[528,512]{1,0:T(8,128)(2,1)S(1)} %collective-permute-done.1.b_ref, bf16[528,512]{1,0:T(8,128)(2,1)S(1)} %collective-permute-done.2.c_ref), custom_call_target="tpu_custom_call" | custom-call | tf_op jit(solution)/shard_map/local_sums/pallas_call | solution.py:165
  53.3 0.4 collective-permute-done.3.a_ref
  53.7 3.5 %collective-permute-done.4.b_ref = f32[192,256]{1,0:T(8,128)S(1)} collective-permute-done((f32[192,256]{1,0:T(8,128)S(1)}, f32[192,256]{1,0:T(8,128)S(1)}, u32[]{:S(2)}, u32[]{:S(2)}) %collective-permute-start.4) | collective-permute-done | bytes 196640 | tf_op jit(solution)/shard_map/ppermute | solution.py:275
  57.2 0.8 merged.1
  58.0 7.3 %all-to-all-start = ((f32[8,24,512]{2,1,0:T(8,128)}), f32[8,24,512]{2,1,0:T(8,128)S(1)}, u32[]{:S(2)}, u32[]{:S(2)}) async-start(f32[8,24,512]{2,1,0:T(8,128)} %bitcast.4), calls=%async_computation | async-start | bytes 786432 | tf_op jit(solution)/shard_map/all_to_all | solution.py:25
  65.3 4.8 %collective-permute-start.5 = (bf16[192,512]{1,0:T(8,128)(2,1)S(1)}, bf16[192,512]{1,0:T(8,128)(2,1)S(1)}, u32[]{:S(2)}, u32[]{:S(2)}) collective-permute-start(bf16[192,512]{1,0:T(8,128)(2,1)S(1)} %bitcast.25), channel_id=1, source_target_pairs={{0,480},{32,64},{64,32},{96,128},{128,96},{160,192},{192,160},{224... | collective-permute-start | bytes 589832 | tf_op jit(solution)/shard_map/ppermute | solution.py:277
  70.2 19.8 %collective-permute-done.5.there_ref = bf16[192,512]{1,0:T(8,128)(2,1)S(1)} collective-permute-done((bf16[192,512]{1,0:T(8,128)(2,1)S(1)}, bf16[192,512]{1,0:T(8,128)(2,1)S(1)}, u32[]{:S(2)}, u32[]{:S(2)}) %collective-permute-start.5) | collective-permute-done | bytes 196640 | tf_op jit(solution)/shard_map/ppermute | solution.py:277
  90.0 3.0 %local_scores.1 = (f32[2,2,512]{2,1,0:T(2,128)S(1)}, f32[2,2,512]{2,1,0:T(2,128)S(1)}, f32[1,512]{1,0:T(1,128)S(1)}) custom-call(s32[3]{0:T(128)S(1)} %pad_add_fusion.pos_ref, bf16[528,512]{1,0:T(8,128)(2,1)S(1)} %pack.1.own_ref, bf16[528,512]{1,0:T(8,128)(2,1)S(1)} %collective-permute-done.a_ref, bf16[528,512]{1,0:T(8,128)(2,1)S(1)} %collective-permute-done.1.b_ref, ...), custom_call_target="tpu_custom_call" | custom-call | tf_op jit(solution)/shard_map/local_scores/pallas_call | solution.py:244
  93.0 3.5 %collective-permute-start.6 = (f32[2,2,512]{2,1,0:T(2,128)S(1)}, f32[2,2,512]{2,1,0:T(2,128)S(1)}, u32[]{:S(2)}, u32[]{:S(2)}) collective-permute-start(f32[2,2,512]{2,1,0:T(2,128)S(1)} %get-tuple-element.12), channel_id=1, source_target_pairs={{0,8},{8,0},{16,24},{24,16},{1,9},{9,1},{17,25},{25,17},{2,10},{10... | collective-permute-start | bytes 24584 | tf_op jit(solution)/shard_map/ppermute | solution.py:283
  96.5 1.0 collective-permute-done.6
  97.6 4.1 %collective-permute-start.7 = (f32[2,512]{1,0:T(2,128)S(1)}, f32[2,512]{1,0:T(2,128)S(1)}, u32[]{:S(2)}, u32[]{:S(2)}) collective-permute-start(f32[2,512]{1,0:T(2,128)S(1)} %slice_bitcast_fusion), channel_id=1, source_target_pairs={{0,24},{24,0},{8,16},{16,8},{1,25},{25,1},{9,17},{17,9},{2,26},{26... | collective-permute-start | bytes 12296 | tf_op jit(solution)/shard_map/ppermute | solution.py:284
  101.7 1.5 %collective-permute-done.7 = f32[2,512]{1,0:T(2,128)S(1)} collective-permute-done((f32[2,512]{1,0:T(2,128)S(1)}, f32[2,512]{1,0:T(2,128)S(1)}, u32[]{:S(2)}, u32[]{:S(2)}) %collective-permute-start.7) | collective-permute-done | bytes 4128 | tf_op jit(solution)/shard_map/ppermute | solution.py:284
  103.3 11.4 %all_to_all.21 = f32[8,1,3072]{2,1,0:T(1,128)S(1)} all-to-all(f32[8,1,3072]{2,1,0:T(1,128)S(1)} %maximum_maximum_fusion), channel_id=1, replica_groups=mesh['zh'=8,'zl'=2,'y'=4,'c'=8] {'c'}, dimensions={0} | all-to-all | bytes 196608 | tf_op jit(solution)/shard_map/all_to_all | solution.py:25
  114.8 0.8 ending.1
  (19 shorter events, 0.3 us)
Async XLA Ops:
  0.6 12.2 %copy-start = (bf16[3,4096]{1,0:T(4,128)(2,1)S(1)}, bf16[3,4096]{1,0:T(4,128)(2,1)}, u32[]{:S(2)}) copy-start(bf16[3,4096]{1,0:T(4,128)(2,1)} %old_ref.1) | copy-start | bytes 73732
  2.5 36.4 %collective-permute-start = (bf16[528,512]{1,0:T(8,128)(2,1)S(1)}, bf16[528,512]{1,0:T(8,128)(2,1)S(1)}, u32[]{:S(2)}, u32[]{:S(2)}) collective-permute-start(bf16[528,512]{1,0:T(8,128)(2,1)S(1)} %pack.1.own_ref), channel_id=1, source_target_pairs={{0,24},{8,0},{16,8},{24,16},{1,25},{9,1},{17,9},{25,17},{2,26},{10... | collective-permute-start | bytes 1622024 | tf_op jit(solution)/shard_map/ppermute | solution.py:21
  7.9 30.9 %collective-permute-start.1 = (bf16[528,512]{1,0:T(8,128)(2,1)S(1)}, bf16[528,512]{1,0:T(8,128)(2,1)S(1)}, u32[]{:S(2)}, u32[]{:S(2)}) collective-permute-start(bf16[528,512]{1,0:T(8,128)(2,1)S(1)} %pack.1.own_ref), channel_id=1, source_target_pairs={{0,16},{8,24},{16,0},{24,8},{1,17},{9,25},{17,1},{25,9},{2,18},{10... | collective-permute-start | bytes 1622024 | tf_op jit(solution)/shard_map/ppermute | solution.py:21
  10.2 28.7 %collective-permute-start.2 = (bf16[528,512]{1,0:T(8,128)(2,1)S(1)}, bf16[528,512]{1,0:T(8,128)(2,1)S(1)}, u32[]{:S(2)}, u32[]{:S(2)}) collective-permute-start(bf16[528,512]{1,0:T(8,128)(2,1)S(1)} %pack.1.own_ref), channel_id=1, source_target_pairs={{0,8},{8,16},{16,24},{24,0},{1,9},{9,17},{17,25},{25,1},{2,10},{10... | collective-permute-start | bytes 1622024 | tf_op jit(solution)/shard_map/ppermute | solution.py:21
  25.1 32.9 %all-to-all-start.2 = ((bf16[8,24,512]{2,1,0:T(8,128)(2,1)}), bf16[8,24,512]{2,1,0:T(8,128)(2,1)S(1)}, u32[]{:S(2)}, u32[]{:S(2)}) async-start(bf16[8,24,512]{2,1,0:T(8,128)(2,1)} %broadcast_in_dim.22), calls=%async_computation.2 | async-start | bytes 393216 | tf_op jit(solution)/shard_map/all_to_all | solution.py:25
  40.1 13.6 %collective-permute-start.3 = (f32[192,256]{1,0:T(8,128)S(1)}, f32[192,256]{1,0:T(8,128)S(1)}, u32[]{:S(2)}, u32[]{:S(2)}) collective-permute-start(f32[192,256]{1,0:T(8,128)S(1)} %get-tuple-element.9), channel_id=1, source_target_pairs={{0,32},{32,0},{1,33},{33,1},{2,34},{34,2},{3,35},{35,3},{4,36},{36... | collective-permute-start | bytes 589832 | tf_op jit(solution)/shard_map/ppermute | solution.py:21
  42.7 14.5 %collective-permute-start.4 = (f32[192,256]{1,0:T(8,128)S(1)}, f32[192,256]{1,0:T(8,128)S(1)}, u32[]{:S(2)}, u32[]{:S(2)}) collective-permute-start(f32[192,256]{1,0:T(8,128)S(1)} %get-tuple-element.10), channel_id=1, source_target_pairs={{0,480},{32,64},{64,32},{96,128},{128,96},{160,192},{192,160},{224... | collective-permute-start | bytes 589832 | tf_op jit(solution)/shard_map/ppermute | solution.py:275
  58.0 45.1 %all-to-all-start = ((f32[8,24,512]{2,1,0:T(8,128)}), f32[8,24,512]{2,1,0:T(8,128)S(1)}, u32[]{:S(2)}, u32[]{:S(2)}) async-start(f32[8,24,512]{2,1,0:T(8,128)} %bitcast.4), calls=%async_computation | async-start | bytes 786432 | tf_op jit(solution)/shard_map/all_to_all | solution.py:25
  65.3 24.6 %collective-permute-start.5 = (bf16[192,512]{1,0:T(8,128)(2,1)S(1)}, bf16[192,512]{1,0:T(8,128)(2,1)S(1)}, u32[]{:S(2)}, u32[]{:S(2)}) collective-permute-start(bf16[192,512]{1,0:T(8,128)(2,1)S(1)} %bitcast.25), channel_id=1, source_target_pairs={{0,480},{32,64},{64,32},{96,128},{128,96},{160,192},{192,160},{224... | collective-permute-start | bytes 589832 | tf_op jit(solution)/shard_map/ppermute | solution.py:277
  93.0 4.6 %collective-permute-start.6 = (f32[2,2,512]{2,1,0:T(2,128)S(1)}, f32[2,2,512]{2,1,0:T(2,128)S(1)}, u32[]{:S(2)}, u32[]{:S(2)}) collective-permute-start(f32[2,2,512]{2,1,0:T(2,128)S(1)} %get-tuple-element.12), channel_id=1, source_target_pairs={{0,8},{8,0},{16,24},{24,16},{1,9},{9,1},{17,25},{25,17},{2,10},{10... | collective-permute-start | bytes 24584 | tf_op jit(solution)/shard_map/ppermute | solution.py:283
  97.6 5.6 %collective-permute-start.7 = (f32[2,512]{1,0:T(2,128)S(1)}, f32[2,512]{1,0:T(2,128)S(1)}, u32[]{:S(2)}, u32[]{:S(2)}) collective-permute-start(f32[2,512]{1,0:T(2,128)S(1)} %slice_bitcast_fusion), channel_id=1, source_target_pairs={{0,24},{24,0},{8,16},{16,8},{1,25},{25,1},{9,17},{17,9},{2,26},{26... | collective-permute-start | bytes 12296 | tf_op jit(solution)/shard_map/ppermute | solution.py:284

commit v6 on v5

--- a/solution.py
+++ b/solution.py
@@ -21,12 +21,21 @@
     return lax.ppermute(x, axis, [(i, (i + by) % size) for i in range(size)])
 
 
-def exchange(x, axis):
-    return lax.all_to_all(x, axis, 0, 0, tiled=True)
+def exchange(x, axis, order=None):
+    groups = None if order is None else [list(order)]
+    return lax.all_to_all(x, axis, 0, 0, tiled=True, axis_index_groups=groups)
 
 
 def copies(x, count):
     return jnp.broadcast_to(x, (count, *x.shape))
+
+
+ROW_TURN = 4
+SUM_TURN = 4
+
+
+def turned(by):
+    return [(i + by) % ZH for i in range(ZH)]
 
 
 LIMIT = pltpu.CompilerParams(vmem_limit_bytes=12 * 1024 * 1024)
@@ -130,10 +139,10 @@
     )(near(got), near(old))
 
 
-def slot_column(rows, pos_ref, partner):
+def slot_column(rows, pos_ref, partner, turn):
     r = lax.broadcasted_iota(jnp.int32, (rows, 1), 0)
     per_z = NC * 3
-    zh = r // per_z
+    zh = (r // per_z + turn) % ZH
     c = (r % per_z) // 3
     half = 1 - pos_ref[1] if partner else pos_ref[1]
     first = (half * NY + pos_ref[0]) * 3
@@ -147,7 +156,7 @@
 
 def sums_kernel(partner, pos_ref, own_ref, a_ref, b_ref, c_ref, *out_refs):
     points = own_ref.shape[0] - 16
-    wanted = slot_column(out_refs[0].shape[0], pos_ref, partner)
+    wanted = slot_column(out_refs[0].shape[0], pos_ref, partner, SUM_TURN)
     total = None
     for ref in (own_ref, a_ref, b_ref, c_ref):
         hot = (wanted == id_row(ref, points)).astype(jnp.float32).astype(jnp.bfloat16)
@@ -208,7 +217,7 @@
         rows = ref[...]
         wide = rows.astype(jnp.float32)
         square = jnp.sum(wide * wide, axis=1, keepdims=True)
-        parts.append((rows, square, slot_column(rows.shape[0], pos_ref, partner)))
+        parts.append((rows, square, slot_column(rows.shape[0], pos_ref, partner, ROW_TURN)))
     for by, ref in enumerate((own_ref, a_ref, b_ref, c_ref)):
         ids = id_row(ref, points)
         score = size = None
@@ -267,7 +276,7 @@
     others = [after, far, before]
     cent = exchange(old_centroids.reshape(3, NC, width).swapaxes(0, 1), "c")
 
-    here = exchange(copies(cent.reshape(NC * 3, width), ZH), "zh")
+    here = exchange(copies(cent.reshape(NC * 3, width), ZH), "zh", turned(ROW_TURN))
     here = here.reshape(ZH * NC * 3, width)
 
     away = local_sums(pos, packed, others, 2, True)
@@ -276,7 +285,7 @@
     (home,) = local_sums(pos, packed, others, 1, False)
     there = lax.ppermute(here, ("zh", "zl"), beside)
     both = merged(home, *arrived).reshape(ZH, NC * 3, width)
-    summed = exchange(both, "zh")
+    summed = exchange(both, "zh", turned(SUM_TURN))
     summed = summed.sum(axis=0)
 
     keep, give, size = local_scores(pos, packed, others, here, there)

time: 116 us -> 117 us (level)
    all_to_all x2, starting transfers between devices: 21.1 us -> 28.2 us  [exchange(): return lax.all_to_all(x, axis, 0, 0, tiled=True, axis_index_groups=groups)]
    ppermute x1, starting transfers between devices: 9.36 us -> 6.35 us  [steps(): lax.ppermute(away[1], ('zh', 'zl'), beside)]
    ppermute x1, starting transfers between devices: 4.84 us -> 1.91 us  [steps(): there = lax.ppermute(here, ('zh', 'zl'), beside)]
    ppermute x1, waiting for transfers between devices: 3.51 us -> 0.94 us  [steps(): lax.ppermute(away[1], ('zh', 'zl'), beside)]
    ppermute x4, waiting for transfers between devices: 0.45 us -> 2.35 us  [shifted(): return lax.ppermute(x, axis, [(i, (i + by) % size) for i in range(size)])]
where the time goes in v6:
time: 117 us; the launch traced here: 116 us
  starting transfers between devices  55.6 us (48%)
  waiting for transfers between devices  26.8 us (23%)
  blocking collectives  23.5 us (20%)
  Pallas kernels  8.78 us (8%)
    all_to_all x2, starting transfers between devices, exchange(): return lax.all_to_all(x, axis, 0, 0, tiled=True, axis_index_groups=groups)  28.2 us
    all_to_all x2, blocking collectives, exchange(): return lax.all_to_all(x, axis, 0, 0, tiled=True, axis_index_groups=groups)  23.5 us
    ppermute x1, waiting for transfers between devices, steps(): there = lax.ppermute(here, ('zh', 'zl'), beside)  19.8 us
    ppermute x4, starting transfers between devices, shifted(): return lax.ppermute(x, axis, [(i, (i + by) % size) for i in range(size)])  13 us
    ppermute x1, starting transfers between devices, steps(): lax.ppermute(away[1], ('zh', 'zl'), beside)  6.35 us
    ppermute x1, starting transfers between devices, steps(): lax.ppermute(kept[1], 'y', [(0, 3), (3, 0), (1, 2), (2, 1)])  3.47 us
    pallas_call x1, Pallas kernels, local_scores(): pl.pallas_call(score_kernel, out_shape=(jax.ShapeDtypeStruct((2, 2, point...  3.05 us
    ppermute x1, starting transfers between devices, steps(): kept = keep + lax.ppermute(give, 'y', [(0, 1), (1, 0), (2, 3), (3, 2)])  2.66 us
  transfers between devices with their start and end apart: 10, of which 5 were waited for; matrix products, arithmetic and copies ran while one was open for 1% of the time, Pallas kernels for 5%

profile of v6, /device:TPU:1, one launch (start us, length us, event | category | flops | bytes accessed | tf_op | source)
XLA Modules:
  0.0 116.5 jit_solution(1241743579566786543)
XLA Ops:
  0.7 1.7 %pack.1.own_ref = bf16[528,512]{1,0:T(8,128)(2,1)S(1)} custom-call(s32[3]{0:T(128)S(1)} %pad_add_fusion.pos_ref, s32[1,512]{1,0:T(1,128)} %bitcast.31, s32[1536]{0:T(1024)} %table_ref.1, bf16[512,4096]{1,0:T(8,128)(2,1)} %emb_ref.1), custom_call_target="tpu_custom_call" | custom-call | tf_op jit(solution)/shard_map/pack/pallas_call | solution.py:92
  2.5 5.5 %collective-permute-start = (bf16[528,512]{1,0:T(8,128)(2,1)S(1)}, bf16[528,512]{1,0:T(8,128)(2,1)S(1)}, u32[]{:S(2)}, u32[]{:S(2)}) collective-permute-start(bf16[528,512]{1,0:T(8,128)(2,1)S(1)} %pack.1.own_ref), channel_id=1, source_target_pairs={{0,24},{8,0},{16,8},{24,16},{1,25},{9,1},{17,9},{25,17},{2,26},{10... | collective-permute-start | bytes 1622024 | tf_op jit(solution)/shard_map/ppermute | solution.py:21
  7.9 2.3 %collective-permute-start.1 = (bf16[528,512]{1,0:T(8,128)(2,1)S(1)}, bf16[528,512]{1,0:T(8,128)(2,1)S(1)}, u32[]{:S(2)}, u32[]{:S(2)}) collective-permute-start(bf16[528,512]{1,0:T(8,128)(2,1)S(1)} %pack.1.own_ref), channel_id=1, source_target_pairs={{0,16},{8,24},{16,0},{24,8},{1,17},{9,25},{17,1},{25,9},{2,18},{10... | collective-permute-start | bytes 1622024 | tf_op jit(solution)/shard_map/ppermute | solution.py:21
  10.2 2.6 %collective-permute-start.2 = (bf16[528,512]{1,0:T(8,128)(2,1)S(1)}, bf16[528,512]{1,0:T(8,128)(2,1)S(1)}, u32[]{:S(2)}, u32[]{:S(2)}) collective-permute-start(bf16[528,512]{1,0:T(8,128)(2,1)S(1)} %pack.1.own_ref), channel_id=1, source_target_pairs={{0,8},{8,16},{16,24},{24,0},{1,9},{9,17},{17,25},{25,1},{2,10},{10... | collective-permute-start | bytes 1622024 | tf_op jit(solution)/shard_map/ppermute | solution.py:21
  12.8 11.6 %all_to_all.20 = bf16[8,3,512]{2,1,0:T(4,128)(2,1)S(1)} all-to-all(bf16[8,3,512]{2,1,0:T(4,128)(2,1)S(1)} %bitcast.28), channel_id=1, replica_groups=mesh['zh'=8,'zl'=2,'y'=4,'c'=8] {'c'}, dimensions={0} | all-to-all | bytes 49152 | tf_op jit(solution)/shard_map/all_to_all | solution.py:26
  24.4 0.7 broadcast_in_dim.22
  25.1 16.7 %all-to-all-start.2 = ((bf16[8,24,512]{2,1,0:T(8,128)(2,1)}), bf16[8,24,512]{2,1,0:T(8,128)(2,1)S(1)}, u32[]{:S(2)}, u32[]{:S(2)}) async-start(bf16[8,24,512]{2,1,0:T(8,128)(2,1)} %broadcast_in_dim.22), calls=%async_computation.2 | async-start | bytes 393216 | tf_op jit(solution)/shard_map/all_to_all | solution.py:26
  41.9 1.2 %local_sums.3 = (f32[192,256]{1,0:T(8,128)S(1)}, f32[192,256]{1,0:T(8,128)S(1)}) custom-call(s32[3]{0:T(128)S(1)} %pad_add_fusion.pos_ref, bf16[528,512]{1,0:T(8,128)(2,1)S(1)} %pack.1.own_ref, bf16[528,512]{1,0:T(8,128)(2,1)S(1)} %collective-permute-done.a_ref, bf16[528,512]{1,0:T(8,128)(2,1)S(1)} %collective-permute-done.1.b_ref, ...), custom_call_target="tpu_custom_call" | custom-call | tf_op jit(solution)/shard_map/local_sums/pallas_call | solution.py:174
  43.1 2.7 %collective-permute-start.3 = (f32[192,256]{1,0:T(8,128)S(1)}, f32[192,256]{1,0:T(8,128)S(1)}, u32[]{:S(2)}, u32[]{:S(2)}) collective-permute-start(f32[192,256]{1,0:T(8,128)S(1)} %get-tuple-element.9), channel_id=1, source_target_pairs={{0,32},{32,0},{1,33},{33,1},{2,34},{34,2},{3,35},{35,3},{4,36},{36... | collective-permute-start | bytes 589832 | tf_op jit(solution)/shard_map/ppermute | solution.py:21
  45.8 6.3 %collective-permute-start.4 = (f32[192,256]{1,0:T(8,128)S(1)}, f32[192,256]{1,0:T(8,128)S(1)}, u32[]{:S(2)}, u32[]{:S(2)}) collective-permute-start(f32[192,256]{1,0:T(8,128)S(1)} %get-tuple-element.10), channel_id=1, source_target_pairs={{0,480},{32,64},{64,32},{96,128},{128,96},{160,192},{192,160},{224... | collective-permute-start | bytes 589832 | tf_op jit(solution)/shard_map/ppermute | solution.py:284
  52.1 1.2 %local_sums.2.home_ref = f32[192,512]{1,0:T(8,128)S(1)} custom-call(s32[3]{0:T(128)S(1)} %pad_add_fusion.pos_ref, bf16[528,512]{1,0:T(8,128)(2,1)S(1)} %pack.1.own_ref, bf16[528,512]{1,0:T(8,128)(2,1)S(1)} %collective-permute-done.a_ref, bf16[528,512]{1,0:T(8,128)(2,1)S(1)} %collective-permute-done.1.b_ref, bf16[528,512]{1,0:T(8,128)(2,1)S(1)} %collective-permute-done.2.c_ref), custom_call_target="tpu_custom_call" | custom-call | tf_op jit(solution)/shard_map/local_sums/pallas_call | solution.py:174
  53.4 2.3 %collective-permute-done.3.a_ref = f32[192,256]{1,0:T(8,128)S(1)} collective-permute-done((f32[192,256]{1,0:T(8,128)S(1)}, f32[192,256]{1,0:T(8,128)S(1)}, u32[]{:S(2)}, u32[]{:S(2)}) %collective-permute-start.3) | collective-permute-done | bytes 196640 | tf_op jit(solution)/shard_map/ppermute | solution.py:21
  55.7 0.9 collective-permute-done.4.b_ref
  56.6 0.8 merged.1
  57.4 11.5 %all-to-all-start = ((f32[8,24,512]{2,1,0:T(8,128)}), f32[8,24,512]{2,1,0:T(8,128)S(1)}, u32[]{:S(2)}, u32[]{:S(2)}) async-start(f32[8,24,512]{2,1,0:T(8,128)} %bitcast.4), calls=%async_computation | async-start | bytes 786432 | tf_op jit(solution)/shard_map/all_to_all | solution.py:26
  68.9 1.9 %collective-permute-start.5 = (bf16[192,512]{1,0:T(8,128)(2,1)S(1)}, bf16[192,512]{1,0:T(8,128)(2,1)S(1)}, u32[]{:S(2)}, u32[]{:S(2)}) collective-permute-start(bf16[192,512]{1,0:T(8,128)(2,1)S(1)} %bitcast.25), channel_id=1, source_target_pairs={{0,480},{32,64},{64,32},{96,128},{128,96},{160,192},{192,160},{224... | collective-permute-start | bytes 589832 | tf_op jit(solution)/shard_map/ppermute | solution.py:286
  70.8 19.8 %collective-permute-done.5.there_ref = bf16[192,512]{1,0:T(8,128)(2,1)S(1)} collective-permute-done((bf16[192,512]{1,0:T(8,128)(2,1)S(1)}, bf16[192,512]{1,0:T(8,128)(2,1)S(1)}, u32[]{:S(2)}, u32[]{:S(2)}) %collective-permute-start.5) | collective-permute-done | bytes 196640 | tf_op jit(solution)/shard_map/ppermute | solution.py:286
  90.6 3.0 %local_scores.1 = (f32[2,2,512]{2,1,0:T(2,128)S(1)}, f32[2,2,512]{2,1,0:T(2,128)S(1)}, f32[1,512]{1,0:T(1,128)S(1)}) custom-call(s32[3]{0:T(128)S(1)} %pad_add_fusion.pos_ref, bf16[528,512]{1,0:T(8,128)(2,1)S(1)} %pack.1.own_ref, bf16[528,512]{1,0:T(8,128)(2,1)S(1)} %collective-permute-done.a_ref, bf16[528,512]{1,0:T(8,128)(2,1)S(1)} %collective-permute-done.1.b_ref, ...), custom_call_target="tpu_custom_call" | custom-call | tf_op jit(solution)/shard_map/local_scores/pallas_call | solution.py:253
  93.6 2.7 %collective-permute-start.6 = (f32[2,2,512]{2,1,0:T(2,128)S(1)}, f32[2,2,512]{2,1,0:T(2,128)S(1)}, u32[]{:S(2)}, u32[]{:S(2)}) collective-permute-start(f32[2,2,512]{2,1,0:T(2,128)S(1)} %get-tuple-element.12), channel_id=1, source_target_pairs={{0,8},{8,0},{16,24},{24,16},{1,9},{9,1},{17,25},{25,17},{2,10},{10... | collective-permute-start | bytes 24584 | tf_op jit(solution)/shard_map/ppermute | solution.py:292
  96.3 1.7 %collective-permute-done.6 = f32[2,2,512]{2,1,0:T(2,128)S(1)} collective-permute-done((f32[2,2,512]{2,1,0:T(2,128)S(1)}, f32[2,2,512]{2,1,0:T(2,128)S(1)}, u32[]{:S(2)}, u32[]{:S(2)}) %collective-permute-start.6) | collective-permute-done | bytes 8224 | tf_op jit(solution)/shard_map/ppermute | solution.py:292
  98.0 3.5 %collective-permute-start.7 = (f32[2,512]{1,0:T(2,128)S(1)}, f32[2,512]{1,0:T(2,128)S(1)}, u32[]{:S(2)}, u32[]{:S(2)}) collective-permute-start(f32[2,512]{1,0:T(2,128)S(1)} %slice_bitcast_fusion), channel_id=1, source_target_pairs={{0,24},{24,0},{8,16},{16,8},{1,25},{25,1},{9,17},{17,9},{2,26},{26... | collective-permute-start | bytes 12296 | tf_op jit(solution)/shard_map/ppermute | solution.py:293
  101.5 2.1 %collective-permute-done.7 = f32[2,512]{1,0:T(2,128)S(1)} collective-permute-done((f32[2,512]{1,0:T(2,128)S(1)}, f32[2,512]{1,0:T(2,128)S(1)}, u32[]{:S(2)}, u32[]{:S(2)}) %collective-permute-start.7) | collective-permute-done | bytes 4128 | tf_op jit(solution)/shard_map/ppermute | solution.py:293
  103.8 11.9 %all_to_all.21 = f32[8,1,3072]{2,1,0:T(1,128)S(1)} all-to-all(f32[8,1,3072]{2,1,0:T(1,128)S(1)} %maximum_maximum_fusion), channel_id=1, replica_groups=mesh['zh'=8,'zl'=2,'y'=4,'c'=8] {'c'}, dimensions={0} | all-to-all | bytes 196608 | tf_op jit(solution)/shard_map/all_to_all | solution.py:26
  115.7 0.8 ending.1
  (19 shorter events, 0.3 us)
Async XLA Ops:
  0.6 12.2 %copy-start = (bf16[3,4096]{1,0:T(4,128)(2,1)S(1)}, bf16[3,4096]{1,0:T(4,128)(2,1)}, u32[]{:S(2)}) copy-start(bf16[3,4096]{1,0:T(4,128)(2,1)} %old_ref.1) | copy-start | bytes 73732
  2.5 39.4 %collective-permute-start = (bf16[528,512]{1,0:T(8,128)(2,1)S(1)}, bf16[528,512]{1,0:T(8,128)(2,1)S(1)}, u32[]{:S(2)}, u32[]{:S(2)}) collective-permute-start(bf16[528,512]{1,0:T(8,128)(2,1)S(1)} %pack.1.own_ref), channel_id=1, source_target_pairs={{0,24},{8,0},{16,8},{24,16},{1,25},{9,1},{17,9},{25,17},{2,26},{10... | collective-permute-start | bytes 1622024 | tf_op jit(solution)/shard_map/ppermute | solution.py:21
  7.9 33.9 %collective-permute-start.1 = (bf16[528,512]{1,0:T(8,128)(2,1)S(1)}, bf16[528,512]{1,0:T(8,128)(2,1)S(1)}, u32[]{:S(2)}, u32[]{:S(2)}) collective-permute-start(bf16[528,512]{1,0:T(8,128)(2,1)S(1)} %pack.1.own_ref), channel_id=1, source_target_pairs={{0,16},{8,24},{16,0},{24,8},{1,17},{9,25},{17,1},{25,9},{2,18},{10... | collective-permute-start | bytes 1622024 | tf_op jit(solution)/shard_map/ppermute | solution.py:21
  10.2 31.7 %collective-permute-start.2 = (bf16[528,512]{1,0:T(8,128)(2,1)S(1)}, bf16[528,512]{1,0:T(8,128)(2,1)S(1)}, u32[]{:S(2)}, u32[]{:S(2)}) collective-permute-start(bf16[528,512]{1,0:T(8,128)(2,1)S(1)} %pack.1.own_ref), channel_id=1, source_target_pairs={{0,8},{8,16},{16,24},{24,0},{1,9},{9,17},{17,25},{25,1},{2,10},{10... | collective-permute-start | bytes 1622024 | tf_op jit(solution)/shard_map/ppermute | solution.py:21
  25.1 32.3 %all-to-all-start.2 = ((bf16[8,24,512]{2,1,0:T(8,128)(2,1)}), bf16[8,24,512]{2,1,0:T(8,128)(2,1)S(1)}, u32[]{:S(2)}, u32[]{:S(2)}) async-start(bf16[8,24,512]{2,1,0:T(8,128)(2,1)} %broadcast_in_dim.22), calls=%async_computation.2 | async-start | bytes 393216 | tf_op jit(solution)/shard_map/all_to_all | solution.py:26
  43.1 12.6 %collective-permute-start.3 = (f32[192,256]{1,0:T(8,128)S(1)}, f32[192,256]{1,0:T(8,128)S(1)}, u32[]{:S(2)}, u32[]{:S(2)}) collective-permute-start(f32[192,256]{1,0:T(8,128)S(1)} %get-tuple-element.9), channel_id=1, source_target_pairs={{0,32},{32,0},{1,33},{33,1},{2,34},{34,2},{3,35},{35,3},{4,36},{36... | collective-permute-start | bytes 589832 | tf_op jit(solution)/shard_map/ppermute | solution.py:21
  45.8 10.9 %collective-permute-start.4 = (f32[192,256]{1,0:T(8,128)S(1)}, f32[192,256]{1,0:T(8,128)S(1)}, u32[]{:S(2)}, u32[]{:S(2)}) collective-permute-start(f32[192,256]{1,0:T(8,128)S(1)} %get-tuple-element.10), channel_id=1, source_target_pairs={{0,480},{32,64},{64,32},{96,128},{128,96},{160,192},{192,160},{224... | collective-permute-start | bytes 589832 | tf_op jit(solution)/shard_map/ppermute | solution.py:284
  57.4 46.2 %all-to-all-start = ((f32[8,24,512]{2,1,0:T(8,128)}), f32[8,24,512]{2,1,0:T(8,128)S(1)}, u32[]{:S(2)}, u32[]{:S(2)}) async-start(f32[8,24,512]{2,1,0:T(8,128)} %bitcast.4), calls=%async_computation | async-start | bytes 786432 | tf_op jit(solution)/shard_map/all_to_all | solution.py:26
  68.9 21.7 %collective-permute-start.5 = (bf16[192,512]{1,0:T(8,128)(2,1)S(1)}, bf16[192,512]{1,0:T(8,128)(2,1)S(1)}, u32[]{:S(2)}, u32[]{:S(2)}) collective-permute-start(bf16[192,512]{1,0:T(8,128)(2,1)S(1)} %bitcast.25), channel_id=1, source_target_pairs={{0,480},{32,64},{64,32},{96,128},{128,96},{160,192},{192,160},{224... | collective-permute-start | bytes 589832 | tf_op jit(solution)/shard_map/ppermute | solution.py:286
  93.6 4.4 %collective-permute-start.6 = (f32[2,2,512]{2,1,0:T(2,128)S(1)}, f32[2,2,512]{2,1,0:T(2,128)S(1)}, u32[]{:S(2)}, u32[]{:S(2)}) collective-permute-start(f32[2,2,512]{2,1,0:T(2,128)S(1)} %get-tuple-element.12), channel_id=1, source_target_pairs={{0,8},{8,0},{16,24},{24,16},{1,9},{9,1},{17,25},{25,17},{2,10},{10... | collective-permute-start | bytes 24584 | tf_op jit(solution)/shard_map/ppermute | solution.py:292
  98.0 5.6 %collective-permute-start.7 = (f32[2,512]{1,0:T(2,128)S(1)}, f32[2,512]{1,0:T(2,128)S(1)}, u32[]{:S(2)}, u32[]{:S(2)}) collective-permute-start(f32[2,512]{1,0:T(2,128)S(1)} %slice_bitcast_fusion), channel_id=1, source_target_pairs={{0,24},{24,0},{8,16},{16,8},{1,25},{25,1},{9,17},{17,9},{2,26},{26... | collective-permute-start | bytes 12296 | tf_op jit(solution)/shard_map/ppermute | solution.py:293

commit v7 on v6

--- a/solution.py
+++ b/solution.py
@@ -32,10 +32,11 @@
 
 ROW_TURN = 4
 SUM_TURN = 4
+WHOLE_TURN = 4
 
 
 def turned(by):
-    return [(i + by) % ZH for i in range(ZH)]
+    return [(i + by) % 8 for i in range(8)]
 
 
 LIMIT = pltpu.CompilerParams(vmem_limit_bytes=12 * 1024 * 1024)
@@ -110,10 +111,11 @@
     width = D // NC
     points = dist_ref.shape[1]
     old = old_ref[...].astype(jnp.float32)
-    for c in range(NC):
+    for i in range(NC):
+        c = (i + WHOLE_TURN) % NC
         for k in range(3):
             new_ref[k : k + 1, c * width : (c + 1) * width] = got_ref[
-                c : c + 1, k * width : (k + 1) * width
+                i : i + 1, k * width : (k + 1) * width
             ]
     overall = new_ref[...] + old
     size = jnp.mean(overall * overall, axis=1, keepdims=True)
@@ -139,11 +141,11 @@
     )(near(got), near(old))
 
 
-def slot_column(rows, pos_ref, partner, turn):
+def slot_column(rows, pos_ref, partner, turn, c_turn):
     r = lax.broadcasted_iota(jnp.int32, (rows, 1), 0)
     per_z = NC * 3
     zh = (r // per_z + turn) % ZH
-    c = (r % per_z) // 3
+    c = ((r % per_z) // 3 + c_turn) % NC
     half = 1 - pos_ref[1] if partner else pos_ref[1]
     first = (half * NY + pos_ref[0]) * 3
     return c * (NZ * NY * 3) + zh * (ZL * NY * 3) + r % 3 + first
@@ -156,7 +158,7 @@
 
 def sums_kernel(partner, pos_ref, own_ref, a_ref, b_ref, c_ref, *out_refs):
     points = own_ref.shape[0] - 16
-    wanted = slot_column(out_refs[0].shape[0], pos_ref, partner, SUM_TURN)
+    wanted = slot_column(out_refs[0].shape[0], pos_ref, partner, SUM_TURN, WHOLE_TURN)
     total = None
     for ref in (own_ref, a_ref, b_ref, c_ref):
         hot = (wanted == id_row(ref, points)).astype(jnp.float32).astype(jnp.bfloat16)
@@ -217,7 +219,7 @@
         rows = ref[...]
         wide = rows.astype(jnp.float32)
         square = jnp.sum(wide * wide, axis=1, keepdims=True)
-        parts.append((rows, square, slot_column(rows.shape[0], pos_ref, partner, ROW_TURN)))
+        parts.append((rows, square, slot_column(rows.shape[0], pos_ref, partner, ROW_TURN, 0)))
     for by, ref in enumerate((own_ref, a_ref, b_ref, c_ref)):
         ids = id_row(ref, points)
         score = size = None
@@ -300,7 +302,7 @@
         ],
         axis=2,
     )
-    got = exchange(sends, "c")[:, 0]
+    got = exchange(sends, "c", turned(WHOLE_TURN))[:, 0]
     updated, distance = ending(got, old_centroids, points)
     return (updated, distance[0])
 

time: 117 us -> 116 us (level)
  blocking collectives: 23.5 us -> 22 us
    all_to_all x2, blocking collectives: 23.5 us -> 22 us  [exchange(): return lax.all_to_all(x, axis, 0, 0, tiled=True, axis_index_groups=groups)]
  transfers between devices with their start and end apart: 10 -> 10, of which waited for: 5 -> 5; matrix products, arithmetic and copies ran while one was open for 1% -> 1% of each run, Pallas kernels for 5% -> 6%
where the time goes in v7:
time: 116 us; the launch traced here: 115 us
  starting transfers between devices  55.3 us (48%)
  waiting for transfers between devices  27 us (23%)
  blocking collectives  22 us (19%)
  Pallas kernels  8.95 us (8%)
    all_to_all x2, starting transfers between devices, exchange(): return lax.all_to_all(x, axis, 0, 0, tiled=True, axis_index_groups=groups)  28.2 us
    all_to_all x2, blocking collectives, exchange(): return lax.all_to_all(x, axis, 0, 0, tiled=True, axis_index_groups=groups)  22 us
    ppermute x1, waiting for transfers between devices, steps(): there = lax.ppermute(here, ('zh', 'zl'), beside)  19.8 us
    ppermute x4, starting transfers between devices, shifted(): return lax.ppermute(x, axis, [(i, (i + by) % size) for i in range(size)])  13 us
    ppermute x1, starting transfers between devices, steps(): lax.ppermute(away[1], ('zh', 'zl'), beside)  6.35 us
    ppermute x1, starting transfers between devices, steps(): lax.ppermute(kept[1], 'y', [(0, 3), (3, 0), (1, 2), (2, 1)])  3.36 us
    pallas_call x1, Pallas kernels, local_scores(): pl.pallas_call(score_kernel, out_shape=(jax.ShapeDtypeStruct((2, 2, point...  3.1 us
    ppermute x1, starting transfers between devices, steps(): kept = keep + lax.ppermute(give, 'y', [(0, 1), (1, 0), (2, 3), (3, 2)])  2.57 us
  transfers between devices with their start and end apart: 10, of which 5 were waited for; matrix products, arithmetic and copies ran while one was open for 1% of the time, Pallas kernels for 6%

profile of v7, /device:TPU:1, one launch (start us, length us, event | category | flops | bytes accessed | tf_op | source)
XLA Modules:
  0.0 115.1 jit_solution(14123638967012409940)
XLA Ops:
  0.7 1.7 %pack.1.own_ref = bf16[528,512]{1,0:T(8,128)(2,1)S(1)} custom-call(s32[3]{0:T(128)S(1)} %pad_add_fusion.pos_ref, s32[1,512]{1,0:T(1,128)} %bitcast.31, s32[1536]{0:T(1024)} %table_ref.1, bf16[512,4096]{1,0:T(8,128)(2,1)} %emb_ref.1), custom_call_target="tpu_custom_call" | custom-call | tf_op jit(solution)/shard_map/pack/pallas_call | solution.py:93
  2.5 5.5 %collective-permute-start = (bf16[528,512]{1,0:T(8,128)(2,1)S(1)}, bf16[528,512]{1,0:T(8,128)(2,1)S(1)}, u32[]{:S(2)}, u32[]{:S(2)}) collective-permute-start(bf16[528,512]{1,0:T(8,128)(2,1)S(1)} %pack.1.own_ref), channel_id=1, source_target_pairs={{0,24},{8,0},{16,8},{24,16},{1,25},{9,1},{17,9},{25,17},{2,26},{10... | collective-permute-start | bytes 1622024 | tf_op jit(solution)/shard_map/ppermute | solution.py:21
  7.9 2.3 %collective-permute-start.1 = (bf16[528,512]{1,0:T(8,128)(2,1)S(1)}, bf16[528,512]{1,0:T(8,128)(2,1)S(1)}, u32[]{:S(2)}, u32[]{:S(2)}) collective-permute-start(bf16[528,512]{1,0:T(8,128)(2,1)S(1)} %pack.1.own_ref), channel_id=1, source_target_pairs={{0,16},{8,24},{16,0},{24,8},{1,17},{9,25},{17,1},{25,9},{2,18},{10... | collective-permute-start | bytes 1622024 | tf_op jit(solution)/shard_map/ppermute | solution.py:21
  10.2 2.6 %collective-permute-start.2 = (bf16[528,512]{1,0:T(8,128)(2,1)S(1)}, bf16[528,512]{1,0:T(8,128)(2,1)S(1)}, u32[]{:S(2)}, u32[]{:S(2)}) collective-permute-start(bf16[528,512]{1,0:T(8,128)(2,1)S(1)} %pack.1.own_ref), channel_id=1, source_target_pairs={{0,8},{8,16},{16,24},{24,0},{1,9},{9,17},{17,25},{25,1},{2,10},{10... | collective-permute-start | bytes 1622024 | tf_op jit(solution)/shard_map/ppermute | solution.py:21
  12.8 11.6 %all_to_all.20 = bf16[8,3,512]{2,1,0:T(4,128)(2,1)S(1)} all-to-all(bf16[8,3,512]{2,1,0:T(4,128)(2,1)S(1)} %bitcast.28), channel_id=1, replica_groups=mesh['zh'=8,'zl'=2,'y'=4,'c'=8] {'c'}, dimensions={0} | all-to-all | bytes 49152 | tf_op jit(solution)/shard_map/all_to_all | solution.py:26
  24.4 0.7 broadcast_in_dim.22
  25.1 16.7 %all-to-all-start.2 = ((bf16[8,24,512]{2,1,0:T(8,128)(2,1)}), bf16[8,24,512]{2,1,0:T(8,128)(2,1)S(1)}, u32[]{:S(2)}, u32[]{:S(2)}) async-start(bf16[8,24,512]{2,1,0:T(8,128)(2,1)} %broadcast_in_dim.22), calls=%async_computation.2 | async-start | bytes 393216 | tf_op jit(solution)/shard_map/all_to_all | solution.py:26
  41.9 1.3 %local_sums.3 = (f32[192,256]{1,0:T(8,128)S(1)}, f32[192,256]{1,0:T(8,128)S(1)}) custom-call(s32[3]{0:T(128)S(1)} %pad_add_fusion.pos_ref, bf16[528,512]{1,0:T(8,128)(2,1)S(1)} %pack.1.own_ref, bf16[528,512]{1,0:T(8,128)(2,1)S(1)} %collective-permute-done.a_ref, bf16[528,512]{1,0:T(8,128)(2,1)S(1)} %collective-permute-done.1.b_ref, ...), custom_call_target="tpu_custom_call" | custom-call | tf_op jit(solution)/shard_map/local_sums/pallas_call | solution.py:176
  43.2 2.6 %collective-permute-start.3 = (f32[192,256]{1,0:T(8,128)S(1)}, f32[192,256]{1,0:T(8,128)S(1)}, u32[]{:S(2)}, u32[]{:S(2)}) collective-permute-start(f32[192,256]{1,0:T(8,128)S(1)} %get-tuple-element.9), channel_id=1, source_target_pairs={{0,32},{32,0},{1,33},{33,1},{2,34},{34,2},{3,35},{35,3},{4,36},{36... | collective-permute-start | bytes 589832 | tf_op jit(solution)/shard_map/ppermute | solution.py:21
  45.8 6.3 %collective-permute-start.4 = (f32[192,256]{1,0:T(8,128)S(1)}, f32[192,256]{1,0:T(8,128)S(1)}, u32[]{:S(2)}, u32[]{:S(2)}) collective-permute-start(f32[192,256]{1,0:T(8,128)S(1)} %get-tuple-element.10), channel_id=1, source_target_pairs={{0,480},{32,64},{64,32},{96,128},{128,96},{160,192},{192,160},{224... | collective-permute-start | bytes 589832 | tf_op jit(solution)/shard_map/ppermute | solution.py:286
  52.2 1.3 %local_sums.2.home_ref = f32[192,512]{1,0:T(8,128)S(1)} custom-call(s32[3]{0:T(128)S(1)} %pad_add_fusion.pos_ref, bf16[528,512]{1,0:T(8,128)(2,1)S(1)} %pack.1.own_ref, bf16[528,512]{1,0:T(8,128)(2,1)S(1)} %collective-permute-done.a_ref, bf16[528,512]{1,0:T(8,128)(2,1)S(1)} %collective-permute-done.1.b_ref, bf16[528,512]{1,0:T(8,128)(2,1)S(1)} %collective-permute-done.2.c_ref), custom_call_target="tpu_custom_call" | custom-call | tf_op jit(solution)/shard_map/local_sums/pallas_call | solution.py:176
  53.4 2.3 %collective-permute-done.3.a_ref = f32[192,256]{1,0:T(8,128)S(1)} collective-permute-done((f32[192,256]{1,0:T(8,128)S(1)}, f32[192,256]{1,0:T(8,128)S(1)}, u32[]{:S(2)}, u32[]{:S(2)}) %collective-permute-start.3) | collective-permute-done | bytes 196640 | tf_op jit(solution)/shard_map/ppermute | solution.py:21
  55.7 0.9 collective-permute-done.4.b_ref
  56.7 0.8 merged.1
  57.4 11.5 %all-to-all-start = ((f32[8,24,512]{2,1,0:T(8,128)}), f32[8,24,512]{2,1,0:T(8,128)S(1)}, u32[]{:S(2)}, u32[]{:S(2)}) async-start(f32[8,24,512]{2,1,0:T(8,128)} %bitcast.4), calls=%async_computation | async-start | bytes 786432 | tf_op jit(solution)/shard_map/all_to_all | solution.py:26
  68.9 1.9 %collective-permute-start.5 = (bf16[192,512]{1,0:T(8,128)(2,1)S(1)}, bf16[192,512]{1,0:T(8,128)(2,1)S(1)}, u32[]{:S(2)}, u32[]{:S(2)}) collective-permute-start(bf16[192,512]{1,0:T(8,128)(2,1)S(1)} %bitcast.25), channel_id=1, source_target_pairs={{0,480},{32,64},{64,32},{96,128},{128,96},{160,192},{192,160},{224... | collective-permute-start | bytes 589832 | tf_op jit(solution)/shard_map/ppermute | solution.py:288
  70.8 19.8 %collective-permute-done.5.there_ref = bf16[192,512]{1,0:T(8,128)(2,1)S(1)} collective-permute-done((bf16[192,512]{1,0:T(8,128)(2,1)S(1)}, bf16[192,512]{1,0:T(8,128)(2,1)S(1)}, u32[]{:S(2)}, u32[]{:S(2)}) %collective-permute-start.5) | collective-permute-done | bytes 196640 | tf_op jit(solution)/shard_map/ppermute | solution.py:288
  90.6 3.1 %local_scores.1 = (f32[2,2,512]{2,1,0:T(2,128)S(1)}, f32[2,2,512]{2,1,0:T(2,128)S(1)}, f32[1,512]{1,0:T(1,128)S(1)}) custom-call(s32[3]{0:T(128)S(1)} %pad_add_fusion.pos_ref, bf16[528,512]{1,0:T(8,128)(2,1)S(1)} %pack.1.own_ref, bf16[528,512]{1,0:T(8,128)(2,1)S(1)} %collective-permute-done.a_ref, bf16[528,512]{1,0:T(8,128)(2,1)S(1)} %collective-permute-done.1.b_ref, ...), custom_call_target="tpu_custom_call" | custom-call | tf_op jit(solution)/shard_map/local_scores/pallas_call | solution.py:255
  93.7 2.6 %collective-permute-start.6 = (f32[2,2,512]{2,1,0:T(2,128)S(1)}, f32[2,2,512]{2,1,0:T(2,128)S(1)}, u32[]{:S(2)}, u32[]{:S(2)}) collective-permute-start(f32[2,2,512]{2,1,0:T(2,128)S(1)} %get-tuple-element.12), channel_id=1, source_target_pairs={{0,8},{8,0},{16,24},{24,16},{1,9},{9,1},{17,25},{25,17},{2,10},{10... | collective-permute-start | bytes 24584 | tf_op jit(solution)/shard_map/ppermute | solution.py:294
  96.3 1.8 %collective-permute-done.6 = f32[2,2,512]{2,1,0:T(2,128)S(1)} collective-permute-done((f32[2,2,512]{2,1,0:T(2,128)S(1)}, f32[2,2,512]{2,1,0:T(2,128)S(1)}, u32[]{:S(2)}, u32[]{:S(2)}) %collective-permute-start.6) | collective-permute-done | bytes 8224 | tf_op jit(solution)/shard_map/ppermute | solution.py:294
  98.1 3.4 %collective-permute-start.7 = (f32[2,512]{1,0:T(2,128)S(1)}, f32[2,512]{1,0:T(2,128)S(1)}, u32[]{:S(2)}, u32[]{:S(2)}) collective-permute-start(f32[2,512]{1,0:T(2,128)S(1)} %slice_bitcast_fusion), channel_id=1, source_target_pairs={{0,24},{24,0},{8,16},{16,8},{1,25},{25,1},{9,17},{17,9},{2,26},{26... | collective-permute-start | bytes 12296 | tf_op jit(solution)/shard_map/ppermute | solution.py:295
  101.5 2.2 %collective-permute-done.7 = f32[2,512]{1,0:T(2,128)S(1)} collective-permute-done((f32[2,512]{1,0:T(2,128)S(1)}, f32[2,512]{1,0:T(2,128)S(1)}, u32[]{:S(2)}, u32[]{:S(2)}) %collective-permute-start.7) | collective-permute-done | bytes 4128 | tf_op jit(solution)/shard_map/ppermute | solution.py:295
  103.9 10.4 %all_to_all.21 = f32[8,1,3072]{2,1,0:T(1,128)S(1)} all-to-all(f32[8,1,3072]{2,1,0:T(1,128)S(1)} %maximum_maximum_fusion), channel_id=1, replica_groups={{4,5,6,7,0,1,2,3},{12,13,14,15,8,9,10,11},{20,21,22,23,16,17,18,19},{28..., dimensions={0} | all-to-all | bytes 196608 | tf_op jit(solution)/shard_map/all_to_all | solution.py:26
  114.3 0.8 ending.1
  (19 shorter events, 0.3 us)
Async XLA Ops:
  0.6 12.2 %copy-start = (bf16[3,4096]{1,0:T(4,128)(2,1)S(1)}, bf16[3,4096]{1,0:T(4,128)(2,1)}, u32[]{:S(2)}) copy-start(bf16[3,4096]{1,0:T(4,128)(2,1)} %old_ref.1) | copy-start | bytes 73732
  2.5 39.4 %collective-permute-start = (bf16[528,512]{1,0:T(8,128)(2,1)S(1)}, bf16[528,512]{1,0:T(8,128)(2,1)S(1)}, u32[]{:S(2)}, u32[]{:S(2)}) collective-permute-start(bf16[528,512]{1,0:T(8,128)(2,1)S(1)} %pack.1.own_ref), channel_id=1, source_target_pairs={{0,24},{8,0},{16,8},{24,16},{1,25},{9,1},{17,9},{25,17},{2,26},{10... | collective-permute-start | bytes 1622024 | tf_op jit(solution)/shard_map/ppermute | solution.py:21
  7.9 33.9 %collective-permute-start.1 = (bf16[528,512]{1,0:T(8,128)(2,1)S(1)}, bf16[528,512]{1,0:T(8,128)(2,1)S(1)}, u32[]{:S(2)}, u32[]{:S(2)}) collective-permute-start(bf16[528,512]{1,0:T(8,128)(2,1)S(1)} %pack.1.own_ref), channel_id=1, source_target_pairs={{0,16},{8,24},{16,0},{24,8},{1,17},{9,25},{17,1},{25,9},{2,18},{10... | collective-permute-start | bytes 1622024 | tf_op jit(solution)/shard_map/ppermute | solution.py:21
  10.2 31.7 %collective-permute-start.2 = (bf16[528,512]{1,0:T(8,128)(2,1)S(1)}, bf16[528,512]{1,0:T(8,128)(2,1)S(1)}, u32[]{:S(2)}, u32[]{:S(2)}) collective-permute-start(bf16[528,512]{1,0:T(8,128)(2,1)S(1)} %pack.1.own_ref), channel_id=1, source_target_pairs={{0,8},{8,16},{16,24},{24,0},{1,9},{9,17},{17,25},{25,1},{2,10},{10... | collective-permute-start | bytes 1622024 | tf_op jit(solution)/shard_map/ppermute | solution.py:21
  25.1 32.3 %all-to-all-start.2 = ((bf16[8,24,512]{2,1,0:T(8,128)(2,1)}), bf16[8,24,512]{2,1,0:T(8,128)(2,1)S(1)}, u32[]{:S(2)}, u32[]{:S(2)}) async-start(bf16[8,24,512]{2,1,0:T(8,128)(2,1)} %broadcast_in_dim.22), calls=%async_computation.2 | async-start | bytes 393216 | tf_op jit(solution)/shard_map/all_to_all | solution.py:26
  43.2 12.6 %collective-permute-start.3 = (f32[192,256]{1,0:T(8,128)S(1)}, f32[192,256]{1,0:T(8,128)S(1)}, u32[]{:S(2)}, u32[]{:S(2)}) collective-permute-start(f32[192,256]{1,0:T(8,128)S(1)} %get-tuple-element.9), channel_id=1, source_target_pairs={{0,32},{32,0},{1,33},{33,1},{2,34},{34,2},{3,35},{35,3},{4,36},{36... | collective-permute-start | bytes 589832 | tf_op jit(solution)/shard_map/ppermute | solution.py:21
  45.8 10.8 %collective-permute-start.4 = (f32[192,256]{1,0:T(8,128)S(1)}, f32[192,256]{1,0:T(8,128)S(1)}, u32[]{:S(2)}, u32[]{:S(2)}) collective-permute-start(f32[192,256]{1,0:T(8,128)S(1)} %get-tuple-element.10), channel_id=1, source_target_pairs={{0,480},{32,64},{64,32},{96,128},{128,96},{160,192},{192,160},{224... | collective-permute-start | bytes 589832 | tf_op jit(solution)/shard_map/ppermute | solution.py:286
  57.4 46.2 %all-to-all-start = ((f32[8,24,512]{2,1,0:T(8,128)}), f32[8,24,512]{2,1,0:T(8,128)S(1)}, u32[]{:S(2)}, u32[]{:S(2)}) async-start(f32[8,24,512]{2,1,0:T(8,128)} %bitcast.4), calls=%async_computation | async-start | bytes 786432 | tf_op jit(solution)/shard_map/all_to_all | solution.py:26
  68.9 21.7 %collective-permute-start.5 = (bf16[192,512]{1,0:T(8,128)(2,1)S(1)}, bf16[192,512]{1,0:T(8,128)(2,1)S(1)}, u32[]{:S(2)}, u32[]{:S(2)}) collective-permute-start(bf16[192,512]{1,0:T(8,128)(2,1)S(1)} %bitcast.25), channel_id=1, source_target_pairs={{0,480},{32,64},{64,32},{96,128},{128,96},{160,192},{192,160},{224... | collective-permute-start | bytes 589832 | tf_op jit(solution)/shard_map/ppermute | solution.py:288
  93.7 4.4 %collective-permute-start.6 = (f32[2,2,512]{2,1,0:T(2,128)S(1)}, f32[2,2,512]{2,1,0:T(2,128)S(1)}, u32[]{:S(2)}, u32[]{:S(2)}) collective-permute-start(f32[2,2,512]{2,1,0:T(2,128)S(1)} %get-tuple-element.12), channel_id=1, source_target_pairs={{0,8},{8,0},{16,24},{24,16},{1,9},{9,1},{17,25},{25,17},{2,10},{10... | collective-permute-start | bytes 24584 | tf_op jit(solution)/shard_map/ppermute | solution.py:294
  98.1 5.6 %collective-permute-start.7 = (f32[2,512]{1,0:T(2,128)S(1)}, f32[2,512]{1,0:T(2,128)S(1)}, u32[]{:S(2)}, u32[]{:S(2)}) collective-permute-start(f32[2,512]{1,0:T(2,128)S(1)} %slice_bitcast_fusion), channel_id=1, source_target_pairs={{0,24},{24,0},{8,16},{16,8},{1,25},{25,1},{9,17},{17,9},{2,26},{26... | collective-permute-start | bytes 12296 | tf_op jit(solution)/shard_map/ppermute | solution.py:295

commit v8 on v7

--- a/solution.py
+++ b/solution.py
@@ -33,6 +33,7 @@
 ROW_TURN = 4
 SUM_TURN = 4
 WHOLE_TURN = 4
+FEATURE_TURN = 7
 
 
 def turned(by):
@@ -219,7 +220,7 @@
         rows = ref[...]
         wide = rows.astype(jnp.float32)
         square = jnp.sum(wide * wide, axis=1, keepdims=True)
-        parts.append((rows, square, slot_column(rows.shape[0], pos_ref, partner, ROW_TURN, 0)))
+        parts.append((rows, square, slot_column(rows.shape[0], pos_ref, partner, ROW_TURN, FEATURE_TURN)))
     for by, ref in enumerate((own_ref, a_ref, b_ref, c_ref)):
         ids = id_row(ref, points)
         score = size = None
@@ -276,7 +277,9 @@
     after = shifted(packed, "y", NY, -1)
     before = shifted(packed, "y", NY, 1)
     others = [after, far, before]
-    cent = exchange(old_centroids.reshape(3, NC, width).swapaxes(0, 1), "c")
+    cent = jnp.roll(old_centroids, -FEATURE_TURN * width, axis=1)
+    cent = cent.reshape(3, NC, width).swapaxes(0, 1)
+    cent = exchange(cent, "c", turned(FEATURE_TURN))
 
     here = exchange(copies(cent.reshape(NC * 3, width), ZH), "zh", turned(ROW_TURN))
     here = here.reshape(ZH * NC * 3, width)

time: 116 us -> 116 us (level)
  waiting for transfers between devices: 27 us -> 28.9 us
  starting transfers between devices: 55.3 us -> 53.8 us
    ppermute x1, starting transfers between devices: 3.36 us -> 2.13 us  [steps(): lax.ppermute(kept[1], 'y', [(0, 3), (3, 0), (1, 2), (2, 1)])]
    ppermute x1, waiting for transfers between devices: 2.18 us -> 3.41 us  [steps(): lax.ppermute(kept[1], 'y', [(0, 3), (3, 0), (1, 2), (2, 1)])]
    ppermute x1, waiting for transfers between devices: 0.93 us -> 2.1 us  [steps(): lax.ppermute(away[1], ('zh', 'zl'), beside)]
    ppermute x4, waiting for transfers between devices: 2.28 us -> 1.11 us  [shifted(): return lax.ppermute(x, axis, [(i, (i + by) % size) for i in range(size)])]
    ppermute x1, starting transfers between devices: 6.35 us -> 7.51 us  [steps(): lax.ppermute(away[1], ('zh', 'zl'), beside)]
where the time goes in v8:
time: 116 us; the launch traced here: 115 us
  starting transfers between devices  53.8 us (46%)
  waiting for transfers between devices  28.9 us (25%)
  blocking collectives  21.6 us (19%)
  Pallas kernels  8.95 us (8%)
    all_to_all x2, starting transfers between devices, exchange(): return lax.all_to_all(x, axis, 0, 0, tiled=True, axis_index_groups=groups)  27.4 us
    all_to_all x2, blocking collectives, exchange(): return lax.all_to_all(x, axis, 0, 0, tiled=True, axis_index_groups=groups)  21.6 us
    ppermute x1, waiting for transfers between devices, steps(): there = lax.ppermute(here, ('zh', 'zl'), beside)  19.8 us
    ppermute x4, starting transfers between devices, shifted(): return lax.ppermute(x, axis, [(i, (i + by) % size) for i in range(size)])  13 us
    ppermute x1, starting transfers between devices, steps(): lax.ppermute(away[1], ('zh', 'zl'), beside)  7.51 us
    ppermute x1, waiting for transfers between devices, steps(): lax.ppermute(kept[1], 'y', [(0, 3), (3, 0), (1, 2), (2, 1)])  3.41 us
    pallas_call x1, Pallas kernels, local_scores(): pl.pallas_call(score_kernel, out_shape=(jax.ShapeDtypeStruct((2, 2, point...  3.09 us
    pallas_call x2, Pallas kernels, local_sums(): pl.pallas_call(functools.partial(sums_kernel, partner), out_shape=(jax.Sh...  2.56 us
  transfers between devices with their start and end apart: 10, of which 5 were waited for; matrix products, arithmetic and copies ran while one was open for 1% of the time, Pallas kernels for 6%

profile of v8, /device:TPU:1, one launch (start us, length us, event | category | flops | bytes accessed | tf_op | source)
XLA Modules:
  0.0 115.1 jit_solution(17781097759328323371)
XLA Ops:
  0.7 1.7 %pack.1.own_ref = bf16[528,512]{1,0:T(8,128)(2,1)S(1)} custom-call(s32[3]{0:T(128)S(1)} %pad_add_fusion.pos_ref, s32[1,512]{1,0:T(1,128)} %bitcast.31, s32[1536]{0:T(1024)} %table_ref.1, bf16[512,4096]{1,0:T(8,128)(2,1)} %emb_ref.1), custom_call_target="tpu_custom_call" | custom-call | tf_op jit(solution)/shard_map/pack/pallas_call | solution.py:94
  2.5 5.5 %collective-permute-start = (bf16[528,512]{1,0:T(8,128)(2,1)S(1)}, bf16[528,512]{1,0:T(8,128)(2,1)S(1)}, u32[]{:S(2)}, u32[]{:S(2)}) collective-permute-start(bf16[528,512]{1,0:T(8,128)(2,1)S(1)} %pack.1.own_ref), channel_id=1, source_target_pairs={{0,24},{8,0},{16,8},{24,16},{1,25},{9,1},{17,9},{25,17},{2,26},{10... | collective-permute-start | bytes 1622024 | tf_op jit(solution)/shard_map/ppermute | solution.py:21
  7.9 2.3 %collective-permute-start.1 = (bf16[528,512]{1,0:T(8,128)(2,1)S(1)}, bf16[528,512]{1,0:T(8,128)(2,1)S(1)}, u32[]{:S(2)}, u32[]{:S(2)}) collective-permute-start(bf16[528,512]{1,0:T(8,128)(2,1)S(1)} %pack.1.own_ref), channel_id=1, source_target_pairs={{0,16},{8,24},{16,0},{24,8},{1,17},{9,25},{17,1},{25,9},{2,18},{10... | collective-permute-start | bytes 1622024 | tf_op jit(solution)/shard_map/ppermute | solution.py:21
  10.2 2.6 %collective-permute-start.2 = (bf16[528,512]{1,0:T(8,128)(2,1)S(1)}, bf16[528,512]{1,0:T(8,128)(2,1)S(1)}, u32[]{:S(2)}, u32[]{:S(2)}) collective-permute-start(bf16[528,512]{1,0:T(8,128)(2,1)S(1)} %pack.1.own_ref), channel_id=1, source_target_pairs={{0,8},{8,16},{16,24},{24,0},{1,9},{9,17},{17,25},{25,1},{2,10},{10... | collective-permute-start | bytes 1622024 | tf_op jit(solution)/shard_map/ppermute | solution.py:21
  12.9 11.2 %all_to_all.20 = bf16[8,3,512]{2,1,0:T(4,128)(2,1)S(1)} all-to-all(bf16[8,3,512]{2,1,0:T(4,128)(2,1)S(1)} %bitcast.29), channel_id=1, replica_groups={{7,0,1,2,3,4,5,6},{15,8,9,10,11,12,13,14},{23,16,17,18,19,20,21,22},{31..., dimensions={0} | all-to-all | bytes 49152 | tf_op jit(solution)/shard_map/all_to_all | solution.py:26
  24.1 0.7 broadcast_in_dim.22
  24.8 15.9 %all-to-all-start.2 = ((bf16[8,24,512]{2,1,0:T(8,128)(2,1)}), bf16[8,24,512]{2,1,0:T(8,128)(2,1)S(1)}, u32[]{:S(2)}, u32[]{:S(2)}) async-start(bf16[8,24,512]{2,1,0:T(8,128)(2,1)} %broadcast_in_dim.22), calls=%async_computation.2 | async-start | bytes 393216 | tf_op jit(solution)/shard_map/all_to_all | solution.py:26
  40.7 1.3 %local_sums.3 = (f32[192,256]{1,0:T(8,128)S(1)}, f32[192,256]{1,0:T(8,128)S(1)}) custom-call(s32[3]{0:T(128)S(1)} %pad_add_fusion.pos_ref, bf16[528,512]{1,0:T(8,128)(2,1)S(1)} %pack.1.own_ref, bf16[528,512]{1,0:T(8,128)(2,1)S(1)} %collective-permute-done.a_ref, bf16[528,512]{1,0:T(8,128)(2,1)S(1)} %collective-permute-done.1.b_ref, ...), custom_call_target="tpu_custom_call" | custom-call | tf_op jit(solution)/shard_map/local_sums/pallas_call | solution.py:177
  42.0 2.6 %collective-permute-start.3 = (f32[192,256]{1,0:T(8,128)S(1)}, f32[192,256]{1,0:T(8,128)S(1)}, u32[]{:S(2)}, u32[]{:S(2)}) collective-permute-start(f32[192,256]{1,0:T(8,128)S(1)} %get-tuple-element.9), channel_id=1, source_target_pairs={{0,32},{32,0},{1,33},{33,1},{2,34},{34,2},{3,35},{35,3},{4,36},{36... | collective-permute-start | bytes 589832 | tf_op jit(solution)/shard_map/ppermute | solution.py:21
  44.7 7.5 %collective-permute-start.4 = (f32[192,256]{1,0:T(8,128)S(1)}, f32[192,256]{1,0:T(8,128)S(1)}, u32[]{:S(2)}, u32[]{:S(2)}) collective-permute-start(f32[192,256]{1,0:T(8,128)S(1)} %get-tuple-element.10), channel_id=1, source_target_pairs={{0,480},{32,64},{64,32},{96,128},{128,96},{160,192},{192,160},{224... | collective-permute-start | bytes 589832 | tf_op jit(solution)/shard_map/ppermute | solution.py:289
  52.2 1.3 %local_sums.2.home_ref = f32[192,512]{1,0:T(8,128)S(1)} custom-call(s32[3]{0:T(128)S(1)} %pad_add_fusion.pos_ref, bf16[528,512]{1,0:T(8,128)(2,1)S(1)} %pack.1.own_ref, bf16[528,512]{1,0:T(8,128)(2,1)S(1)} %collective-permute-done.a_ref, bf16[528,512]{1,0:T(8,128)(2,1)S(1)} %collective-permute-done.1.b_ref, bf16[528,512]{1,0:T(8,128)(2,1)S(1)} %collective-permute-done.2.c_ref), custom_call_target="tpu_custom_call" | custom-call | tf_op jit(solution)/shard_map/local_sums/pallas_call | solution.py:177
  53.5 1.1 collective-permute-done.3.a_ref
  54.6 2.1 %collective-permute-done.4.b_ref = f32[192,256]{1,0:T(8,128)S(1)} collective-permute-done((f32[192,256]{1,0:T(8,128)S(1)}, f32[192,256]{1,0:T(8,128)S(1)}, u32[]{:S(2)}, u32[]{:S(2)}) %collective-permute-start.4) | collective-permute-done | bytes 196640 | tf_op jit(solution)/shard_map/ppermute | solution.py:289
  56.7 0.8 merged.1
  57.5 11.5 %all-to-all-start = ((f32[8,24,512]{2,1,0:T(8,128)}), f32[8,24,512]{2,1,0:T(8,128)S(1)}, u32[]{:S(2)}, u32[]{:S(2)}) async-start(f32[8,24,512]{2,1,0:T(8,128)} %bitcast.4), calls=%async_computation | async-start | bytes 786432 | tf_op jit(solution)/shard_map/all_to_all | solution.py:26
  68.9 1.9 %collective-permute-start.5 = (bf16[192,512]{1,0:T(8,128)(2,1)S(1)}, bf16[192,512]{1,0:T(8,128)(2,1)S(1)}, u32[]{:S(2)}, u32[]{:S(2)}) collective-permute-start(bf16[192,512]{1,0:T(8,128)(2,1)S(1)} %bitcast.25), channel_id=1, source_target_pairs={{0,480},{32,64},{64,32},{96,128},{128,96},{160,192},{192,160},{224... | collective-permute-start | bytes 589832 | tf_op jit(solution)/shard_map/ppermute | solution.py:291
  70.9 19.8 %collective-permute-done.5.there_ref = bf16[192,512]{1,0:T(8,128)(2,1)S(1)} collective-permute-done((bf16[192,512]{1,0:T(8,128)(2,1)S(1)}, bf16[192,512]{1,0:T(8,128)(2,1)S(1)}, u32[]{:S(2)}, u32[]{:S(2)}) %collective-permute-start.5) | collective-permute-done | bytes 196640 | tf_op jit(solution)/shard_map/ppermute | solution.py:291
  90.6 3.1 %local_scores.1 = (f32[2,2,512]{2,1,0:T(2,128)S(1)}, f32[2,2,512]{2,1,0:T(2,128)S(1)}, f32[1,512]{1,0:T(1,128)S(1)}) custom-call(s32[3]{0:T(128)S(1)} %pad_add_fusion.pos_ref, bf16[528,512]{1,0:T(8,128)(2,1)S(1)} %pack.1.own_ref, bf16[528,512]{1,0:T(8,128)(2,1)S(1)} %collective-permute-done.a_ref, bf16[528,512]{1,0:T(8,128)(2,1)S(1)} %collective-permute-done.1.b_ref, ...), custom_call_target="tpu_custom_call" | custom-call | tf_op jit(solution)/shard_map/local_scores/pallas_call | solution.py:256
  93.7 1.9 %collective-permute-start.6 = (f32[2,2,512]{2,1,0:T(2,128)S(1)}, f32[2,2,512]{2,1,0:T(2,128)S(1)}, u32[]{:S(2)}, u32[]{:S(2)}) collective-permute-start(f32[2,2,512]{2,1,0:T(2,128)S(1)} %get-tuple-element.12), channel_id=1, source_target_pairs={{0,8},{8,0},{16,24},{24,16},{1,9},{9,1},{17,25},{25,17},{2,10},{10... | collective-permute-start | bytes 24584 | tf_op jit(solution)/shard_map/ppermute | solution.py:297
  95.6 2.5 %collective-permute-done.6 = f32[2,2,512]{2,1,0:T(2,128)S(1)} collective-permute-done((f32[2,2,512]{2,1,0:T(2,128)S(1)}, f32[2,2,512]{2,1,0:T(2,128)S(1)}, u32[]{:S(2)}, u32[]{:S(2)}) %collective-permute-start.6) | collective-permute-done | bytes 8224 | tf_op jit(solution)/shard_map/ppermute | solution.py:297
  98.1 2.1 %collective-permute-start.7 = (f32[2,512]{1,0:T(2,128)S(1)}, f32[2,512]{1,0:T(2,128)S(1)}, u32[]{:S(2)}, u32[]{:S(2)}) collective-permute-start(f32[2,512]{1,0:T(2,128)S(1)} %slice_bitcast_fusion), channel_id=1, source_target_pairs={{0,24},{24,0},{8,16},{16,8},{1,25},{25,1},{9,17},{17,9},{2,26},{26... | collective-permute-start | bytes 12296 | tf_op jit(solution)/shard_map/ppermute | solution.py:298
  100.3 3.4 %collective-permute-done.7 = f32[2,512]{1,0:T(2,128)S(1)} collective-permute-done((f32[2,512]{1,0:T(2,128)S(1)}, f32[2,512]{1,0:T(2,128)S(1)}, u32[]{:S(2)}, u32[]{:S(2)}) %collective-permute-start.7) | collective-permute-done | bytes 4128 | tf_op jit(solution)/shard_map/ppermute | solution.py:298
  103.9 10.4 %all_to_all.21 = f32[8,1,3072]{2,1,0:T(1,128)S(1)} all-to-all(f32[8,1,3072]{2,1,0:T(1,128)S(1)} %maximum_maximum_fusion), channel_id=1, replica_groups={{4,5,6,7,0,1,2,3},{12,13,14,15,8,9,10,11},{20,21,22,23,16,17,18,19},{28..., dimensions={0} | all-to-all | bytes 196608 | tf_op jit(solution)/shard_map/all_to_all | solution.py:26
  114.4 0.8 ending.1
  (24 shorter events, 0.4 us)
Async XLA Ops:
  0.6 12.2 %slice-start = ((bf16[3,4096]{1,0:T(4,128)(2,1)}), bf16[3,3584]{1,0:T(4,128)(2,1)S(1)}, s32[]{:S(2)}) async-start(bf16[3,4096]{1,0:T(4,128)(2,1)} %old_ref.1), calls=%async_computation.4 | async-start | bytes 57344 | tf_op jit(solution)/shard_map/jit(_roll_static)/slice | solution.py:280
  0.6 12.2 %slice-start.1 = ((bf16[3,4096]{1,0:T(4,128)(2,1)}), bf16[3,512]{1,0:T(4,128)(2,1)S(1)}, s32[]{:S(2)}) async-start(bf16[3,4096]{1,0:T(4,128)(2,1)} %old_ref.1), calls=%async_computation.5 | async-start | bytes 8192 | tf_op jit(solution)/shard_map/jit(_roll_static)/slice | solution.py:280
  2.5 38.2 %collective-permute-start = (bf16[528,512]{1,0:T(8,128)(2,1)S(1)}, bf16[528,512]{1,0:T(8,128)(2,1)S(1)}, u32[]{:S(2)}, u32[]{:S(2)}) collective-permute-start(bf16[528,512]{1,0:T(8,128)(2,1)S(1)} %pack.1.own_ref), channel_id=1, source_target_pairs={{0,24},{8,0},{16,8},{24,16},{1,25},{9,1},{17,9},{25,17},{2,26},{10... | collective-permute-start | bytes 1622024 | tf_op jit(solution)/shard_map/ppermute | solution.py:21
  7.9 32.8 %collective-permute-start.1 = (bf16[528,512]{1,0:T(8,128)(2,1)S(1)}, bf16[528,512]{1,0:T(8,128)(2,1)S(1)}, u32[]{:S(2)}, u32[]{:S(2)}) collective-permute-start(bf16[528,512]{1,0:T(8,128)(2,1)S(1)} %pack.1.own_ref), channel_id=1, source_target_pairs={{0,16},{8,24},{16,0},{24,8},{1,17},{9,25},{17,1},{25,9},{2,18},{10... | collective-permute-start | bytes 1622024 | tf_op jit(solution)/shard_map/ppermute | solution.py:21
  10.2 30.5 %collective-permute-start.2 = (bf16[528,512]{1,0:T(8,128)(2,1)S(1)}, bf16[528,512]{1,0:T(8,128)(2,1)S(1)}, u32[]{:S(2)}, u32[]{:S(2)}) collective-permute-start(bf16[528,512]{1,0:T(8,128)(2,1)S(1)} %pack.1.own_ref), channel_id=1, source_target_pairs={{0,8},{8,16},{16,24},{24,0},{1,9},{9,17},{17,25},{25,1},{2,10},{10... | collective-permute-start | bytes 1622024 | tf_op jit(solution)/shard_map/ppermute | solution.py:21
  24.8 32.7 %all-to-all-start.2 = ((bf16[8,24,512]{2,1,0:T(8,128)(2,1)}), bf16[8,24,512]{2,1,0:T(8,128)(2,1)S(1)}, u32[]{:S(2)}, u32[]{:S(2)}) async-start(bf16[8,24,512]{2,1,0:T(8,128)(2,1)} %broadcast_in_dim.22), calls=%async_computation.2 | async-start | bytes 393216 | tf_op jit(solution)/shard_map/all_to_all | solution.py:26
  42.0 72.3 %copy-start = (bf16[3,4096]{1,0:T(4,128)(2,1)S(1)}, bf16[3,4096]{1,0:T(4,128)(2,1)}, u32[]{:S(2)}) copy-start(bf16[3,4096]{1,0:T(4,128)(2,1)} %old_ref.1) | copy-start | bytes 73732
  42.0 12.6 %collective-permute-start.3 = (f32[192,256]{1,0:T(8,128)S(1)}, f32[192,256]{1,0:T(8,128)S(1)}, u32[]{:S(2)}, u32[]{:S(2)}) collective-permute-start(f32[192,256]{1,0:T(8,128)S(1)} %get-tuple-element.9), channel_id=1, source_target_pairs={{0,32},{32,0},{1,33},{33,1},{2,34},{34,2},{3,35},{35,3},{4,36},{36... | collective-permute-start | bytes 589832 | tf_op jit(solution)/shard_map/ppermute | solution.py:21
  44.7 12.0 %collective-permute-start.4 = (f32[192,256]{1,0:T(8,128)S(1)}, f32[192,256]{1,0:T(8,128)S(1)}, u32[]{:S(2)}, u32[]{:S(2)}) collective-permute-start(f32[192,256]{1,0:T(8,128)S(1)} %get-tuple-element.10), channel_id=1, source_target_pairs={{0,480},{32,64},{64,32},{96,128},{128,96},{160,192},{192,160},{224... | collective-permute-start | bytes 589832 | tf_op jit(solution)/shard_map/ppermute | solution.py:289
  57.5 46.2 %all-to-all-start = ((f32[8,24,512]{2,1,0:T(8,128)}), f32[8,24,512]{2,1,0:T(8,128)S(1)}, u32[]{:S(2)}, u32[]{:S(2)}) async-start(f32[8,24,512]{2,1,0:T(8,128)} %bitcast.4), calls=%async_computation | async-start | bytes 786432 | tf_op jit(solution)/shard_map/all_to_all | solution.py:26
  68.9 21.7 %collective-permute-start.5 = (bf16[192,512]{1,0:T(8,128)(2,1)S(1)}, bf16[192,512]{1,0:T(8,128)(2,1)S(1)}, u32[]{:S(2)}, u32[]{:S(2)}) collective-permute-start(bf16[192,512]{1,0:T(8,128)(2,1)S(1)} %bitcast.25), channel_id=1, source_target_pairs={{0,480},{32,64},{64,32},{96,128},{128,96},{160,192},{192,160},{224... | collective-permute-start | bytes 589832 | tf_op jit(solution)/shard_map/ppermute | solution.py:291
  93.7 4.4 %collective-permute-start.6 = (f32[2,2,512]{2,1,0:T(2,128)S(1)}, f32[2,2,512]{2,1,0:T(2,128)S(1)}, u32[]{:S(2)}, u32[]{:S(2)}) collective-permute-start(f32[2,2,512]{2,1,0:T(2,128)S(1)} %get-tuple-element.12), channel_id=1, source_target_pairs={{0,8},{8,0},{16,24},{24,16},{1,9},{9,1},{17,25},{25,17},{2,10},{10... | collective-permute-start | bytes 24584 | tf_op jit(solution)/shard_map/ppermute | solution.py:297
  98.1 5.6 %collective-permute-start.7 = (f32[2,512]{1,0:T(2,128)S(1)}, f32[2,512]{1,0:T(2,128)S(1)}, u32[]{:S(2)}, u32[]{:S(2)}) collective-permute-start(f32[2,512]{1,0:T(2,128)S(1)} %slice_bitcast_fusion), channel_id=1, source_target_pairs={{0,24},{24,0},{8,16},{16,8},{1,25},{25,1},{9,17},{17,9},{2,26},{26... | collective-permute-start | bytes 12296 | tf_op jit(solution)/shard_map/ppermute | solution.py:298
